TPU v7x, 256 devices: a whole 4x4x8 slice. The times are simulated.
256 devices in a mesh: rep: 2 (over z_hi), kv: 32 (over y, x, core), tp: 4 (over z_lo).
Axes of the slice: x: 4, y: 4, z: 8 (z_hi: 2, z_lo: 4; z = z_hi * 4 + z_lo), core: 2. Of those that a mesh axis runs over, the one named last changes fastest.
Arguments:
- token_state: bfloat16 [256, 1280], P('kv'), may hold values from -6 to 6
- attn_gain: float32 [1280], replicated, may hold values from 0.1 to 1.9
- qkv_weight: bfloat16 [1280, 3840], P(None, 'tp'), may hold values from -0.15625 to 0.15625
- out_weight: bfloat16 [1280, 1280], P('tp'), may hold values from -0.15625 to 0.15625
- mlp_gain: float32 [1280], replicated, may hold values from 0.1 to 1.9
- up_weight: bfloat16 [1280, 1280], P(None, 'tp'), may hold values from -0.15625 to 0.15625
- down_weight: bfloat16 [1280, 1280], P('tp'), may hold values from -0.15625 to 0.15625
- kv_cache: bfloat16 [2, 352, 512, 2560], P('rep', 'kv', None, 'tp'), as said below
- home_replica: int32 [256], replicated, may hold values from 0 to 1, as said below
- moving: int32 [256], replicated, may hold values 0 or 1
- cache_length: int32 [256], replicated, may hold values from 1 to 32768, as said below
- block_owner: int32 [2, 352], P('rep', 'kv'), may hold values from 0 to 256, as said below
- block_index: int32 [2, 352], P('rep', 'kv'), may hold values from 0 to 63, as said below
Outputs:
- hidden_out: float32 [2, 256, 1280], P('rep', 'kv')
- new_entries: float32 [2, 256, 2560], P('rep', 'kv', 'tp')
Inputs may be any that keep to these rules, and one draw needn't show every extreme that they name: `home_replica`: both replicas hold at least one slot. `cache_length`: a slot's cache lies whole in the pool of its home replica; one slot of each replica has exactly 32768 tokens. `block_owner`: a slot owns exactly ceil(cache_length / 512) blocks, all in the pool of its home replica; 256 marks a free block. `block_index`: the blocks of one slot carry 0 to ceil(cache_length / 512) - 1, each once; free blocks carry 0. `kv_cache`: keys may be large in a few tokens.
All inputs are finite; a program needn't handle non-finite values.
Results may differ from a plain program's by a relative error of at most 0.0061.
Values may be sent and summed in bfloat16 or wider, within the bound.
No kernel may reach another device: no remote copies, remote signals or barrier semaphores. Data moves between devices by JAX's collectives and lax.ppermute only.
A program may use at most 128 MiB of HBM per device.

v0:
```python
import jax
import jax.numpy as jnp
from jax import lax
from jax.sharding import PartitionSpec as P

HD = 80


very_low = -1e30
norm_eps = 1e-06


def combined_all(value, axis, join):
    pieces = jax.tree.map(lambda part: lax.all_gather(part, axis), value)
    head = jax.tree.map(lambda part: part[0], pieces)
    tail = jax.tree.map(lambda part: part[1:], pieces)
    running, _ = lax.scan(lambda running, share: (join(running, share), None), head, tail)
    return running


def from_partner(block, axis, bit):
    count = lax.axis_size(axis)
    route = []
    for low in range(count):
        high = low | 1 << bit
        if high != low and high < count:
            route += [(low, high), (high, low)]
    return lax.ppermute(block, axis, route)


def root_norm(values_in, gain_vector):
    values_in = values_in.astype(jnp.float32)
    scaled = values_in * lax.rsqrt(
        jnp.mean(values_in * values_in, axis=-1, keepdims=True) + norm_eps
    )
    return scaled * gain_vector


def softmax_merge(earlier, later):
    peak_one, total_one, sums_one = earlier
    peak_two, total_two, sums_two = later
    joint_peak = jnp.maximum(peak_one, peak_two)
    factor_one = jnp.exp(peak_one - joint_peak)
    factor_two = jnp.exp(peak_two - joint_peak)
    return (
        joint_peak,
        total_one * factor_one + total_two * factor_two,
        sums_one * factor_one[..., None] + sums_two * factor_two[..., None],
    )


def body(
    token_state,
    attn_gain,
    qkv_weight,
    out_weight,
    mlp_gain,
    up_weight,
    down_weight,
    kv_cache,
    home_replica,
    moving,
    cache_length,
    block_owner,
    block_index,
):
    rows_kv = token_state.shape[0]
    requests = home_replica.shape[0]
    head_count = out_weight.shape[0] // HD
    normed = root_norm(lax.all_gather(token_state, "kv", axis=0, tiled=True), attn_gain).astype(
        jnp.bfloat16
    )
    projected = jnp.dot(normed, qkv_weight, preferred_element_type=jnp.float32)
    projected = projected.reshape(requests, head_count, 3, HD)
    query = (projected[:, :, 0] * HD ** (-0.5)).astype(jnp.bfloat16)
    fresh_pairs = projected[:, :, 1:].astype(jnp.bfloat16)
    blocks = kv_cache[0].reshape(kv_cache.shape[1], kv_cache.shape[2], head_count, 2, HD)
    owners = block_owner[0]
    is_owned = owners < requests
    clipped = jnp.minimum(owners, requests - 1)
    block_query = query[clipped]
    scores = jnp.einsum(
        "bhd,bthd->bth", block_query, blocks[:, :, :, 0], preferred_element_type=jnp.float32
    )
    positions = (
        block_index[0][:, None] * blocks.shape[1]
        + jnp.arange(blocks.shape[1], dtype=jnp.int32)[None, :]
    )
    usable = is_owned[:, None] & (positions < cache_length[clipped][:, None])
    masked = jnp.where(usable[:, :, None], scores, very_low)
    block_peak = jnp.max(masked, axis=1)
    onehot = (clipped[:, None] == jnp.arange(requests, dtype=jnp.int32)[None, :]) & is_owned[
        :, None
    ]
    local_peak = jnp.max(jnp.where(onehot[:, :, None], block_peak[:, None, :], very_low), axis=0)
    shift_by = local_peak[clipped]
    weights = jnp.where(usable[:, :, None], jnp.exp(masked - shift_by[:, None, :]), 0.0)
    block_total = jnp.sum(weights, axis=1)
    block_acc = jnp.einsum(
        "bth,bthd->bhd",
        weights.astype(jnp.bfloat16),
        blocks[:, :, :, 1],
        preferred_element_type=jnp.float32,
    )
    selector = onehot.astype(jnp.float32)
    local_total = jnp.einsum("bq,bh->qh", selector, block_total, precision=lax.Precision.HIGHEST)
    local_acc = jnp.einsum("bq,bhd->qhd", selector, block_acc, precision=lax.Precision.HIGHEST)
    local_parts = (local_peak, local_total, local_acc)
    replica = lax.axis_index("rep")
    row_start = lax.axis_index("kv") * rows_kv

    def own_rows(source_array):
        return lax.dynamic_slice_in_dim(source_array, row_start, rows_kv, 0)

    global_peak, global_total, global_acc = combined_all(
        (local_parts[0], local_parts[1], local_parts[2]), "kv", softmax_merge
    )
    global_peak = own_rows(global_peak)
    global_total = own_rows(global_total)
    global_acc = own_rows(global_acc)
    pair_rows = own_rows(fresh_pairs)
    query_rows = own_rows(query)
    self_score = jnp.sum(
        query_rows.astype(jnp.float32) * pair_rows[:, :, 0].astype(jnp.float32), axis=-1
    )
    top_score = jnp.maximum(global_peak, self_score)
    cache_scale = jnp.exp(global_peak - top_score)
    self_weight = jnp.exp(self_score - top_score)
    rounded_self = lax.optimization_barrier(self_weight.astype(jnp.bfloat16)).astype(jnp.float32)
    denominator = global_total * cache_scale + self_weight
    numerator = global_acc * cache_scale[..., None] + rounded_self[..., None] * pair_rows[
        :, :, 1
    ].astype(jnp.float32)
    attended = (
        (numerator / denominator[..., None]).astype(jnp.bfloat16).reshape(rows_kv, head_count * HD)
    )
    home_rows = own_rows(home_replica)
    attended_other = from_partner(attended, "rep", 0)
    attended = jnp.where((home_rows == replica)[:, None], attended, attended_other)
    partial_out = jnp.dot(attended, out_weight, preferred_element_type=jnp.float32)
    residual = token_state.astype(jnp.float32) + lax.psum(partial_out, "tp")
    normed_mlp = root_norm(residual, mlp_gain).astype(jnp.bfloat16)
    activated = jax.nn.gelu(
        jnp.dot(normed_mlp, up_weight, preferred_element_type=jnp.float32), approximate=True
    ).astype(jnp.bfloat16)
    result = residual + lax.psum(
        jnp.dot(activated, down_weight, preferred_element_type=jnp.float32), "tp"
    )
    target = jnp.bitwise_xor(home_rows, own_rows(moving))
    served_here = target == replica
    hidden_out = jnp.where(served_here[:, None], result, jnp.zeros_like(result))[None]
    entries = own_rows(projected[:, :, 1:]).reshape(rows_kv, head_count * 2 * HD)
    new_entries = jnp.where(served_here[:, None], entries, jnp.zeros_like(entries))[None]
    return (hidden_out, new_entries)


def solution(mesh):
    return jax.shard_map(
        body,
        mesh=mesh,
        in_specs=(
            P("kv", None),
            P(),
            P(None, "tp"),
            P("tp", None),
            P(),
            P(None, "tp"),
            P("tp", None),
            P("rep", "kv", None, "tp"),
            P(),
            P(),
            P(),
            P("rep", "kv"),
            P("rep", "kv"),
        ),
        out_specs=(P("rep", "kv", None), P("rep", "kv", "tp")),
        check_vma=False,
    )
```

profile of v0, /device:TPU:2, one launch (start us, length us, event | category | flops | bytes accessed | tf_op | source)
XLA Modules:
  0.0 320.5 jit_solution(10536080218962608810)
XLA Ops:
  10.0 24.8 %all_gather.21 = bf16[256,1280]{1,0:T(8,128)(2,1)S(1)} all-gather(bf16[8,1280]{1,0:T(8,128)(2,1)} %param.15), channel_id=1, replica_groups=mesh['rep'=2,'kv'=32,'tp'=4] {'kv'}, dimensions={0}, use_global_device_ids=true | all-gather | bytes 675840 | tf_op jit(solution)/shard_map/all_gather | solution.py:70
  35.1 1.6 fusion.8
  39.3 10.3 %copy.71 = bf16[1,11,512,640]{2,3,1,0:T(8,128)(2,1)} copy(bf16[1,11,512,640]{3,2,1,0:T(8,128)(2,1)} %param.22) | data formatting | bytes 14417920 | tf_op args[7]
  49.8 2.6 fusion.4
  53.5 3.1 fusion.3
  57.7 2.0 slice.70
  59.6 22.4 %all-gather = f32[8192,4]{0,1:T(4,128)S(1)} all-gather(f32[256,4]{0,1:T(4,128)S(1)} %select_reduce_fusion), channel_id=2, replica_groups=mesh['rep'=2,'kv'=32,'tp'=4] {'kv'}, dimensions={0}, use_global_device_ids=true | all-gather | bytes 135168 | tf_op jit(solution)/shard_map/all_gather | solution.py:14
  82.2 24.0 %all-gather.1 = f32[8192,4]{0,1:T(4,128)S(1)} all-gather(f32[256,4]{0,1:T(4,128)S(1)} %fusion.54), channel_id=3, replica_groups=mesh['rep'=2,'kv'=32,'tp'=4] {'kv'}, dimensions={0}, use_global_device_ids=true | all-gather | bytes 135168 | tf_op jit(solution)/shard_map/all_gather | solution.py:14
  108.6 20.0 %all-gather.5.cloned.1.call-done = f32[8192,4,80]{0,2,1:T(8,128)} async-done(((f32[256,4,80]{0,2,1:T(8,128)}), f32[8192,4,80]{0,2,1:T(8,128)}) %all-gather.5.cloned.1.call-update) | async-done | bytes 10485776 | tf_op jit(solution)/shard_map/all_gather | solution.py:14
  129.8 8.7 %slice.69 = f32[7936,4,80]{0,2,1:T(8,128)} slice(f32[8192,4,80]{0,2,1:T(8,128)} %all-gather.5.cloned.1.call-done), slice={[256:8192], [0:4], [0:80]} | slice | bytes 20316160 | tf_op jit(solution)/shard_map/slice | solution.py:16
  138.5 15.9 %copy.85 = f32[7936,4,80]{2,1,0:T(4,128)} copy(f32[7936,4,80]{0,2,1:T(8,128)} %slice.69) | data formatting | bytes 20316160 | tf_op jit(solution)/shard_map/while | solution.py:17
  154.4 111.1 %while.14 = (s32[]{:T(128)}, f32[256,4]{0,1:T(4,128)S(1)}, f32[256,4]{0,1:T(4,128)S(1)}, f32[256,4,80]{2,1,0:T(4,128)S(1)}, f32[31,256,4]{1,2,0:T(4,128)S(1)}, /...) while((s32[]{:T(128)}, f32[256,4]{0,1:T(4,128)S(1)}, f32[256,4]{0,1:T(4,128)S(1)}, ...), condition=%wide.region_5.6_spmd, body=%wide.region_4.5_spmd.sunk | while | flops 251906 | bytes 1040485 | solution.py:17
  155.4 2.6 fusion.67
  159.0 2.6 fusion.67
  162.5 2.6 fusion.67
  166.1 2.6 fusion.67
  169.7 2.6 fusion.67
  173.3 2.6 fusion.67
  176.9 2.6 fusion.67
  180.5 2.6 fusion.67
  184.0 2.6 fusion.67
  187.6 2.6 fusion.67
  191.2 2.6 fusion.67
  194.8 2.6 fusion.67
  198.4 2.6 fusion.67
  202.0 2.6 fusion.67
  205.5 2.6 fusion.67
  209.1 2.6 fusion.67
  212.7 2.6 fusion.67
  216.3 2.6 fusion.67
  219.9 2.6 fusion.67
  223.4 2.6 fusion.67
  227.0 2.6 fusion.67
  230.6 2.6 fusion.67
  234.2 2.6 fusion.67
  237.8 2.6 fusion.67
  241.4 2.6 fusion.67
  244.9 2.6 fusion.67
  248.5 2.6 fusion.67
  252.1 2.6 fusion.67
  255.7 2.6 fusion.67
  259.3 2.6 fusion.67
  262.9 2.6 fusion.67
  266.0 5.8 %collective-permute-start = (bf16[8,320]{1,0:T(8,128)(2,1)S(1)}, bf16[8,320]{1,0:T(8,128)(2,1)S(1)}, u32[]{:S(2)}, u32[]{:S(2)}) collective-permute-start(bf16[8,320]{1,0:T(8,128)(2,1)S(1)} %reshape.204), channel_id=1, source_target_pairs={{0,128},{128,0},{1,129},{129,1},{2,130},{130,2},{3,131},{131,3},{4... | collective-permute-start | bytes 15368 | tf_op jit(solution)/shard_map/ppermute | solution.py:28
  273.5 1.4 fusion.42
  274.9 19.6 %psum.14 = f32[8,1280]{1,0:T(8,128)S(1)} all-reduce(f32[8,1280]{1,0:T(8,128)S(1)} %fusion.42), channel_id=1, replica_groups=mesh['rep'=2,'kv'=32,'tp'=4] {'tp'}, use_global_device_ids=true, to_apply=%region_7.8 | all-reduce | flops 10240 | bytes 81920 | tf_op jit(solution)/shard_map/psum | solution.py:141
  294.7 2.1 fusion.37
  296.8 16.1 %psum.15 = f32[8,1280]{1,0:T(8,128)S(1)} all-reduce(f32[8,1280]{1,0:T(8,128)S(1)} %fusion.37), channel_id=1, replica_groups=mesh['rep'=2,'kv'=32,'tp'=4] {'tp'}, use_global_device_ids=true, to_apply=%region_9.10 | all-reduce | flops 10240 | bytes 81920 | tf_op jit(solution)/shard_map/psum | solution.py:146
  (153 shorter events, 45.1 us)
Async XLA Ops:
  7.2 27.9 %copy-start = (bf16[1280,960]{0,1:T(8,128)(2,1)S(1)}, bf16[1280,960]{0,1:T(8,128)(2,1)}, u32[]{:S(2)}) copy-start(bf16[1280,960]{0,1:T(8,128)(2,1)} %param.17) | copy-start | bytes 7372804
  7.2 121.4 %all-gather.5.cloned.1.call-start = ((), (), s32[]{:S(2)}) async-start(), calls=%async_computation | async-start | bytes 10813440 | tf_op jit(solution)/shard_map/all_gather | solution.py:14
  34.8 3.2 %copy-start.1 = (s32[256]{0:T(256)S(1)}, s32[256]{0:T(256)}, u32[]{:S(2)}) copy-start(s32[256]{0:T(256)} %param.25) | copy-start | bytes 3076
  36.7 1.0 copy-start.2
  53.5 54.8 %copy-start.5 = (s32[256]{0:T(256)S(1)}, s32[256]{0:T(256)}, u32[]{:S(2)}) copy-start(s32[256]{0:T(256)} %param.24) | copy-start | bytes 3076
  53.5 54.8 %copy-start.6 = (s32[256]{0:T(256)S(1)}, s32[256]{0:T(256)}, u32[]{:S(2)}) copy-start(s32[256]{0:T(256)} %param.23) | copy-start | bytes 3076
  154.4 140.2 %copy-start.3 = (bf16[8,1280]{1,0:T(8,128)(2,1)S(1)}, bf16[8,1280]{1,0:T(8,128)(2,1)}, u32[]{:S(2)}) copy-start(bf16[8,1280]{1,0:T(8,128)(2,1)} %param.15) | copy-start | bytes 61444
  154.4 140.3 %copy-start.4 = (f32[1280]{0:T(1024)S(1)}, f32[1280]{0:T(1024)}, u32[]{:S(2)}) copy-start(f32[1280]{0:T(1024)} %param.19) | copy-start | bytes 15364
  266.0 7.6 %collective-permute-start = (bf16[8,320]{1,0:T(8,128)(2,1)S(1)}, bf16[8,320]{1,0:T(8,128)(2,1)S(1)}, u32[]{:S(2)}, u32[]{:S(2)}) collective-permute-start(bf16[8,320]{1,0:T(8,128)(2,1)S(1)} %reshape.204), channel_id=1, source_target_pairs={{0,128},{128,0},{1,129},{129,1},{2,130},{130,2},{3,131},{131,3},{4... | collective-permute-start | bytes 15368 | tf_op jit(solution)/shard_map/ppermute | solution.py:28
Sparse Core Ops, SparseCore 0:
  57.8 70.7 all-gather.4
where the time goes:
time: 324 us; the launch traced here: 320 us
  other arithmetic  107 us (33%)
  blocking collectives  107 us (33%)
  local copies, waits for them, and re-layouts  52 us (16%)
  waiting for transfers between devices  21.1 us (7%)
  between operations  14.2 us (4%)
  matrix products  12.1 us (4%)
  starting transfers between devices  5.8 us (2%)
    add x31, other arithmetic, softmax_merge(): sums_one * factor_one[..., None] + sums_two * factor_two[..., None]  79.9 us
    all_gather x2, blocking collectives, combined_all(): pieces = jax.tree.map(lambda part: lax.all_gather(part, axis), value)  46.4 us
    all_gather x1, blocking collectives, body(): lax.all_gather(token_state, 'kv', axis=0, tiled=True)  24.8 us
    add x31, other arithmetic, softmax_merge(): total_one * factor_one + total_two * factor_two  21.8 us
    all_gather x1, waiting for transfers between devices, combined_all(): pieces = jax.tree.map(lambda part: lax.all_gather(part, axis), value)  20 us
    psum x1, blocking collectives, body(): residual = token_state.astype(jnp.float32) + lax.psum(partial_out, 'tp')  19.6 us
    while x4, local copies, waits for them, and re-layouts, combined_all(): lax.scan(lambda running, share: (join(running, share), None), head, tail)  16.4 us
    psum x1, blocking collectives, body(): lax.psum(jnp.dot(activated, down_weight, preferred_element_type=jnp.float...  16.1 us
  transfers between devices with their start and end apart: 2, of which 2 were waited for; matrix products, arithmetic and copies ran while one was open for 2% of the time, Pallas kernels for 0%

commit v1 on v0

v1 whole, which is shorter than its diff:
```python
import functools

import jax
import jax.numpy as jnp
from jax import lax
from jax.experimental import pallas as pl
from jax.experimental.pallas import tpu as pltpu
from jax.sharding import PartitionSpec as P

HD = 80
PAIR = 2 * HD
VERY_LOW = -1e30
NORM_EPS = 1e-06
STATS = 320
WIDE = 384
F32 = jnp.float32
BF16 = jnp.bfloat16

VMEM = pl.BlockSpec(memory_space=pltpu.VMEM)
SMEM = pl.BlockSpec(memory_space=pltpu.SMEM)
PARAMS = pltpu.CompilerParams(vmem_limit_bytes=48 * 1024 * 1024)


def iota(shape, axis):
    return lax.broadcasted_iota(jnp.int32, shape, axis)


def root_norm(values, gain):
    mean = jnp.mean(values * values, axis=-1, keepdims=True)
    return values * lax.rsqrt(mean + NORM_EPS) * gain


def row_values(ref, start, rows, lanes):
    row = iota((rows, lanes), 0)
    out = jnp.zeros((rows, lanes), jnp.int32)
    for r in range(rows):
        out = jnp.where(row == r, ref[start + r], out)
    return out


def split3(value):
    high = value.astype(BF16).astype(F32)
    rest = value - high
    middle = rest.astype(BF16).astype(F32)
    return high, middle, (rest - middle).astype(BF16).astype(F32)


def project_kernel(place, home, moving, token, gain, weight, spread, query, fresh, entries):
    rows = token.shape[0]
    heads = weight.shape[1] // (3 * HD)
    normed = root_norm(token[...].astype(F32), gain[...]).astype(BF16)
    projected = jnp.dot(normed, weight[...], preferred_element_type=F32)
    own = jnp.concatenate(
        [projected[:, h * 3 * HD : h * 3 * HD + HD] for h in range(heads)]
        + [jnp.zeros((rows, WIDE - heads * HD), F32)],
        axis=1,
    )
    own = (own * HD ** (-0.5)).astype(BF16)
    query[...] = own
    for copy in range(spread.shape[0] // rows):
        spread[copy * rows : (copy + 1) * rows, :] = own
    pairs = jnp.concatenate(
        [projected[:, h * 3 * HD + HD : (h + 1) * 3 * HD] for h in range(heads)], axis=1
    )
    fresh[...] = pairs
    start = place[1] * rows
    target = row_values(home, start, rows, pairs.shape[1]) ^ row_values(
        moving, start, rows, pairs.shape[1]
    )
    entries[...] = jnp.where(target == place[0], pairs, 0.0)


def attend_kernel(owner, index, length, queries, cache, out, buffer, scores, sums, sems):
    blocks, tokens, width = cache.shape
    heads = width // PAIR
    requests = queries.shape[0]
    rows = sums.shape[0]
    copies = [
        pltpu.make_async_copy(cache.at[b], buffer.at[b], sems.at[b]) for b in range(blocks)
    ]
    for copy in copies:
        copy.start()
    row = iota((rows, 1), 0)
    owners = jnp.full((rows, 1), requests, jnp.int32)
    for b in range(blocks):
        owners = jnp.where(row == b, owner[0, b], owners)
    onehot = (iota((rows, requests), 1) == owners).astype(BF16)
    picked = jnp.dot(onehot, queries[...], preferred_element_type=F32)
    picked = jnp.concatenate([picked, jnp.zeros((rows, width - WIDE), F32)], axis=1)
    lane = iota((rows, width), 1)
    spread = jnp.zeros((rows, width), F32)
    for h in range(heads):
        moved = picked if h == 0 else pltpu.roll(picked, HD * h, 1)
        spread = jnp.where((lane >= PAIR * h) & (lane < PAIR * h + HD), moved, spread)
    head_lane = iota((8, width), 1) - PAIR * iota((8, width), 0)
    key_lanes = (head_lane >= 0) & (head_lane < HD)
    value_lanes = (head_lane >= HD) & (head_lane < PAIR)
    usable = []
    peaks = []
    for b in range(blocks):
        ask = jnp.where(key_lanes, jnp.broadcast_to(spread[b : b + 1], (8, width)), 0.0)
        copies[b].wait()
        score = lax.dot_general(
            ask.astype(BF16), buffer[b], (((1,), (1,)), ((), ())), preferred_element_type=F32
        )
        holder = owner[0, b]
        most = jnp.where(holder < requests, length[jnp.minimum(holder, requests - 1)], 0)
        use = iota((8, tokens), 1) < most - index[0, b] * tokens
        score = jnp.where(use, score, VERY_LOW)
        scores[b] = score
        usable.append(use)
        peaks.append(jnp.max(score, axis=1, keepdims=True))
    joint = []
    for b in range(blocks):
        peak = peaks[b]
        for c in range(blocks):
            if c != b:
                peak = jnp.maximum(peak, jnp.where(owner[0, c] == owner[0, b], peaks[c], VERY_LOW))
        joint.append(peak)
    stat_lane = iota((8, 128), 1) - (STATS - 256)
    stat_row = iota((8, 128), 0)
    stats = []
    for b in range(blocks):
        weights = jnp.where(usable[b], jnp.exp(scores[b] - joint[b]), 0.0)
        total = jnp.sum(weights, axis=1, keepdims=True)
        acc = jnp.dot(weights.astype(BF16), buffer[b], preferred_element_type=F32)
        sums[b : b + 1, :] = jnp.sum(jnp.where(value_lanes, acc, 0.0), axis=0, keepdims=True)
        stat = jnp.where(stat_lane == stat_row, joint[b], 0.0)
        stat = stat + jnp.where(stat_lane == stat_row + 8, total, 0.0)
        stats.append(jnp.sum(jnp.where(stat_row < heads, stat, 0.0), axis=0, keepdims=True))
    stats += [jnp.zeros((1, 128), F32)] * (rows - blocks)
    stats = jnp.concatenate(stats, axis=0)
    sums[blocks:rows, :] = jnp.zeros((rows - blocks, width), F32)
    packed = jnp.zeros((rows, width), F32)
    every = sums[...]
    for h in range(heads):
        moved = pltpu.roll(every, width - HD * (h + 1), 1)
        packed = jnp.where((lane >= HD * h) & (lane < HD * (h + 1)), moved, packed)
    packed = packed[:, :WIDE]
    added = jnp.zeros((rows, WIDE), F32)
    totals = jnp.zeros((rows, 128), F32)
    first = row < blocks
    for b in range(blocks):
        same = owners == owner[0, b]
        added = added + jnp.where(same, packed[b : b + 1], 0.0)
        totals = totals + jnp.where(same, stats[b : b + 1], 0.0)
        first = first & ((row <= b) | ~same)
    tail = iota((rows, 128), 1) - (STATS - 256)
    peak_part = jnp.where((tail >= 0) & (tail < 8), stats, 0.0)
    total_part = jnp.where((tail >= 8) & (tail < 16), totals, 0.0)
    parts = jnp.zeros((rows, 128), F32)
    for k, part in enumerate(split3(peak_part)):
        parts = parts + (part if k == 0 else pltpu.roll(part, 16 * k, 1))
    for k, part in enumerate(split3(total_part)):
        parts = parts + (part if k == 0 else pltpu.roll(part, 16 * k, 1))
    last = jnp.where(tail >= 0, parts, added[:, 256:])
    full = jnp.concatenate([added[:, :256], last], axis=1)
    full = jnp.where(first, full, 0.0).astype(BF16)
    place = (iota((rows, requests), 1) == owners) & first
    out[...] = lax.dot_general(
        place.astype(F32).astype(BF16),
        full,
        (((0,), (0,)), ((), ())),
        preferred_element_type=F32,
    ).astype(BF16)


def merge_kernel(shares, query, fresh, attended):
    rows = query.shape[0]
    count = shares.shape[0] // rows
    heads = fresh.shape[1] // PAIR
    sums = shares[...].astype(F32)
    tail = sums[:, 256:]
    joined = tail + pltpu.roll(tail, 128 - 16, 1) + pltpu.roll(tail, 128 - 32, 1)
    totals = pltpu.roll(joined, 128 - 8, 1)
    lane = iota(joined.shape, 1) - (STATS - 256)
    peaks = jnp.where((lane >= 0) & (lane < heads) & (totals > 0.0), joined, VERY_LOW)
    pair = fresh[...].astype(BF16).astype(F32)
    own = query[...].astype(F32)
    keys = jnp.concatenate([pair[:, PAIR * h : PAIR * h + HD] for h in range(heads)], axis=1)
    values = jnp.concatenate(
        [pair[:, PAIR * h + HD : PAIR * (h + 1)] for h in range(heads)], axis=1
    )
    product = own[:, : heads * HD] * keys
    head_of = iota((rows, heads * HD), 1) // HD
    own_lane = iota((rows, 128), 1) - (STATS - 256)
    self_score = jnp.full((rows, 128), VERY_LOW, F32)
    for h in range(heads):
        score = jnp.sum(jnp.where(head_of == h, product, 0.0), axis=1, keepdims=True)
        self_score = jnp.where(own_lane == h, score, self_score)
    top = self_score
    for s in range(count):
        top = jnp.maximum(top, peaks[s * rows : (s + 1) * rows])
    denominator = jnp.exp(self_score - top)
    self_weight = denominator.astype(BF16).astype(F32)
    wide_of = iota((rows, WIDE), 1) // HD

    def per_head(value):
        out = jnp.zeros((rows, WIDE), F32)
        for h in range(heads):
            at = STATS - 256 + h
            out = jnp.where(wide_of == h, value[:, at : at + 1], out)
        return out

    values = jnp.concatenate([values, jnp.zeros((rows, WIDE - heads * HD), F32)], axis=1)
    numerator = per_head(self_weight) * values
    for s in range(count):
        at = slice(s * rows, (s + 1) * rows)
        factor = jnp.exp(peaks[at] - top)
        denominator = denominator + factor * totals[at]
        numerator = numerator + per_head(factor) * sums[at]
    result = numerator / jnp.where(wide_of < heads, per_head(denominator), 1.0)
    attended[...] = result.astype(BF16)


def out_kernel(place, home, here, there, weight, partial):
    rows = here.shape[0]
    stay = row_values(home, place[1] * rows, rows, here.shape[1]) == place[0]
    attended = jnp.where(stay, here[...].astype(F32), there[...].astype(F32)).astype(BF16)
    partial[...] = jnp.dot(
        attended[:, : weight.shape[0]], weight[...], preferred_element_type=F32
    )


def hidden_kernel(token, own, left, right, across, gain, up, down, residual, partial):
    total = (own[...] + across[...]) + (left[...] + right[...])
    value = token[...].astype(F32) + total
    residual[...] = value
    normed = root_norm(value, gain[...]).astype(BF16)
    hidden = jnp.dot(normed, up[...], preferred_element_type=F32)
    active = jax.nn.gelu(hidden, approximate=True).astype(BF16)
    partial[...] = jnp.dot(active, down[...], preferred_element_type=F32)


def finish_kernel(place, home, moving, residual, own, left, right, across, out):
    rows = residual.shape[0]
    start = place[1] * rows
    result = residual[...] + ((own[...] + across[...]) + (left[...] + right[...]))
    target = row_values(home, start, rows, result.shape[1]) ^ row_values(
        moving, start, rows, result.shape[1]
    )
    out[...] = jnp.where(target == place[0], result, 0.0)


def shape(dims, dtype):
    return jax.ShapeDtypeStruct(dims, dtype)


def shifted(value, by):
    axes = ("rep", "tp")
    count = lax.axis_size("rep") * lax.axis_size("tp")
    return lax.ppermute(value, axes, [(i, (i + by) % count) for i in range(count)])


def from_ring(value):
    return shifted(value, 1), shifted(value, -1), shifted(value, 2)


def body(
    token_state,
    attn_gain,
    qkv_weight,
    out_weight,
    mlp_gain,
    up_weight,
    down_weight,
    kv_cache,
    home_replica,
    moving,
    cache_length,
    block_owner,
    block_index,
):
    rows, features = token_state.shape
    requests = home_replica.shape[0]
    _, blocks, tokens, width = kv_cache.shape
    place = jnp.stack([lax.axis_index("rep"), lax.axis_index("kv")]).astype(jnp.int32)

    spread, query, fresh, entries = pl.pallas_call(
        project_kernel,
        out_shape=(
            shape((requests, WIDE), BF16),
            shape((rows, WIDE), BF16),
            shape((rows, width), F32),
            shape((rows, width), F32),
        ),
        in_specs=[SMEM] * 3 + [VMEM] * 3,
        out_specs=(VMEM,) * 4,
        compiler_params=PARAMS,
        name="project",
    )(place, home_replica, moving, token_state, attn_gain[None], qkv_weight)
    queries = lax.all_to_all(spread, "kv", 0, 0, tiled=True)

    padded = -(-blocks // 16) * 16
    shares = pl.pallas_call(
        attend_kernel,
        out_shape=shape((requests, WIDE), BF16),
        in_specs=[SMEM] * 3 + [VMEM, pl.BlockSpec(memory_space=pl.ANY)],
        out_specs=VMEM,
        scratch_shapes=[
            pltpu.VMEM((blocks, tokens, width), BF16),
            pltpu.VMEM((blocks, 8, tokens), F32),
            pltpu.VMEM((padded, width), F32),
            pltpu.SemaphoreType.DMA((blocks,)),
        ],
        compiler_params=PARAMS,
        name="attend",
    )(block_owner, block_index, cache_length, queries, kv_cache[0])
    shares = lax.all_to_all(shares, "kv", 0, 0, tiled=True)

    attended = pl.pallas_call(
        merge_kernel,
        out_shape=shape((rows, WIDE), BF16),
        in_specs=[VMEM] * 3,
        out_specs=VMEM,
        compiler_params=PARAMS,
        name="merge",
    )(shares, query, fresh)
    other = lax.ppermute(attended, "rep", [(0, 1), (1, 0)])

    partial = pl.pallas_call(
        out_kernel,
        out_shape=shape((rows, features), F32),
        in_specs=[SMEM] * 2 + [VMEM] * 3,
        out_specs=VMEM,
        compiler_params=PARAMS,
        name="out_projection",
    )(place, home_replica, attended, other, out_weight)
    residual, partial = pl.pallas_call(
        hidden_kernel,
        out_shape=(shape((rows, features), F32),) * 2,
        in_specs=[VMEM] * 8,
        out_specs=(VMEM,) * 2,
        compiler_params=PARAMS,
        name="hidden",
    )(token_state, partial, *from_ring(partial), mlp_gain[None], up_weight, down_weight)
    result = pl.pallas_call(
        finish_kernel,
        out_shape=shape((rows, features), F32),
        in_specs=[SMEM] * 3 + [VMEM] * 5,
        out_specs=VMEM,
        compiler_params=PARAMS,
        name="finish",
    )(place, home_replica, moving, residual, partial, *from_ring(partial))
    return (result[None], entries[None])


def solution(mesh):
    return jax.shard_map(
        body,
        mesh=mesh,
        in_specs=(
            P("kv", None),
            P(),
            P(None, "tp"),
            P("tp", None),
            P(),
            P(None, "tp"),
            P("tp", None),
            P("rep", "kv", None, "tp"),
            P(),
            P(),
            P(),
            P("rep", "kv"),
            P("rep", "kv"),
        ),
        out_specs=(P("rep", "kv", None), P("rep", "kv", "tp")),
        check_vma=False,
    )
```

time: 324 us -> 72 us (0.22); the launches traced: 320 us -> 71.7 us
  other arithmetic: 107 us -> 0.08 us
  blocking collectives: 107 us -> 26.4 us
  local copies, waits for them, and re-layouts: 52 us -> 3.69 us
  between operations: 14.2 us -> 0.8 us
  matrix products: 12.1 us -> 0 us
  Pallas kernels: 0 us -> 11.9 us
  starting transfers between devices: 5.8 us -> 15.3 us
  waiting for transfers between devices: 21.1 us -> 13.6 us
    add x63 -> x0, other arithmetic: 102 us -> none  [the longest x31 79.9 us: softmax_merge(): sums_one * factor_one[..., None] + sums_two * factor_two[..., None]]
    all_gather x3 -> x0, blocking collectives: 71.2 us -> none  [the longest x2 46.4 us: combined_all(): pieces = jax.tree.map(lambda part: lax.all_gather(part, axis), value)]
    psum x2 -> x0, blocking collectives: 35.7 us -> none  [the longest x1 19.6 us: body(): residual = token_state.astype(jnp.float32) + lax.psum(partial_out, 'tp')]
    all_to_all x0 -> x2, blocking collectives: none -> 26.4 us  [the longest x1 14.4 us: body(): queries = lax.all_to_all(spread, 'kv', 0, 0, tiled=True)]
    all_gather x1 -> x0, waiting for transfers between devices: 20 us -> none  [combined_all(): pieces = jax.tree.map(lambda part: lax.all_gather(part, axis), value)]
    while x4 -> x0, local copies, waits for them, and re-layouts: 16.4 us -> none  [combined_all(): lax.scan(lambda running, share: (join(running, share), None), head, tail)]
    ppermute x1 -> x7, waiting for transfers between devices: 1.12 us -> 13.6 us  [the longest x6 12 us: shifted(): lax.ppermute(value, axes, [(i, (i + by) % count) for i in range(count)])]
    slice x8 -> x0, local copies, waits for them, and re-layouts: 12.4 us -> none  [the longest x3 9.4 us: combined_all(): tail = jax.tree.map(lambda part: part[1:], pieces)]
  transfers between devices with their start and end apart: 2 -> 7, of which waited for: 2 -> 5; matrix products, arithmetic and copies ran while one was open for 2% -> 1% of each run, Pallas kernels for 0% -> 0%
where the time goes in v1:
time: 72 us; the launch traced here: 71.7 us
  blocking collectives  26.4 us (37%)
  starting transfers between devices  15.3 us (21%)
  waiting for transfers between devices  13.6 us (19%)
  Pallas kernels  11.9 us (17%)
  local copies, waits for them, and re-layouts  3.69 us (5%)
  between operations  0.8 us (1%)
    all_to_all x1, blocking collectives, body(): queries = lax.all_to_all(spread, 'kv', 0, 0, tiled=True)  14.4 us
    all_to_all x1, blocking collectives, body(): shares = lax.all_to_all(shares, 'kv', 0, 0, tiled=True)  12 us
    ppermute x6, waiting for transfers between devices, shifted(): lax.ppermute(value, axes, [(i, (i + by) % count) for i in range(count)])  12 us
    ppermute x6, starting transfers between devices, shifted(): lax.ppermute(value, axes, [(i, (i + by) % count) for i in range(count)])  8.01 us
    ppermute x1, starting transfers between devices, body(): other = lax.ppermute(attended, 'rep', [(0, 1), (1, 0)])  7.28 us
    pallas_call x1, Pallas kernels, body(): pl.pallas_call(attend_kernel, out_shape=shape((requests, WIDE), BF16), in...  7.07 us
    unnamed x24, local copies, waits for them, and re-layouts  3.68 us
    pallas_call x1, Pallas kernels, body(): pl.pallas_call(project_kernel, out_shape=(shape((requests, WIDE), BF16),...  1.79 us
  transfers between devices with their start and end apart: 7, of which 5 were waited for; matrix products, arithmetic and copies ran while one was open for 1% of the time, Pallas kernels for 0%

profile of v1, /device:TPU:2, one launch (start us, length us, event | category | flops | bytes accessed | tf_op | source)
XLA Modules:
  0.0 71.7 jit_solution(4910970003358123100)
XLA Ops:
  0.6 0.0 copy-start.9
  0.6 0.0 copy-start.2
  0.7 0.0 copy-start.3
  0.7 0.0 copy-start.4
  0.7 3.0 %copy.15.weight = bf16[1280,960]{1,0:T(8,128)(2,1)S(1)} copy(bf16[1280,960]{0,1:T(8,128)(2,1)} %param.15) | data formatting | bytes 4915200 | tf_op args[2]
  3.7 0.0 copy-done.9
  3.7 0.0 copy-start.5
  3.7 0.0 copy-start.6
  3.7 0.0 copy-start.7
  3.7 0.1 pad_add_fusion.place
  3.8 0.0 copy-done.2
  3.8 0.0 copy-done.3
  3.8 0.0 copy-done.4
  3.8 1.8 %project.1 = (bf16[256,384]{1,0:T(8,128)(2,1)S(1)}, bf16[8,384]{1,0:T(8,128)(2,1)S(1)}, f32[8,640]{1,0:T(8,128)S(1)}, f32[8,640]{1,0:T(8,128)}) custom-call(s32[2]{0:T(128)S(1)} %pad_add_fusion.place, s32[256]{0:T(256)S(1)} %copy-done.3, s32[256]{0:T(256)S(1)} %copy-done.4, bf16[8,1280]{1,0:T(8,128)(2,1)S(1)} %copy-done.2, ...), custom_call_target="tpu_custom_call" | custom-call | tf_op jit(solution)/shard_map/project/pallas_call | solution.py:279
  5.6 14.4 %all_to_all.22 = bf16[32,8,384]{2,1,0:T(8,128)(2,1)S(1)} all-to-all(bf16[32,8,384]{2,1,0:T(8,128)(2,1)S(1)} %bitcast.12), channel_id=1, replica_groups=mesh['rep'=2,'kv'=32,'tp'=4] {'kv'}, dimensions={0} | all-to-all | bytes 393216 | tf_op jit(solution)/shard_map/all_to_all | solution.py:292
  20.0 0.0 copy-done.5
  20.0 0.0 copy-done.6
  20.0 0.0 copy-done.7
  20.0 0.0 copy-start.1
  20.0 0.0 copy-start.8
  20.0 7.1 %attend.1 = bf16[256,384]{1,0:T(8,128)(2,1)S(1)} custom-call(s32[1,11]{1,0:T(1,128)S(1)} %copy-done.6, s32[1,11]{1,0:T(1,128)S(1)} %copy-done.7, s32[256]{0:T(256)S(1)} %copy-done.5, bf16[256,384]{1,0:T(8,128)(2,1)S(1)} %bitcast.10, bf16[11,512,640]{2,1,0:T(8,128)(2,1)} %bitcast.13), custom_call_target="tpu_custom_call" | custom-call | tf_op jit(solution)/shard_map/attend/pallas_call | solution.py:295
  27.1 0.0 copy-start.10
  27.1 0.0 copy-start
  27.1 12.0 %all_to_all.23 = bf16[32,8,384]{2,1,0:T(8,128)(2,1)S(1)} all-to-all(bf16[32,8,384]{2,1,0:T(8,128)(2,1)S(1)} %bitcast.11), channel_id=1, replica_groups=mesh['rep'=2,'kv'=32,'tp'=4] {'kv'}, dimensions={0} | all-to-all | bytes 393216 | tf_op jit(solution)/shard_map/all_to_all | solution.py:309
  39.1 0.5 merge.1.here
  39.7 7.3 %collective-permute-start = (bf16[8,384]{1,0:T(8,128)(2,1)S(1)}, bf16[8,384]{1,0:T(8,128)(2,1)S(1)}, u32[]{:S(2)}, u32[]{:S(2)}) collective-permute-start(bf16[8,384]{1,0:T(8,128)(2,1)S(1)} %merge.1.here), channel_id=1, source_target_pairs={{0,128},{128,0},{1,129},{129,1},{2,130},{130,2},{3,131},{131,3},{4... | collective-permute-start | bytes 18440 | tf_op jit(solution)/shard_map/ppermute | solution.py:319
  47.0 1.6 %collective-permute-done.there = bf16[8,384]{1,0:T(8,128)(2,1)S(1)} collective-permute-done((bf16[8,384]{1,0:T(8,128)(2,1)S(1)}, bf16[8,384]{1,0:T(8,128)(2,1)S(1)}, u32[]{:S(2)}, u32[]{:S(2)}) %collective-permute-start) | collective-permute-done | bytes 6176 | tf_op jit(solution)/shard_map/ppermute | solution.py:319
  48.6 0.0 copy-done.1
  48.6 0.7 %out_projection.1.own = f32[8,1280]{1,0:T(8,128)S(1)} custom-call(s32[2]{0:T(128)S(1)} %pad_add_fusion.place, s32[256]{0:T(256)S(1)} %copy-done.3, bf16[8,384]{1,0:T(8,128)(2,1)S(1)} %merge.1.here, bf16[8,384]{1,0:T(8,128)(2,1)S(1)} %collective-permute-done.there, bf16[320,1280]{1,0:T(8,128)(2,1)S(1)} %copy-done.1), custom_call_target="tpu_custom_call" | custom-call | tf_op jit(solution)/shard_map/out_projection/pallas_call | solution.py:321
  49.3 1.1 %collective-permute-start.1 = (f32[8,1280]{1,0:T(8,128)S(1)}, f32[8,1280]{1,0:T(8,128)S(1)}, u32[]{:S(2)}, u32[]{:S(2)}) collective-permute-start(f32[8,1280]{1,0:T(8,128)S(1)} %out_projection.1.own), channel_id=1, source_target_pairs={{0,1},{1,2},{2,3},{3,128},{128,129},{129,130},{130,131},{131,0},{4... | collective-permute-start | bytes 122888 | tf_op jit(solution)/shard_map/ppermute | solution.py:252
  50.4 3.7 %collective-permute-start.2 = (f32[8,1280]{1,0:T(8,128)S(1)}, f32[8,1280]{1,0:T(8,128)S(1)}, u32[]{:S(2)}, u32[]{:S(2)}) collective-permute-start(f32[8,1280]{1,0:T(8,128)S(1)} %out_projection.1.own), channel_id=1, source_target_pairs={{0,131},{1,0},{2,1},{3,2},{128,3},{129,128},{130,129},{131,130},{4... | collective-permute-start | bytes 122888 | tf_op jit(solution)/shard_map/ppermute | solution.py:252
  54.1 0.0 collective-permute-start.3
  54.1 0.0 copy-done.8
  54.1 0.6 copy.16.up
  54.7 0.0 copy-done.10
  54.7 1.6 %collective-permute-done.1.left = f32[8,1280]{1,0:T(8,128)S(1)} collective-permute-done((f32[8,1280]{1,0:T(8,128)S(1)}, f32[8,1280]{1,0:T(8,128)S(1)}, u32[]{:S(2)}, u32[]{:S(2)}) %collective-permute-start.1) | collective-permute-done | bytes 40992 | tf_op jit(solution)/shard_map/ppermute | solution.py:252
  56.3 0.0 collective-permute-done.2.right
  56.3 4.3 %collective-permute-done.3.across = f32[8,1280]{1,0:T(8,128)S(1)} collective-permute-done((f32[8,1280]{1,0:T(8,128)S(1)}, f32[8,1280]{1,0:T(8,128)S(1)}, u32[]{:S(2)}, u32[]{:S(2)}) %collective-permute-start.3) | collective-permute-done | bytes 40992 | tf_op jit(solution)/shard_map/ppermute | solution.py:252
  60.6 0.0 copy-done
  60.6 0.6 hidden.1
  61.2 0.0 collective-permute-start.4
  61.2 3.2 %collective-permute-start.5 = (f32[8,1280]{1,0:T(8,128)S(1)}, f32[8,1280]{1,0:T(8,128)S(1)}, u32[]{:S(2)}, u32[]{:S(2)}) collective-permute-start(f32[8,1280]{1,0:T(8,128)S(1)} %get-tuple-element.12.own), channel_id=1, source_target_pairs={{0,131},{1,0},{2,1},{3,2},{128,3},{129,128},{130,129},{131,130},{4... | collective-permute-start | bytes 122888 | tf_op jit(solution)/shard_map/ppermute | solution.py:252
  64.4 0.0 collective-permute-start.6
  64.4 2.0 %collective-permute-done.4.left = f32[8,1280]{1,0:T(8,128)S(1)} collective-permute-done((f32[8,1280]{1,0:T(8,128)S(1)}, f32[8,1280]{1,0:T(8,128)S(1)}, u32[]{:S(2)}, u32[]{:S(2)}) %collective-permute-start.4) | collective-permute-done | bytes 40992 | tf_op jit(solution)/shard_map/ppermute | solution.py:252
  66.4 0.0 collective-permute-done.5.right
  66.4 4.1 %collective-permute-done.6.across = f32[8,1280]{1,0:T(8,128)S(1)} collective-permute-done((f32[8,1280]{1,0:T(8,128)S(1)}, f32[8,1280]{1,0:T(8,128)S(1)}, u32[]{:S(2)}, u32[]{:S(2)}) %collective-permute-start.6) | collective-permute-done | bytes 40992 | tf_op jit(solution)/shard_map/ppermute | solution.py:252
  70.5 1.2 %finish.1 = f32[8,1280]{1,0:T(8,128)} custom-call(s32[2]{0:T(128)S(1)} %pad_add_fusion.place, s32[256]{0:T(256)S(1)} %copy-done.3, s32[256]{0:T(256)S(1)} %copy-done.4, f32[8,1280]{1,0:T(8,128)S(1)} %get-tuple-element.11.residual, f32[8,1280]{1,0:T(8,128)S(1)} %get-tuple-element.12.own, f32[8,1280]{1,0:T(8,128)S(1)} %collective-permute-done.4.left, ...), custom_call_target="tpu_custom_call" | custom-call | tf_op jit(solution)/shard_map/finish/pallas_call | solution.py:337
  (2 shorter events, 0.0 us)
Async XLA Ops:
  0.6 3.0 %copy-start.9 = (f32[1280]{0:T(1024)S(1)}, f32[1280]{0:T(1024)}, u32[]{:S(2)}) copy-start(f32[1280]{0:T(1024)} %param.14) | copy-start | bytes 15364
  0.6 3.2 %copy-start.2 = (bf16[8,1280]{1,0:T(8,128)(2,1)S(1)}, bf16[8,1280]{1,0:T(8,128)(2,1)}, u32[]{:S(2)}) copy-start(bf16[8,1280]{1,0:T(8,128)(2,1)} %token_.3) | copy-start | bytes 61444
  0.7 3.2 %copy-start.3 = (s32[256]{0:T(256)S(1)}, s32[256]{0:T(256)}, u32[]{:S(2)}) copy-start(s32[256]{0:T(256)} %home.5) | copy-start | bytes 3076
  0.7 3.2 %copy-start.4 = (s32[256]{0:T(256)S(1)}, s32[256]{0:T(256)}, u32[]{:S(2)}) copy-start(s32[256]{0:T(256)} %moving.3) | copy-start | bytes 3076
  3.7 16.3 %copy-start.5 = (s32[256]{0:T(256)S(1)}, s32[256]{0:T(256)}, u32[]{:S(2)}) copy-start(s32[256]{0:T(256)} %length.1) | copy-start | bytes 3076
  3.7 16.3 %copy-start.6 = (s32[1,11]{1,0:T(1,128)S(1)}, s32[1,11]{1,0:T(1,128)}, u32[]{:S(2)}) copy-start(s32[1,11]{1,0:T(1,128)} %owner.1) | copy-start | bytes 136
  3.7 16.3 %copy-start.7 = (s32[1,11]{1,0:T(1,128)S(1)}, s32[1,11]{1,0:T(1,128)}, u32[]{:S(2)}) copy-start(s32[1,11]{1,0:T(1,128)} %index.1) | copy-start | bytes 136
  20.0 28.6 %copy-start.1 = (bf16[320,1280]{1,0:T(8,128)(2,1)S(1)}, bf16[320,1280]{1,0:T(8,128)(2,1)}, u32[]{:S(2)}) copy-start(bf16[320,1280]{1,0:T(8,128)(2,1)} %weight.2) | copy-start | bytes 2457604
  20.0 34.0 %copy-start.8 = (bf16[1280,320]{0,1:T(8,128)(2,1)S(1)}, bf16[1280,320]{0,1:T(8,128)(2,1)}, u32[]{:S(2)}) copy-start(bf16[1280,320]{0,1:T(8,128)(2,1)} %param.18) | copy-start | bytes 2457604
  27.1 27.6 %copy-start.10 = (f32[1280]{0:T(1024)S(1)}, f32[1280]{0:T(1024)}, u32[]{:S(2)}) copy-start(f32[1280]{0:T(1024)} %param.17) | copy-start | bytes 15364
  27.1 33.5 %copy-start = (bf16[320,1280]{1,0:T(8,128)(2,1)S(1)}, bf16[320,1280]{1,0:T(8,128)(2,1)}, u32[]{:S(2)}) copy-start(bf16[320,1280]{1,0:T(8,128)(2,1)} %down.1) | copy-start | bytes 2457604
  39.7 8.9 %collective-permute-start = (bf16[8,384]{1,0:T(8,128)(2,1)S(1)}, bf16[8,384]{1,0:T(8,128)(2,1)S(1)}, u32[]{:S(2)}, u32[]{:S(2)}) collective-permute-start(bf16[8,384]{1,0:T(8,128)(2,1)S(1)} %merge.1.here), channel_id=1, source_target_pairs={{0,128},{128,0},{1,129},{129,1},{2,130},{130,2},{3,131},{131,3},{4... | collective-permute-start | bytes 18440 | tf_op jit(solution)/shard_map/ppermute | solution.py:319
  49.3 7.0 %collective-permute-start.1 = (f32[8,1280]{1,0:T(8,128)S(1)}, f32[8,1280]{1,0:T(8,128)S(1)}, u32[]{:S(2)}, u32[]{:S(2)}) collective-permute-start(f32[8,1280]{1,0:T(8,128)S(1)} %out_projection.1.own), channel_id=1, source_target_pairs={{0,1},{1,2},{2,3},{3,128},{128,129},{129,130},{130,131},{131,0},{4... | collective-permute-start | bytes 122888 | tf_op jit(solution)/shard_map/ppermute | solution.py:252
  50.4 5.9 %collective-permute-start.2 = (f32[8,1280]{1,0:T(8,128)S(1)}, f32[8,1280]{1,0:T(8,128)S(1)}, u32[]{:S(2)}, u32[]{:S(2)}) collective-permute-start(f32[8,1280]{1,0:T(8,128)S(1)} %out_projection.1.own), channel_id=1, source_target_pairs={{0,131},{1,0},{2,1},{3,2},{128,3},{129,128},{130,129},{131,130},{4... | collective-permute-start | bytes 122888 | tf_op jit(solution)/shard_map/ppermute | solution.py:252
  54.1 6.6 %collective-permute-start.3 = (f32[8,1280]{1,0:T(8,128)S(1)}, f32[8,1280]{1,0:T(8,128)S(1)}, u32[]{:S(2)}, u32[]{:S(2)}) collective-permute-start(f32[8,1280]{1,0:T(8,128)S(1)} %out_projection.1.own), channel_id=1, source_target_pairs={{0,2},{1,3},{2,128},{3,129},{128,130},{129,131},{130,0},{131,1},{4... | collective-permute-start | bytes 122888 | tf_op jit(solution)/shard_map/ppermute | solution.py:252
  61.2 5.2 %collective-permute-start.4 = (f32[8,1280]{1,0:T(8,128)S(1)}, f32[8,1280]{1,0:T(8,128)S(1)}, u32[]{:S(2)}, u32[]{:S(2)}) collective-permute-start(f32[8,1280]{1,0:T(8,128)S(1)} %get-tuple-element.12.own), channel_id=1, source_target_pairs={{0,1},{1,2},{2,3},{3,128},{128,129},{129,130},{130,131},{131,0},{4... | collective-permute-start | bytes 122888 | tf_op jit(solution)/shard_map/ppermute | solution.py:252
  61.2 5.2 %collective-permute-start.5 = (f32[8,1280]{1,0:T(8,128)S(1)}, f32[8,1280]{1,0:T(8,128)S(1)}, u32[]{:S(2)}, u32[]{:S(2)}) collective-permute-start(f32[8,1280]{1,0:T(8,128)S(1)} %get-tuple-element.12.own), channel_id=1, source_target_pairs={{0,131},{1,0},{2,1},{3,2},{128,3},{129,128},{130,129},{131,130},{4... | collective-permute-start | bytes 122888 | tf_op jit(solution)/shard_map/ppermute | solution.py:252
  64.4 6.1 %collective-permute-start.6 = (f32[8,1280]{1,0:T(8,128)S(1)}, f32[8,1280]{1,0:T(8,128)S(1)}, u32[]{:S(2)}, u32[]{:S(2)}) collective-permute-start(f32[8,1280]{1,0:T(8,128)S(1)} %get-tuple-element.12.own), channel_id=1, source_target_pairs={{0,2},{1,3},{2,128},{3,129},{128,130},{129,131},{130,0},{131,1},{4... | collective-permute-start | bytes 122888 | tf_op jit(solution)/shard_map/ppermute | solution.py:252

commit v2 on v1

--- a/solution.py
+++ b/solution.py
@@ -18,7 +18,7 @@
 
 VMEM = pl.BlockSpec(memory_space=pltpu.VMEM)
 SMEM = pl.BlockSpec(memory_space=pltpu.SMEM)
-PARAMS = pltpu.CompilerParams(vmem_limit_bytes=48 * 1024 * 1024)
+PARAMS = pltpu.CompilerParams(vmem_limit_bytes=16 * 1024 * 1024)
 
 
 def iota(shape, axis):
@@ -38,6 +38,10 @@
     return out
 
 
+def widen(value, lanes):
+    return jnp.concatenate([value] * (lanes // value.shape[1]), axis=1)
+
+
 def split3(value):
     high = value.astype(BF16).astype(F32)
     rest = value - high
@@ -45,11 +49,17 @@
     return high, middle, (rest - middle).astype(BF16).astype(F32)
 
 
-def project_kernel(place, home, moving, token, gain, weight, spread, query, fresh, entries):
+def dot_transposed(left, right):
+    return lax.dot_general(left, right, (((1,), (1,)), ((), ())), preferred_element_type=F32)
+
+
+def project_kernel(
+    place, home, moving, token, gain, weight, spread, query, fresh, entries, homed, served
+):
     rows = token.shape[0]
-    heads = weight.shape[1] // (3 * HD)
+    heads = weight.shape[0] // (3 * HD)
     normed = root_norm(token[...].astype(F32), gain[...]).astype(BF16)
-    projected = jnp.dot(normed, weight[...], preferred_element_type=F32)
+    projected = dot_transposed(normed, weight[...])
     own = jnp.concatenate(
         [projected[:, h * 3 * HD : h * 3 * HD + HD] for h in range(heads)]
         + [jnp.zeros((rows, WIDE - heads * HD), F32)],
@@ -64,22 +74,19 @@
     )
     fresh[...] = pairs
     start = place[1] * rows
-    target = row_values(home, start, rows, pairs.shape[1]) ^ row_values(
-        moving, start, rows, pairs.shape[1]
-    )
-    entries[...] = jnp.where(target == place[0], pairs, 0.0)
-
-
-def attend_kernel(owner, index, length, queries, cache, out, buffer, scores, sums, sems):
+    at_home = row_values(home, start, rows, 128)
+    target = at_home ^ row_values(moving, start, rows, 128)
+    homed[...] = jnp.where(at_home == place[0], 1.0, 0.0)
+    serves = jnp.where(target == place[0], 1.0, 0.0)
+    served[...] = serves
+    entries[...] = jnp.where(widen(serves, pairs.shape[1]) > 0.0, pairs, 0.0)
+
+
+def attend_kernel(owner, index, length, queries, cache, out, scores, sums):
     blocks, tokens, width = cache.shape
     heads = width // PAIR
     requests = queries.shape[0]
     rows = sums.shape[0]
-    copies = [
-        pltpu.make_async_copy(cache.at[b], buffer.at[b], sems.at[b]) for b in range(blocks)
-    ]
-    for copy in copies:
-        copy.start()
     row = iota((rows, 1), 0)
     owners = jnp.full((rows, 1), requests, jnp.int32)
     for b in range(blocks):
@@ -99,10 +106,7 @@
     peaks = []
     for b in range(blocks):
         ask = jnp.where(key_lanes, jnp.broadcast_to(spread[b : b + 1], (8, width)), 0.0)
-        copies[b].wait()
-        score = lax.dot_general(
-            ask.astype(BF16), buffer[b], (((1,), (1,)), ((), ())), preferred_element_type=F32
-        )
+        score = dot_transposed(ask.astype(BF16), cache[b])
         holder = owner[0, b]
         most = jnp.where(holder < requests, length[jnp.minimum(holder, requests - 1)], 0)
         use = iota((8, tokens), 1) < most - index[0, b] * tokens
@@ -123,7 +127,7 @@
     for b in range(blocks):
         weights = jnp.where(usable[b], jnp.exp(scores[b] - joint[b]), 0.0)
         total = jnp.sum(weights, axis=1, keepdims=True)
-        acc = jnp.dot(weights.astype(BF16), buffer[b], preferred_element_type=F32)
+        acc = jnp.dot(weights.astype(BF16), cache[b], preferred_element_type=F32)
         sums[b : b + 1, :] = jnp.sum(jnp.where(value_lanes, acc, 0.0), axis=0, keepdims=True)
         stat = jnp.where(stat_lane == stat_row, joint[b], 0.0)
         stat = stat + jnp.where(stat_lane == stat_row + 8, total, 0.0)
@@ -165,7 +169,7 @@
     ).astype(BF16)
 
 
-def merge_kernel(shares, query, fresh, attended):
+def merge_kernel(shares, query, fresh, homed, weight, spread):
     rows = query.shape[0]
     count = shares.shape[0] // rows
     heads = fresh.shape[1] // PAIR
@@ -210,50 +214,41 @@
         denominator = denominator + factor * totals[at]
         numerator = numerator + per_head(factor) * sums[at]
     result = numerator / jnp.where(wide_of < heads, per_head(denominator), 1.0)
-    attended[...] = result.astype(BF16)
-
-
-def out_kernel(place, home, here, there, weight, partial):
-    rows = here.shape[0]
-    stay = row_values(home, place[1] * rows, rows, here.shape[1]) == place[0]
-    attended = jnp.where(stay, here[...].astype(F32), there[...].astype(F32)).astype(BF16)
-    partial[...] = jnp.dot(
+    attended = jnp.where(widen(homed[...], WIDE) > 0.0, result, 0.0).astype(BF16)
+    partial = jnp.dot(
         attended[:, : weight.shape[0]], weight[...], preferred_element_type=F32
-    )
-
-
-def hidden_kernel(token, own, left, right, across, gain, up, down, residual, partial):
-    total = (own[...] + across[...]) + (left[...] + right[...])
-    value = token[...].astype(F32) + total
-    residual[...] = value
-    normed = root_norm(value, gain[...]).astype(BF16)
-    hidden = jnp.dot(normed, up[...], preferred_element_type=F32)
+    ).astype(BF16)
+    for copy in range(spread.shape[0]):
+        spread[copy] = partial
+
+
+def hidden_kernel(token, shares, gain, up, down, residual, partial):
+    total = token[...].astype(F32)
+    for share in range(shares.shape[0]):
+        total = total + shares[share].astype(F32)
+    residual[...] = total
+    normed = root_norm(total, gain[...]).astype(BF16)
+    hidden = dot_transposed(normed, up[...])
     active = jax.nn.gelu(hidden, approximate=True).astype(BF16)
-    partial[...] = jnp.dot(active, down[...], preferred_element_type=F32)
-
-
-def finish_kernel(place, home, moving, residual, own, left, right, across, out):
-    rows = residual.shape[0]
-    start = place[1] * rows
-    result = residual[...] + ((own[...] + across[...]) + (left[...] + right[...]))
-    target = row_values(home, start, rows, result.shape[1]) ^ row_values(
-        moving, start, rows, result.shape[1]
-    )
-    out[...] = jnp.where(target == place[0], result, 0.0)
+    partial[...] = jnp.dot(active, down[...], preferred_element_type=F32).astype(BF16)
+
+
+def finish_kernel(served, residual, own, near, across, far, out):
+    own, near, across, far = (v[...].astype(F32) for v in (own, near, across, far))
+    result = residual[...] + ((own + near) + (across + far))
+    out[...] = jnp.where(widen(served[...], result.shape[1]) > 0.0, result, 0.0)
 
 
 def shape(dims, dtype):
     return jax.ShapeDtypeStruct(dims, dtype)
 
 
-def shifted(value, by):
-    axes = ("rep", "tp")
-    count = lax.axis_size("rep") * lax.axis_size("tp")
-    return lax.ppermute(value, axes, [(i, (i + by) % count) for i in range(count)])
-
-
-def from_ring(value):
-    return shifted(value, 1), shifted(value, -1), shifted(value, 2)
+def from_others(value, axis):
+    count = lax.axis_size(axis)
+    return [
+        lax.ppermute(value, axis, [(i, i ^ bits) for i in range(count)])
+        for bits in range(1, count)
+    ]
 
 
 def body(
@@ -276,72 +271,66 @@
     _, blocks, tokens, width = kv_cache.shape
     place = jnp.stack([lax.axis_index("rep"), lax.axis_index("kv")]).astype(jnp.int32)
 
-    spread, query, fresh, entries = pl.pallas_call(
+    spread, query, fresh, entries, homed, served = pl.pallas_call(
         project_kernel,
         out_shape=(
             shape((requests, WIDE), BF16),
             shape((rows, WIDE), BF16),
             shape((rows, width), F32),
             shape((rows, width), F32),
+            shape((rows, 128), F32),
+            shape((rows, 128), F32),
         ),
         in_specs=[SMEM] * 3 + [VMEM] * 3,
-        out_specs=(VMEM,) * 4,
+        out_specs=(VMEM,) * 6,
         compiler_params=PARAMS,
         name="project",
-    )(place, home_replica, moving, token_state, attn_gain[None], qkv_weight)
+    )(place, home_replica, moving, token_state, attn_gain[None], qkv_weight.T)
     queries = lax.all_to_all(spread, "kv", 0, 0, tiled=True)
 
     padded = -(-blocks // 16) * 16
     shares = pl.pallas_call(
         attend_kernel,
         out_shape=shape((requests, WIDE), BF16),
-        in_specs=[SMEM] * 3 + [VMEM, pl.BlockSpec(memory_space=pl.ANY)],
+        in_specs=[SMEM] * 3 + [VMEM] * 2,
         out_specs=VMEM,
         scratch_shapes=[
-            pltpu.VMEM((blocks, tokens, width), BF16),
             pltpu.VMEM((blocks, 8, tokens), F32),
             pltpu.VMEM((padded, width), F32),
-            pltpu.SemaphoreType.DMA((blocks,)),
         ],
         compiler_params=PARAMS,
         name="attend",
     )(block_owner, block_index, cache_length, queries, kv_cache[0])
     shares = lax.all_to_all(shares, "kv", 0, 0, tiled=True)
 
-    attended = pl.pallas_call(
+    everyone = ("rep", "tp")
+    count = lax.axis_size("rep") * lax.axis_size("tp")
+    partials = pl.pallas_call(
         merge_kernel,
-        out_shape=shape((rows, WIDE), BF16),
-        in_specs=[VMEM] * 3,
+        out_shape=shape((count, rows, features), BF16),
+        in_specs=[VMEM] * 5,
         out_specs=VMEM,
         compiler_params=PARAMS,
         name="merge",
-    )(shares, query, fresh)
-    other = lax.ppermute(attended, "rep", [(0, 1), (1, 0)])
-
-    partial = pl.pallas_call(
-        out_kernel,
-        out_shape=shape((rows, features), F32),
-        in_specs=[SMEM] * 2 + [VMEM] * 3,
-        out_specs=VMEM,
-        compiler_params=PARAMS,
-        name="out_projection",
-    )(place, home_replica, attended, other, out_weight)
+    )(shares, query, fresh, homed, out_weight)
+    partials = lax.all_to_all(partials, everyone, 0, 0, tiled=True)
+
     residual, partial = pl.pallas_call(
         hidden_kernel,
-        out_shape=(shape((rows, features), F32),) * 2,
-        in_specs=[VMEM] * 8,
+        out_shape=(shape((rows, features), F32), shape((rows, features), BF16)),
+        in_specs=[VMEM] * 5,
         out_specs=(VMEM,) * 2,
         compiler_params=PARAMS,
         name="hidden",
-    )(token_state, partial, *from_ring(partial), mlp_gain[None], up_weight, down_weight)
+    )(token_state, partials, mlp_gain[None], up_weight.T, down_weight)
     result = pl.pallas_call(
         finish_kernel,
         out_shape=shape((rows, features), F32),
-        in_specs=[SMEM] * 3 + [VMEM] * 5,
+        in_specs=[VMEM] * 6,
         out_specs=VMEM,
         compiler_params=PARAMS,
         name="finish",
-    )(place, home_replica, moving, residual, partial, *from_ring(partial))
+    )(served, residual, partial, *from_others(partial, "tp"))
     return (result[None], entries[None])
 
 

time: 72 us -> 71.6 us (level)
  local copies, waits for them, and re-layouts: 3.69 us -> 9.54 us
  Pallas kernels: 11.9 us -> 9.02 us
  starting transfers between devices: 15.3 us -> 12.9 us
  waiting for transfers between devices: 13.6 us -> 12.6 us
    ppermute x7 -> x3, waiting for transfers between devices: 13.6 us -> 2.25 us  [from_others(): lax.ppermute(value, axis, [(i, i ^ bits) for i in range(count)])]
    ppermute x7 -> x3, starting transfers between devices: 15.3 us -> 4.4 us  [from_others(): lax.ppermute(value, axis, [(i, i ^ bits) for i in range(count)])]
    all_to_all x0 -> x1, waiting for transfers between devices: none -> 10.4 us  [body(): partials = lax.all_to_all(partials, everyone, 0, 0, tiled=True)]
    all_to_all x0 -> x1, starting transfers between devices: none -> 8.46 us  [body(): partials = lax.all_to_all(partials, everyone, 0, 0, tiled=True)]
    unnamed x24 -> x26, local copies, waits for them, and re-layouts: 3.68 us -> 8.83 us
    pallas_call x1, Pallas kernels: 7.07 us -> 4.12 us  [body(): pl.pallas_call(attend_kernel, out_shape=shape((requests, WIDE), BF16), in...]
    pallas_call x3 -> x2, Pallas kernels: 1.83 us -> 2.21 us  [the longest x1 1.41 us: body(): pl.pallas_call(merge_kernel, out_shape=shape((count, rows, features), BF1...]
  transfers between devices with their start and end apart: 7 -> 4, of which waited for: 5 -> 3; matrix products, arithmetic and copies ran while one was open for 1% -> 0% of each run, Pallas kernels for 0% -> 0%
where the time goes in v2:
time: 71.6 us; the launch traced here: 71.1 us
  blocking collectives  26.3 us (37%)
  starting transfers between devices  12.9 us (18%)
  waiting for transfers between devices  12.6 us (18%)
  local copies, waits for them, and re-layouts  9.54 us (13%)
  Pallas kernels  9.02 us (13%)
    all_to_all x1, blocking collectives, body(): queries = lax.all_to_all(spread, 'kv', 0, 0, tiled=True)  14.4 us
    all_to_all x1, blocking collectives, body(): shares = lax.all_to_all(shares, 'kv', 0, 0, tiled=True)  11.9 us
    all_to_all x1, waiting for transfers between devices, body(): partials = lax.all_to_all(partials, everyone, 0, 0, tiled=True)  10.4 us
    unnamed x26, local copies, waits for them, and re-layouts  8.83 us
    all_to_all x1, starting transfers between devices, body(): partials = lax.all_to_all(partials, everyone, 0, 0, tiled=True)  8.46 us
    ppermute x3, starting transfers between devices, from_others(): lax.ppermute(value, axis, [(i, i ^ bits) for i in range(count)])  4.4 us
    pallas_call x1, Pallas kernels, body(): pl.pallas_call(attend_kernel, out_shape=shape((requests, WIDE), BF16), in...  4.12 us
    ppermute x3, waiting for transfers between devices, from_others(): lax.ppermute(value, axis, [(i, i ^ bits) for i in range(count)])  2.25 us
  transfers between devices with their start and end apart: 4, of which 3 were waited for; matrix products, arithmetic and copies ran while one was open for 0% of the time, Pallas kernels for 0%

profile of v2, /device:TPU:2, one launch (start us, length us, event | category | flops | bytes accessed | tf_op | source)
XLA Modules:
  0.0 71.1 jit_solution(8047857329440605482)
XLA Ops:
  0.6 0.0 copy-start.6
  0.6 0.0 copy-start.12
  0.7 0.7 broadcast_in_dim.12.gain
  1.4 0.1 pad_add_fusion.place
  1.4 0.0 copy-start.1
  1.4 1.7 %copy-done.1 = bf16[1280,960]{0,1:T(8,128)(2,1)S(1)} copy-done((bf16[1280,960]{0,1:T(8,128)(2,1)S(1)}, bf16[1280,960]{0,1:T(8,128)(2,1)}, u32[]{:S(2)}) %copy-start.1) | copy-done | bytes 2457624
  3.1 0.0 copy-start.5
  3.1 0.7 %copy-done.5 = bf16[8,1280]{1,0:T(8,128)(2,1)S(1)} copy-done((bf16[8,1280]{1,0:T(8,128)(2,1)S(1)}, bf16[8,1280]{1,0:T(8,128)(2,1)}, u32[]{:S(2)}) %copy-start.5) | copy-done | bytes 20504
  3.9 0.0 copy-start.7
  3.9 0.7 copy-done.7
  4.5 0.0 copy-start.8
  4.5 0.7 copy-done.8
  5.2 0.0 copy-start.2
  5.2 0.0 copy-start.3
  5.2 0.0 copy-start.4
  5.2 2.1 %project.1 = (bf16[256,384]{1,0:T(8,128)(2,1)S(1)}, bf16[8,384]{1,0:T(8,128)(2,1)S(1)}, f32[8,640]{1,0:T(8,128)S(1)}, f32[8,640]{1,0:T(8,128)}, f32[8,128]{1,0:T(8,128)S(1)}, /*index=5*/f32[8,128]{1,0:T(8,128)S(1)}) custom-call(s32[2]{0:T(128)S(1)} %pad_add_fusion.place, s32[256]{0:T(256)S(1)} %copy-done.7, s32[256]{0:T(256)S(1)} %copy-done.8, ...), custom_call_target="tpu_custom_call" | custom-call | tf_op jit(solution)/shard_map/project/pallas_call | solution.py:274
  7.3 14.4 %all_to_all.27 = bf16[32,8,384]{2,1,0:T(8,128)(2,1)S(1)} all-to-all(bf16[32,8,384]{2,1,0:T(8,128)(2,1)S(1)} %bitcast.17), channel_id=1, replica_groups=mesh['rep'=2,'kv'=32,'tp'=4] {'kv'}, dimensions={0} | all-to-all | bytes 393216 | tf_op jit(solution)/shard_map/all_to_all | solution.py:289
  21.7 0.0 copy-start
  21.7 3.0 %copy-done = bf16[1,11,512,640]{3,2,1,0:T(8,128)(2,1)S(1)} copy-done((bf16[1,11,512,640]{3,2,1,0:T(8,128)(2,1)S(1)}, bf16[1,11,512,640]{3,2,1,0:T(8,128)(2,1)}, u32[]{:S(2)}) %copy-start) | copy-done | bytes 7208984
  24.7 0.0 copy-start.9
  24.7 0.7 copy-done.9
  25.4 0.0 copy-start.10
  25.4 0.7 copy-done.10
  26.1 0.0 copy-start.11
  26.1 0.7 copy-done.11
  26.7 4.1 %attend.1 = bf16[256,384]{1,0:T(8,128)(2,1)S(1)} custom-call(s32[1,11]{1,0:T(1,128)S(1)} %copy-done.10, s32[1,11]{1,0:T(1,128)S(1)} %copy-done.11, s32[256]{0:T(256)S(1)} %copy-done.9, bf16[256,384]{1,0:T(8,128)(2,1)S(1)} %bitcast.15, bf16[11,512,640]{2,1,0:T(8,128)(2,1)S(1)} %bitcast.11), custom_call_target="tpu_custom_call" | custom-call | tf_op jit(solution)/shard_map/attend/pallas_call | solution.py:292
  30.8 11.9 %all_to_all.28 = bf16[32,8,384]{2,1,0:T(8,128)(2,1)S(1)} all-to-all(bf16[32,8,384]{2,1,0:T(8,128)(2,1)S(1)} %bitcast.16), channel_id=1, replica_groups=mesh['rep'=2,'kv'=32,'tp'=4] {'kv'}, dimensions={0} | all-to-all | bytes 393216 | tf_op jit(solution)/shard_map/all_to_all | solution.py:304
  42.7 0.0 copy-done.2
  42.7 1.4 %merge.1 = bf16[8,8,1280]{2,1,0:T(8,128)(2,1)} custom-call(bf16[256,384]{1,0:T(8,128)(2,1)S(1)} %bitcast.14, bf16[8,384]{1,0:T(8,128)(2,1)S(1)} %get-tuple-element.12.query, f32[8,640]{1,0:T(8,128)S(1)} %get-tuple-element.13.fresh, f32[8,128]{1,0:T(8,128)S(1)} %get-tuple-element.14.homed, bf16[320,1280]{1,0:T(8,128)(2,1)S(1)} %copy-done.2), custom_call_target="tpu_custom_call" | custom-call | tf_op jit(solution)/shard_map/merge/pallas_call | solution.py:308
  44.1 8.5 %all-to-all-start.2 = ((bf16[8,8,1280]{2,1,0:T(8,128)(2,1)}), bf16[8,8,1280]{2,1,0:T(8,128)(2,1)S(1)}, u32[]{:S(2)}, u32[]{:S(2)}) async-start(bf16[8,8,1280]{2,1,0:T(8,128)(2,1)} %merge.1), calls=%async_computation.2 | async-start | bytes 327680 | tf_op jit(solution)/shard_map/all_to_all | solution.py:316
  52.6 0.0 copy-done.12
  52.6 10.4 %all-to-all-done.2.shares = bf16[8,8,1280]{2,1,0:T(8,128)(2,1)S(1)} async-done(((bf16[8,8,1280]{2,1,0:T(8,128)(2,1)}), bf16[8,8,1280]{2,1,0:T(8,128)(2,1)S(1)}, u32[]{:S(2)}, u32[]{:S(2)}) %all-to-all-start.2) | async-done | bytes 163872 | tf_op jit(solution)/shard_map/all_to_all | solution.py:316
  63.0 0.0 copy-done.6
  63.0 0.0 copy-done.3
  63.0 0.0 copy-done.4
  63.0 0.8 %hidden.1 = (f32[8,1280]{1,0:T(8,128)S(1)}, bf16[8,1280]{1,0:T(8,128)(2,1)S(1)}) custom-call(bf16[8,1280]{1,0:T(8,128)(2,1)S(1)} %copy-done.6, bf16[8,8,1280]{2,1,0:T(8,128)(2,1)S(1)} %all-to-all-done.2.shares, f32[1,1280]{1,0:T(1,128)S(1)} %broadcast_in_dim.13.gain, bf16[320,1280]{1,0:T(8,128)(2,1)S(1)} %bitcast.13, bf16[320,1280]{1,0:T(8,128)(2,1)S(1)} %copy-done.4), custom_call_target="tpu_custom_call" | custom-call | tf_op jit(solution)/shard_map/hidden/pallas_call | solution.py:318
  63.8 0.6 collective-permute-start
  64.4 0.5 collective-permute-start.1
  64.9 3.3 %collective-permute-start.2 = (bf16[8,1280]{1,0:T(8,128)(2,1)S(1)}, bf16[8,1280]{1,0:T(8,128)(2,1)S(1)}, u32[]{:S(2)}, u32[]{:S(2)}) collective-permute-start(bf16[8,1280]{1,0:T(8,128)(2,1)S(1)} %get-tuple-element.16.own), channel_id=1, source_target_pairs={{0,3},{1,2},{2,1},{3,0},{4,7},{5,6},{6,5},{7,4},{8,11},{9,10},{10,... | collective-permute-start | bytes 61448 | tf_op jit(solution)/shard_map/ppermute | solution.py:249
  68.2 0.0 collective-permute-done.near
  68.2 0.9 %collective-permute-done.1.across = bf16[8,1280]{1,0:T(8,128)(2,1)S(1)} collective-permute-done((bf16[8,1280]{1,0:T(8,128)(2,1)S(1)}, bf16[8,1280]{1,0:T(8,128)(2,1)S(1)}, u32[]{:S(2)}, u32[]{:S(2)}) %collective-permute-start.1) | collective-permute-done | bytes 20512 | tf_op jit(solution)/shard_map/ppermute | solution.py:249
  69.1 1.4 %collective-permute-done.2.far = bf16[8,1280]{1,0:T(8,128)(2,1)S(1)} collective-permute-done((bf16[8,1280]{1,0:T(8,128)(2,1)S(1)}, bf16[8,1280]{1,0:T(8,128)(2,1)S(1)}, u32[]{:S(2)}, u32[]{:S(2)}) %collective-permute-start.2) | collective-permute-done | bytes 20512 | tf_op jit(solution)/shard_map/ppermute | solution.py:249
  70.5 0.6 finish.1
  (1 shorter events, 0.0 us)
Async XLA Ops:
  0.6 62.4 %copy-start.6 = (bf16[8,1280]{1,0:T(8,128)(2,1)S(1)}, bf16[8,1280]{1,0:T(8,128)(2,1)}, u32[]{:S(2)}) copy-start(bf16[8,1280]{1,0:T(8,128)(2,1)} %token_.3) | copy-start | bytes 61444
  0.6 52.0 %copy-start.12 = (f32[1280]{0:T(1024)S(1)}, f32[1280]{0:T(1024)}, u32[]{:S(2)}) copy-start(f32[1280]{0:T(1024)} %param.17) | copy-start | bytes 15364
  1.4 1.7 %copy-start.1 = (bf16[1280,960]{0,1:T(8,128)(2,1)S(1)}, bf16[1280,960]{0,1:T(8,128)(2,1)}, u32[]{:S(2)}) copy-start(bf16[1280,960]{0,1:T(8,128)(2,1)} %param.15) | copy-start | bytes 7372804
  3.1 0.7 %copy-start.5 = (bf16[8,1280]{1,0:T(8,128)(2,1)S(1)}, bf16[8,1280]{1,0:T(8,128)(2,1)}, u32[]{:S(2)}) copy-start(bf16[8,1280]{1,0:T(8,128)(2,1)} %token_.3) | copy-start | bytes 61444
  3.9 0.7 copy-start.7
  4.5 0.7 copy-start.8
  5.2 37.5 %copy-start.2 = (bf16[320,1280]{1,0:T(8,128)(2,1)S(1)}, bf16[320,1280]{1,0:T(8,128)(2,1)}, u32[]{:S(2)}) copy-start(bf16[320,1280]{1,0:T(8,128)(2,1)} %weight.1) | copy-start | bytes 2457604
  5.2 57.8 %copy-start.3 = (bf16[1280,320]{0,1:T(8,128)(2,1)S(1)}, bf16[1280,320]{0,1:T(8,128)(2,1)}, u32[]{:S(2)}) copy-start(bf16[1280,320]{0,1:T(8,128)(2,1)} %param.18) | copy-start | bytes 2457604
  5.2 57.8 %copy-start.4 = (bf16[320,1280]{1,0:T(8,128)(2,1)S(1)}, bf16[320,1280]{1,0:T(8,128)(2,1)}, u32[]{:S(2)}) copy-start(bf16[320,1280]{1,0:T(8,128)(2,1)} %down.1) | copy-start | bytes 2457604
  21.7 3.0 %copy-start = (bf16[1,11,512,640]{3,2,1,0:T(8,128)(2,1)S(1)}, bf16[1,11,512,640]{3,2,1,0:T(8,128)(2,1)}, u32[]{:S(2)}) copy-start(bf16[1,11,512,640]{3,2,1,0:T(8,128)(2,1)} %param.20) | copy-start | bytes 21626884
  24.7 0.7 copy-start.9
  25.4 0.7 copy-start.10
  26.1 0.7 copy-start.11
  44.1 18.9 %all-to-all-start.2 = ((bf16[8,8,1280]{2,1,0:T(8,128)(2,1)}), bf16[8,8,1280]{2,1,0:T(8,128)(2,1)S(1)}, u32[]{:S(2)}, u32[]{:S(2)}) async-start(bf16[8,8,1280]{2,1,0:T(8,128)(2,1)} %merge.1), calls=%async_computation.2 | async-start | bytes 327680 | tf_op jit(solution)/shard_map/all_to_all | solution.py:316
  63.8 4.4 %collective-permute-start = (bf16[8,1280]{1,0:T(8,128)(2,1)S(1)}, bf16[8,1280]{1,0:T(8,128)(2,1)S(1)}, u32[]{:S(2)}, u32[]{:S(2)}) collective-permute-start(bf16[8,1280]{1,0:T(8,128)(2,1)S(1)} %get-tuple-element.16.own), channel_id=1, source_target_pairs={{0,1},{1,0},{2,3},{3,2},{4,5},{5,4},{6,7},{7,6},{8,9},{9,8},{10,11... | collective-permute-start | bytes 61448 | tf_op jit(solution)/shard_map/ppermute | solution.py:249
  64.4 4.7 %collective-permute-start.1 = (bf16[8,1280]{1,0:T(8,128)(2,1)S(1)}, bf16[8,1280]{1,0:T(8,128)(2,1)S(1)}, u32[]{:S(2)}, u32[]{:S(2)}) collective-permute-start(bf16[8,1280]{1,0:T(8,128)(2,1)S(1)} %get-tuple-element.16.own), channel_id=1, source_target_pairs={{0,2},{1,3},{2,0},{3,1},{4,6},{5,7},{6,4},{7,5},{8,10},{9,11},{10,... | collective-permute-start | bytes 61448 | tf_op jit(solution)/shard_map/ppermute | solution.py:249
  64.9 5.6 %collective-permute-start.2 = (bf16[8,1280]{1,0:T(8,128)(2,1)S(1)}, bf16[8,1280]{1,0:T(8,128)(2,1)S(1)}, u32[]{:S(2)}, u32[]{:S(2)}) collective-permute-start(bf16[8,1280]{1,0:T(8,128)(2,1)S(1)} %get-tuple-element.16.own), channel_id=1, source_target_pairs={{0,3},{1,2},{2,1},{3,0},{4,7},{5,6},{6,5},{7,4},{8,11},{9,10},{10,... | collective-permute-start | bytes 61448 | tf_op jit(solution)/shard_map/ppermute | solution.py:249

commit v3 on v2

--- a/solution.py
+++ b/solution.py
@@ -11,14 +11,20 @@
 PAIR = 2 * HD
 VERY_LOW = -1e30
 NORM_EPS = 1e-06
+EARLY = 3
 STATS = 320
 WIDE = 384
 F32 = jnp.float32
 BF16 = jnp.bfloat16
 
 VMEM = pl.BlockSpec(memory_space=pltpu.VMEM)
+HBM = pl.BlockSpec(memory_space=pltpu.HBM)
 SMEM = pl.BlockSpec(memory_space=pltpu.SMEM)
 PARAMS = pltpu.CompilerParams(vmem_limit_bytes=16 * 1024 * 1024)
+
+
+def in_hbm(*arrays):
+    return [pltpu.with_memory_space_constraint(a, pltpu.HBM) for a in arrays]
 
 
 def iota(shape, axis):
@@ -53,12 +59,25 @@
     return lax.dot_general(left, right, (((1,), (1,)), ((), ())), preferred_element_type=F32)
 
 
+def fetch(pairs, sems):
+    copies = [pltpu.make_async_copy(a, b, sems.at[i]) for i, (a, b) in enumerate(pairs)]
+    for copy in copies:
+        copy.start()
+    return copies
+
+
 def project_kernel(
-    place, home, moving, token, gain, weight, spread, query, fresh, entries, homed, served
+    token_hbm, gain_hbm, weight_hbm, spread, query, fresh, token, gain, weight, sems
 ):
     rows = token.shape[0]
     heads = weight.shape[0] // (3 * HD)
+    copies = fetch(
+        [(token_hbm, token), (gain_hbm, gain.at[0]), (weight_hbm, weight)], sems
+    )
+    copies[0].wait()
+    copies[1].wait()
     normed = root_norm(token[...].astype(F32), gain[...]).astype(BF16)
+    copies[2].wait()
     projected = dot_transposed(normed, weight[...])
     own = jnp.concatenate(
         [projected[:, h * 3 * HD : h * 3 * HD + HD] for h in range(heads)]
@@ -69,29 +88,86 @@
     query[...] = own
     for copy in range(spread.shape[0] // rows):
         spread[copy * rows : (copy + 1) * rows, :] = own
-    pairs = jnp.concatenate(
+    fresh[...] = jnp.concatenate(
         [projected[:, h * 3 * HD + HD : (h + 1) * 3 * HD] for h in range(heads)], axis=1
     )
-    fresh[...] = pairs
+
+
+def side_kernel(
+    place,
+    owner_hbm,
+    index_hbm,
+    length_hbm,
+    home_hbm,
+    moving_hbm,
+    cache_hbm,
+    fresh,
+    cache,
+    owners,
+    remains,
+    entries,
+    homed,
+    served,
+    owner,
+    index,
+    length,
+    home,
+    moving,
+    sems,
+):
+    rows = fresh.shape[0]
+    blocks, tokens, _ = cache_hbm.shape
+    requests = length.shape[0]
+    copies = fetch(
+        [
+            (owner_hbm, owner),
+            (index_hbm, index),
+            (length_hbm, length),
+            (home_hbm, home),
+            (moving_hbm, moving),
+            (cache_hbm.at[: cache.shape[0]], cache),
+        ],
+        sems,
+    )
+    for copy in copies[:5]:
+        copy.wait()
+    row = iota(owners.shape, 0)
+    holders = jnp.full(owners.shape, requests, jnp.int32)
+    left = jnp.zeros(owners.shape, jnp.int32)
+    for b in range(blocks):
+        holder = owner[0, b]
+        most = jnp.where(holder < requests, length[jnp.minimum(holder, requests - 1)], 0)
+        holders = jnp.where(row == b, holder, holders)
+        left = jnp.where(row == b, most - index[0, b] * tokens, left)
+    owners[...] = holders
+    remains[...] = left
     start = place[1] * rows
     at_home = row_values(home, start, rows, 128)
     target = at_home ^ row_values(moving, start, rows, 128)
     homed[...] = jnp.where(at_home == place[0], 1.0, 0.0)
     serves = jnp.where(target == place[0], 1.0, 0.0)
     served[...] = serves
+    pairs = fresh[...]
     entries[...] = jnp.where(widen(serves, pairs.shape[1]) > 0.0, pairs, 0.0)
-
-
-def attend_kernel(owner, index, length, queries, cache, out, scores, sums):
-    blocks, tokens, width = cache.shape
+    copies[5].wait()
+
+
+def attend_kernel(
+    owner_of, remains, queries, early, cache_hbm, out, late, scores, sums, sems
+):
+    blocks, tokens, width = cache_hbm.shape
+    ready = early.shape[0]
+    copies = fetch(
+        [(cache_hbm.at[b], late.at[b - ready]) for b in range(ready, blocks)], sems
+    )
+
+    def cache(b):
+        return early[b] if b < ready else late[b - ready]
+
     heads = width // PAIR
     requests = queries.shape[0]
     rows = sums.shape[0]
-    row = iota((rows, 1), 0)
-    owners = jnp.full((rows, 1), requests, jnp.int32)
-    for b in range(blocks):
-        owners = jnp.where(row == b, owner[0, b], owners)
-    onehot = (iota((rows, requests), 1) == owners).astype(BF16)
+    onehot = (iota((rows, requests), 1) == widen(owner_of[...], requests)).astype(BF16)
     picked = jnp.dot(onehot, queries[...], preferred_element_type=F32)
     picked = jnp.concatenate([picked, jnp.zeros((rows, width - WIDE), F32)], axis=1)
     lane = iota((rows, width), 1)
@@ -102,34 +178,34 @@
     head_lane = iota((8, width), 1) - PAIR * iota((8, width), 0)
     key_lanes = (head_lane >= 0) & (head_lane < HD)
     value_lanes = (head_lane >= HD) & (head_lane < PAIR)
+    block_lane = iota((8, 128), 1)
+    token_lane = iota((8, tokens), 1)
+    every_peak = jnp.full((8, 128), VERY_LOW, F32)
+    holders = jnp.full((8, 128), requests, jnp.int32)
     usable = []
-    peaks = []
     for b in range(blocks):
         ask = jnp.where(key_lanes, jnp.broadcast_to(spread[b : b + 1], (8, width)), 0.0)
-        score = dot_transposed(ask.astype(BF16), cache[b])
-        holder = owner[0, b]
-        most = jnp.where(holder < requests, length[jnp.minimum(holder, requests - 1)], 0)
-        use = iota((8, tokens), 1) < most - index[0, b] * tokens
+        if b >= ready:
+            copies[b - ready].wait()
+        score = dot_transposed(ask.astype(BF16), cache(b))
+        use = token_lane < widen(jnp.broadcast_to(remains[b : b + 1, :], (8, 128)), tokens)
         score = jnp.where(use, score, VERY_LOW)
         scores[b] = score
         usable.append(use)
-        peaks.append(jnp.max(score, axis=1, keepdims=True))
-    joint = []
-    for b in range(blocks):
-        peak = peaks[b]
-        for c in range(blocks):
-            if c != b:
-                peak = jnp.maximum(peak, jnp.where(owner[0, c] == owner[0, b], peaks[c], VERY_LOW))
-        joint.append(peak)
+        peak = jnp.max(score, axis=1, keepdims=True)
+        every_peak = jnp.where(block_lane == b, peak, every_peak)
+        holders = jnp.where(block_lane == b, owner_of[b : b + 1, :], holders)
     stat_lane = iota((8, 128), 1) - (STATS - 256)
     stat_row = iota((8, 128), 0)
     stats = []
     for b in range(blocks):
-        weights = jnp.where(usable[b], jnp.exp(scores[b] - joint[b]), 0.0)
+        peers = jnp.where(holders == owner_of[b : b + 1, :], every_peak, VERY_LOW)
+        joint = jnp.max(peers, axis=1, keepdims=True)
+        weights = jnp.where(usable[b], jnp.exp(scores[b] - joint), 0.0)
         total = jnp.sum(weights, axis=1, keepdims=True)
-        acc = jnp.dot(weights.astype(BF16), cache[b], preferred_element_type=F32)
+        acc = jnp.dot(weights.astype(BF16), cache(b), preferred_element_type=F32)
         sums[b : b + 1, :] = jnp.sum(jnp.where(value_lanes, acc, 0.0), axis=0, keepdims=True)
-        stat = jnp.where(stat_lane == stat_row, joint[b], 0.0)
+        stat = jnp.where(stat_lane == stat_row, joint, 0.0)
         stat = stat + jnp.where(stat_lane == stat_row + 8, total, 0.0)
         stats.append(jnp.sum(jnp.where(stat_row < heads, stat, 0.0), axis=0, keepdims=True))
     stats += [jnp.zeros((1, 128), F32)] * (rows - blocks)
@@ -143,12 +219,12 @@
     packed = packed[:, :WIDE]
     added = jnp.zeros((rows, WIDE), F32)
     totals = jnp.zeros((rows, 128), F32)
-    first = row < blocks
+    first = iota((rows, 128), 0) < blocks
     for b in range(blocks):
-        same = owners == owner[0, b]
-        added = added + jnp.where(same, packed[b : b + 1], 0.0)
+        same = owner_of[...] == owner_of[b : b + 1, :]
+        added = added + jnp.where(widen(same, WIDE), packed[b : b + 1], 0.0)
         totals = totals + jnp.where(same, stats[b : b + 1], 0.0)
-        first = first & ((row <= b) | ~same)
+        first = first & ((iota((rows, 128), 0) <= b) | ~same)
     tail = iota((rows, 128), 1) - (STATS - 256)
     peak_part = jnp.where((tail >= 0) & (tail < 8), stats, 0.0)
     total_part = jnp.where((tail >= 8) & (tail < 16), totals, 0.0)
@@ -159,10 +235,10 @@
         parts = parts + (part if k == 0 else pltpu.roll(part, 16 * k, 1))
     last = jnp.where(tail >= 0, parts, added[:, 256:])
     full = jnp.concatenate([added[:, :256], last], axis=1)
-    full = jnp.where(first, full, 0.0).astype(BF16)
-    place = (iota((rows, requests), 1) == owners) & first
+    keep = jnp.where(first, 1.0, 0.0)
+    full = jnp.where(widen(keep, WIDE) > 0.0, full, 0.0).astype(BF16)
     out[...] = lax.dot_general(
-        place.astype(F32).astype(BF16),
+        onehot,
         full,
         (((0,), (0,)), ((), ())),
         preferred_element_type=F32,
@@ -271,36 +347,75 @@
     _, blocks, tokens, width = kv_cache.shape
     place = jnp.stack([lax.axis_index("rep"), lax.axis_index("kv")]).astype(jnp.int32)
 
-    spread, query, fresh, entries, homed, served = pl.pallas_call(
+    spread, query, fresh = pl.pallas_call(
         project_kernel,
         out_shape=(
             shape((requests, WIDE), BF16),
             shape((rows, WIDE), BF16),
             shape((rows, width), F32),
+        ),
+        in_specs=[HBM] * 3,
+        out_specs=(VMEM,) * 3,
+        scratch_shapes=[
+            pltpu.VMEM((rows, features), BF16),
+            pltpu.VMEM((1, features), F32),
+            pltpu.VMEM(qkv_weight.shape[::-1], BF16),
+            pltpu.SemaphoreType.DMA((3,)),
+        ],
+        compiler_params=PARAMS,
+        name="project",
+    )(*in_hbm(token_state, attn_gain, qkv_weight.T))
+    queries = lax.all_to_all(spread, "kv", 0, 0, tiled=True)
+
+    padded = -(-blocks // 16) * 16
+    early, owners, remains, entries, homed, served = pl.pallas_call(
+        side_kernel,
+        out_shape=(
+            pltpu.VMEM((EARLY, tokens, width), BF16),
+            shape((padded, 128), jnp.int32),
+            shape((padded, 128), jnp.int32),
             shape((rows, width), F32),
             shape((rows, 128), F32),
             shape((rows, 128), F32),
         ),
-        in_specs=[SMEM] * 3 + [VMEM] * 3,
+        in_specs=[SMEM] + [HBM] * 6 + [VMEM],
         out_specs=(VMEM,) * 6,
-        compiler_params=PARAMS,
-        name="project",
-    )(place, home_replica, moving, token_state, attn_gain[None], qkv_weight.T)
-    queries = lax.all_to_all(spread, "kv", 0, 0, tiled=True)
-
-    padded = -(-blocks // 16) * 16
+        scratch_shapes=[pltpu.SMEM((1, blocks), jnp.int32)] * 2
+        + [pltpu.SMEM((requests,), jnp.int32)] * 3
+        + [pltpu.SemaphoreType.DMA((6,))],
+        compiler_params=PARAMS,
+        cost_estimate=pl.CostEstimate(
+            flops=0, bytes_accessed=2 * EARLY * tokens * width * 2, transcendentals=0
+        ),
+        name="side",
+    )(
+        place,
+        *in_hbm(
+            block_owner, block_index, cache_length, home_replica, moving, kv_cache[0]
+        ),
+        fresh,
+    )
+
     shares = pl.pallas_call(
         attend_kernel,
         out_shape=shape((requests, WIDE), BF16),
-        in_specs=[SMEM] * 3 + [VMEM] * 2,
+        in_specs=[VMEM] * 4 + [HBM],
         out_specs=VMEM,
         scratch_shapes=[
+            pltpu.VMEM((blocks - EARLY, tokens, width), BF16),
             pltpu.VMEM((blocks, 8, tokens), F32),
             pltpu.VMEM((padded, width), F32),
+            pltpu.SemaphoreType.DMA((blocks - EARLY,)),
         ],
         compiler_params=PARAMS,
         name="attend",
-    )(block_owner, block_index, cache_length, queries, kv_cache[0])
+    )(
+        owners,
+        remains,
+        queries,
+        pltpu.with_memory_space_constraint(early, pltpu.VMEM),
+        *in_hbm(kv_cache[0]),
+    )
     shares = lax.all_to_all(shares, "kv", 0, 0, tiled=True)
 
     everyone = ("rep", "tp")

time: 71.6 us -> 65.3 us (0.912); the launches traced: 71.1 us -> 64.1 us
  blocking collectives: 26.3 us -> 12 us
  local copies, waits for them, and re-layouts: 9.54 us -> 0.03 us
  starting transfers between devices: 12.9 us -> 20.5 us
  Pallas kernels: 9.02 us -> 14.5 us
  waiting for transfers between devices: 12.6 us -> 16.3 us
    all_to_all x1 -> x0, blocking collectives: 14.4 us -> none  [body(): queries = lax.all_to_all(spread, 'kv', 0, 0, tiled=True)]
    unnamed x26 -> x10, local copies, waits for them, and re-layouts: 8.83 us -> 0.02 us
    all_to_all x0 -> x1, starting transfers between devices: none -> 7.63 us  [body(): queries = lax.all_to_all(spread, 'kv', 0, 0, tiled=True)]
    all_to_all x0 -> x1, waiting for transfers between devices: none -> 4.15 us  [body(): queries = lax.all_to_all(spread, 'kv', 0, 0, tiled=True)]
    pallas_call x0 -> x1, Pallas kernels: none -> 2.75 us  [body(): pl.pallas_call(side_kernel, out_shape=(pltpu.VMEM((EARLY, tokens, width),...]
    pallas_call x1, Pallas kernels: 4.12 us -> 5.56 us  [body(): pl.pallas_call(attend_kernel, out_shape=shape((requests, WIDE), BF16), in...]
    pallas_call x1, Pallas kernels: 2.06 us -> 3.29 us  [body(): pl.pallas_call(project_kernel, out_shape=(shape((requests, WIDE), BF16),...]
  transfers between devices with their start and end apart: 4 -> 5, of which waited for: 3 -> 4; matrix products, arithmetic and copies ran while one was open for 0% -> 0% of each run, Pallas kernels for 0% -> 4%
where the time goes in v3:
time: 65.3 us; the launch traced here: 64.1 us
  starting transfers between devices  20.5 us (31%)
  waiting for transfers between devices  16.3 us (25%)
  Pallas kernels  14.5 us (22%)
  blocking collectives  12 us (18%)
  between operations  0.71 us (1%)
    all_to_all x1, blocking collectives, body(): shares = lax.all_to_all(shares, 'kv', 0, 0, tiled=True)  12 us
    all_to_all x1, waiting for transfers between devices, body(): partials = lax.all_to_all(partials, everyone, 0, 0, tiled=True)  10.4 us
    all_to_all x1, starting transfers between devices, body(): partials = lax.all_to_all(partials, everyone, 0, 0, tiled=True)  8.47 us
    all_to_all x1, starting transfers between devices, body(): queries = lax.all_to_all(spread, 'kv', 0, 0, tiled=True)  7.63 us
    pallas_call x1, Pallas kernels, body(): pl.pallas_call(attend_kernel, out_shape=shape((requests, WIDE), BF16), in...  5.56 us
    ppermute x3, starting transfers between devices, from_others(): lax.ppermute(value, axis, [(i, i ^ bits) for i in range(count)])  4.4 us
    all_to_all x1, waiting for transfers between devices, body(): queries = lax.all_to_all(spread, 'kv', 0, 0, tiled=True)  4.15 us
    pallas_call x1, Pallas kernels, body(): pl.pallas_call(project_kernel, out_shape=(shape((requests, WIDE), BF16),...  3.29 us
  transfers between devices with their start and end apart: 5, of which 4 were waited for; matrix products, arithmetic and copies ran while one was open for 0% of the time, Pallas kernels for 4%

profile of v3, /device:TPU:2, one launch (start us, length us, event | category | flops | bytes accessed | tf_op | source)
XLA Modules:
  0.0 64.1 jit_solution(8884050699857153263)
XLA Ops:
  0.6 3.3 %project.1 = (bf16[256,384]{1,0:T(8,128)(2,1)}, bf16[8,384]{1,0:T(8,128)(2,1)S(1)}, f32[8,640]{1,0:T(8,128)S(1)}) custom-call(bf16[8,1280]{1,0:T(8,128)(2,1)} %token_.1, f32[1280]{0:T(1024)} %gain_hbm.1, bf16[960,1280]{1,0:T(8,128)(2,1)} %bitcast.17), custom_call_target="tpu_custom_call" | custom-call | tf_op jit(solution)/shard_map/project/pallas_call | solution.py:350
  3.9 7.6 %all-to-all-start = ((bf16[32,8,384]{2,1,0:T(8,128)(2,1)}), bf16[32,8,384]{2,1,0:T(8,128)(2,1)S(1)}, u32[]{:S(2)}, u32[]{:S(2)}) async-start(bf16[32,8,384]{2,1,0:T(8,128)(2,1)} %bitcast.4), calls=%async_computation | async-start | bytes 393216 | tf_op jit(solution)/shard_map/all_to_all | solution.py:368
  11.6 0.1 pad_add_fusion.place
  11.7 2.7 %side.1 = (bf16[3,512,640]{2,1,0:T(8,128)(2,1)S(1)}, s32[16,128]{1,0:T(8,128)S(1)}, s32[16,128]{1,0:T(8,128)S(1)}, f32[8,640]{1,0:T(8,128)}, f32[8,128]{1,0:T(8,128)S(1)}, /*index=5*/f32[8,128]{1,0:T(8,128)S(1)}) custom-call(s32[2]{0:T(128)S(1)} %pad_add_fusion.place, s32[1,11]{1,0:T(1,128)} %owner_hbm.1, s32[1,11]{1,0:T(1,128)} %index_hbm.1, ...), custom_call_target="tpu_custom_call" | custom-call | bytes 3932160 | tf_op jit(solution)/shard_map/side/pallas_call | solution.py:371
  14.4 4.2 %all-to-all-done = bf16[32,8,384]{2,1,0:T(8,128)(2,1)S(1)} async-done(((bf16[32,8,384]{2,1,0:T(8,128)(2,1)}), bf16[32,8,384]{2,1,0:T(8,128)(2,1)S(1)}, u32[]{:S(2)}, u32[]{:S(2)}) %all-to-all-start) | async-done | bytes 196640 | tf_op jit(solution)/shard_map/all_to_all | solution.py:368
  18.6 0.0 copy-start
  18.6 0.0 copy-start.4
  18.6 0.0 copy-start.3
  18.6 5.6 %attend.1 = bf16[256,384]{1,0:T(8,128)(2,1)S(1)} custom-call(s32[16,128]{1,0:T(8,128)S(1)} %get-tuple-element.15.owner_of, s32[16,128]{1,0:T(8,128)S(1)} %get-tuple-element.16.remains, bf16[256,384]{1,0:T(8,128)(2,1)S(1)} %bitcast.13, bf16[3,512,640]{2,1,0:T(8,128)(2,1)S(1)} %get-tuple-element.18.early, bf16[11,512,640]{2,1,0:T(8,128)(2,1)} %bitcast.16), custom_call_target="tpu_custom_call" | custom-call | tf_op jit(solution)/shard_map/attend/pallas_call | solution.py:399
  24.1 0.0 copy-start.1
  24.1 0.0 copy-start.2
  24.2 12.0 %all_to_all.27 = bf16[32,8,384]{2,1,0:T(8,128)(2,1)S(1)} all-to-all(bf16[32,8,384]{2,1,0:T(8,128)(2,1)S(1)} %bitcast.14), channel_id=1, replica_groups=mesh['rep'=2,'kv'=32,'tp'=4] {'kv'}, dimensions={0} | all-to-all | bytes 393216 | tf_op jit(solution)/shard_map/all_to_all | solution.py:419
  36.2 0.0 copy-done
  36.2 1.4 %merge.1 = bf16[8,8,1280]{2,1,0:T(8,128)(2,1)} custom-call(bf16[256,384]{1,0:T(8,128)(2,1)S(1)} %bitcast.12, bf16[8,384]{1,0:T(8,128)(2,1)S(1)} %get-tuple-element.19.query, f32[8,640]{1,0:T(8,128)S(1)} %get-tuple-element.13.fresh, f32[8,128]{1,0:T(8,128)S(1)} %get-tuple-element.20.homed, bf16[320,1280]{1,0:T(8,128)(2,1)S(1)} %copy-done), custom_call_target="tpu_custom_call" | custom-call | tf_op jit(solution)/shard_map/merge/pallas_call | solution.py:423
  37.6 8.5 %all-to-all-start.2 = ((bf16[8,8,1280]{2,1,0:T(8,128)(2,1)}), bf16[8,8,1280]{2,1,0:T(8,128)(2,1)S(1)}, u32[]{:S(2)}, u32[]{:S(2)}) async-start(bf16[8,8,1280]{2,1,0:T(8,128)(2,1)} %merge.1), calls=%async_computation.2 | async-start | bytes 327680 | tf_op jit(solution)/shard_map/all_to_all | solution.py:431
  46.0 0.0 copy-done.4
  46.1 10.4 %all-to-all-done.2.shares = bf16[8,8,1280]{2,1,0:T(8,128)(2,1)S(1)} async-done(((bf16[8,8,1280]{2,1,0:T(8,128)(2,1)}), bf16[8,8,1280]{2,1,0:T(8,128)(2,1)S(1)}, u32[]{:S(2)}, u32[]{:S(2)}) %all-to-all-start.2) | async-done | bytes 163872 | tf_op jit(solution)/shard_map/all_to_all | solution.py:431
  56.4 0.0 copy-done.3
  56.4 0.0 copy-done.1
  56.5 0.0 copy-done.2
  56.5 0.8 %hidden.1 = (f32[8,1280]{1,0:T(8,128)S(1)}, bf16[8,1280]{1,0:T(8,128)(2,1)S(1)}) custom-call(bf16[8,1280]{1,0:T(8,128)(2,1)S(1)} %copy-done.3, bf16[8,8,1280]{2,1,0:T(8,128)(2,1)S(1)} %all-to-all-done.2.shares, f32[1,1280]{1,0:T(1,128)S(1)} %broadcast_in_dim.9.gain, bf16[320,1280]{1,0:T(8,128)(2,1)S(1)} %bitcast.11, bf16[320,1280]{1,0:T(8,128)(2,1)S(1)} %copy-done.2), custom_call_target="tpu_custom_call" | custom-call | tf_op jit(solution)/shard_map/hidden/pallas_call | solution.py:433
  57.3 0.5 collective-permute-start.2
  57.8 1.5 %collective-permute-start.1 = (bf16[8,1280]{1,0:T(8,128)(2,1)S(1)}, bf16[8,1280]{1,0:T(8,128)(2,1)S(1)}, u32[]{:S(2)}, u32[]{:S(2)}) collective-permute-start(bf16[8,1280]{1,0:T(8,128)(2,1)S(1)} %get-tuple-element.22.own), channel_id=1, source_target_pairs={{0,2},{1,3},{2,0},{3,1},{4,6},{5,7},{6,4},{7,5},{8,10},{9,11},{10,... | collective-permute-start | bytes 61448 | tf_op jit(solution)/shard_map/ppermute | solution.py:325
  59.3 2.4 %collective-permute-start = (bf16[8,1280]{1,0:T(8,128)(2,1)S(1)}, bf16[8,1280]{1,0:T(8,128)(2,1)S(1)}, u32[]{:S(2)}, u32[]{:S(2)}) collective-permute-start(bf16[8,1280]{1,0:T(8,128)(2,1)S(1)} %get-tuple-element.22.own), channel_id=1, source_target_pairs={{0,1},{1,0},{2,3},{3,2},{4,5},{5,4},{6,7},{7,6},{8,9},{9,8},{10,11... | collective-permute-start | bytes 61448 | tf_op jit(solution)/shard_map/ppermute | solution.py:325
  61.7 1.2 %collective-permute-done.2.far = bf16[8,1280]{1,0:T(8,128)(2,1)S(1)} collective-permute-done((bf16[8,1280]{1,0:T(8,128)(2,1)S(1)}, bf16[8,1280]{1,0:T(8,128)(2,1)S(1)}, u32[]{:S(2)}, u32[]{:S(2)}) %collective-permute-start.2) | collective-permute-done | bytes 20512 | tf_op jit(solution)/shard_map/ppermute | solution.py:325
  62.9 0.0 collective-permute-done.1.across
  62.9 0.6 collective-permute-done.near
  63.4 0.6 finish.1
  (1 shorter events, 0.0 us)
Async XLA Ops:
  3.9 14.6 %all-to-all-start = ((bf16[32,8,384]{2,1,0:T(8,128)(2,1)}), bf16[32,8,384]{2,1,0:T(8,128)(2,1)S(1)}, u32[]{:S(2)}, u32[]{:S(2)}) async-start(bf16[32,8,384]{2,1,0:T(8,128)(2,1)} %bitcast.4), calls=%async_computation | async-start | bytes 393216 | tf_op jit(solution)/shard_map/all_to_all | solution.py:368
  18.6 17.6 %copy-start = (bf16[320,1280]{1,0:T(8,128)(2,1)S(1)}, bf16[320,1280]{1,0:T(8,128)(2,1)}, u32[]{:S(2)}) copy-start(bf16[320,1280]{1,0:T(8,128)(2,1)} %weight.1) | copy-start | bytes 2457604
  18.6 27.5 %copy-start.4 = (f32[1280]{0:T(1024)S(1)}, f32[1280]{0:T(1024)}, u32[]{:S(2)}) copy-start(f32[1280]{0:T(1024)} %param.17) | copy-start | bytes 15364
  18.6 37.9 %copy-start.3 = (bf16[8,1280]{1,0:T(8,128)(2,1)S(1)}, bf16[8,1280]{1,0:T(8,128)(2,1)}, u32[]{:S(2)}) copy-start(bf16[8,1280]{1,0:T(8,128)(2,1)} %token_.1) | copy-start | bytes 61444
  24.1 32.3 %copy-start.1 = (bf16[1280,320]{0,1:T(8,128)(2,1)S(1)}, bf16[1280,320]{0,1:T(8,128)(2,1)}, u32[]{:S(2)}) copy-start(bf16[1280,320]{0,1:T(8,128)(2,1)} %param.18) | copy-start | bytes 2457604
  24.1 32.3 %copy-start.2 = (bf16[320,1280]{1,0:T(8,128)(2,1)S(1)}, bf16[320,1280]{1,0:T(8,128)(2,1)}, u32[]{:S(2)}) copy-start(bf16[320,1280]{1,0:T(8,128)(2,1)} %down.1) | copy-start | bytes 2457604
  37.6 18.9 %all-to-all-start.2 = ((bf16[8,8,1280]{2,1,0:T(8,128)(2,1)}), bf16[8,8,1280]{2,1,0:T(8,128)(2,1)S(1)}, u32[]{:S(2)}, u32[]{:S(2)}) async-start(bf16[8,8,1280]{2,1,0:T(8,128)(2,1)} %merge.1), calls=%async_computation.2 | async-start | bytes 327680 | tf_op jit(solution)/shard_map/all_to_all | solution.py:431
  57.3 5.6 %collective-permute-start.2 = (bf16[8,1280]{1,0:T(8,128)(2,1)S(1)}, bf16[8,1280]{1,0:T(8,128)(2,1)S(1)}, u32[]{:S(2)}, u32[]{:S(2)}) collective-permute-start(bf16[8,1280]{1,0:T(8,128)(2,1)S(1)} %get-tuple-element.22.own), channel_id=1, source_target_pairs={{0,3},{1,2},{2,1},{3,0},{4,7},{5,6},{6,5},{7,4},{8,11},{9,10},{10,... | collective-permute-start | bytes 61448 | tf_op jit(solution)/shard_map/ppermute | solution.py:325
  57.8 5.1 %collective-permute-start.1 = (bf16[8,1280]{1,0:T(8,128)(2,1)S(1)}, bf16[8,1280]{1,0:T(8,128)(2,1)S(1)}, u32[]{:S(2)}, u32[]{:S(2)}) collective-permute-start(bf16[8,1280]{1,0:T(8,128)(2,1)S(1)} %get-tuple-element.22.own), channel_id=1, source_target_pairs={{0,2},{1,3},{2,0},{3,1},{4,6},{5,7},{6,4},{7,5},{8,10},{9,11},{10,... | collective-permute-start | bytes 61448 | tf_op jit(solution)/shard_map/ppermute | solution.py:325
  59.3 4.1 %collective-permute-start = (bf16[8,1280]{1,0:T(8,128)(2,1)S(1)}, bf16[8,1280]{1,0:T(8,128)(2,1)S(1)}, u32[]{:S(2)}, u32[]{:S(2)}) collective-permute-start(bf16[8,1280]{1,0:T(8,128)(2,1)S(1)} %get-tuple-element.22.own), channel_id=1, source_target_pairs={{0,1},{1,0},{2,3},{3,2},{4,5},{5,4},{6,7},{7,6},{8,9},{9,8},{10,11... | collective-permute-start | bytes 61448 | tf_op jit(solution)/shard_map/ppermute | solution.py:325

commit v4 on v3

--- a/solution.py
+++ b/solution.py
@@ -11,7 +11,7 @@
 PAIR = 2 * HD
 VERY_LOW = -1e30
 NORM_EPS = 1e-06
-EARLY = 3
+EARLY = 4
 STATS = 320
 WIDE = 384
 F32 = jnp.float32
@@ -66,31 +66,30 @@
     return copies
 
 
-def project_kernel(
-    token_hbm, gain_hbm, weight_hbm, spread, query, fresh, token, gain, weight, sems
+def query_kernel(
+    token_hbm, gain_hbm, weight_hbm, spread, query, normed, token, gain, weight, sems
 ):
     rows = token.shape[0]
-    heads = weight.shape[0] // (3 * HD)
+    heads = weight_hbm.shape[0] // (3 * HD)
     copies = fetch(
-        [(token_hbm, token), (gain_hbm, gain.at[0]), (weight_hbm, weight)], sems
-    )
+        [(token_hbm, token), (gain_hbm, gain.at[0])]
+        + [
+            (weight_hbm.at[3 * HD * h : 3 * HD * h + HD], weight.at[HD * h : HD * (h + 1)])
+            for h in range(heads)
+        ],
+        sems,
+    )
+    weight[heads * HD :, :] = jnp.zeros((WIDE - heads * HD, weight.shape[1]), BF16)
     copies[0].wait()
     copies[1].wait()
-    normed = root_norm(token[...].astype(F32), gain[...]).astype(BF16)
-    copies[2].wait()
-    projected = dot_transposed(normed, weight[...])
-    own = jnp.concatenate(
-        [projected[:, h * 3 * HD : h * 3 * HD + HD] for h in range(heads)]
-        + [jnp.zeros((rows, WIDE - heads * HD), F32)],
-        axis=1,
-    )
-    own = (own * HD ** (-0.5)).astype(BF16)
+    norm = root_norm(token[...].astype(F32), gain[...]).astype(BF16)
+    normed[...] = norm
+    for copy in copies[2:]:
+        copy.wait()
+    own = (dot_transposed(norm, weight[...]) * HD ** (-0.5)).astype(BF16)
     query[...] = own
     for copy in range(spread.shape[0] // rows):
         spread[copy * rows : (copy + 1) * rows, :] = own
-    fresh[...] = jnp.concatenate(
-        [projected[:, h * 3 * HD + HD : (h + 1) * 3 * HD] for h in range(heads)], axis=1
-    )
 
 
 def side_kernel(
@@ -101,10 +100,12 @@
     home_hbm,
     moving_hbm,
     cache_hbm,
-    fresh,
+    weight_hbm,
+    normed,
     cache,
     owners,
     remains,
+    fresh,
     entries,
     homed,
     served,
@@ -113,10 +114,12 @@
     length,
     home,
     moving,
+    weight,
     sems,
 ):
-    rows = fresh.shape[0]
+    rows = normed.shape[0]
     blocks, tokens, _ = cache_hbm.shape
+    heads = weight_hbm.shape[0] // (3 * HD)
     requests = length.shape[0]
     copies = fetch(
         [
@@ -125,8 +128,15 @@
             (length_hbm, length),
             (home_hbm, home),
             (moving_hbm, moving),
-            (cache_hbm.at[: cache.shape[0]], cache),
-        ],
+        ]
+        + [
+            (
+                weight_hbm.at[3 * HD * h + HD : 3 * HD * (h + 1)],
+                weight.at[PAIR * h : PAIR * (h + 1)],
+            )
+            for h in range(heads)
+        ]
+        + [(cache_hbm.at[: cache.shape[0]], cache)],
         sems,
     )
     for copy in copies[:5]:
@@ -147,13 +157,16 @@
     homed[...] = jnp.where(at_home == place[0], 1.0, 0.0)
     serves = jnp.where(target == place[0], 1.0, 0.0)
     served[...] = serves
-    pairs = fresh[...]
+    for copy in copies[5:-1]:
+        copy.wait()
+    pairs = dot_transposed(normed[...], weight[...])
+    fresh[...] = pairs
     entries[...] = jnp.where(widen(serves, pairs.shape[1]) > 0.0, pairs, 0.0)
-    copies[5].wait()
+    copies[-1].wait()
 
 
 def attend_kernel(
-    owner_of, remains, queries, early, cache_hbm, out, late, scores, sums, sems
+    owner_of, remains, queries, early, cache_hbm, out, mark, late, scores, sums, sems
 ):
     blocks, tokens, width = cache_hbm.shape
     ready = early.shape[0]
@@ -170,6 +183,7 @@
     onehot = (iota((rows, requests), 1) == widen(owner_of[...], requests)).astype(BF16)
     picked = jnp.dot(onehot, queries[...], preferred_element_type=F32)
     picked = jnp.concatenate([picked, jnp.zeros((rows, width - WIDE), F32)], axis=1)
+    mark[...] = picked[:8, :128]
     lane = iota((rows, width), 1)
     spread = jnp.zeros((rows, width), F32)
     for h in range(heads):
@@ -245,21 +259,43 @@
     ).astype(BF16)
 
 
-def merge_kernel(shares, query, fresh, homed, weight, spread):
-    rows = query.shape[0]
-    count = shares.shape[0] // rows
-    heads = fresh.shape[1] // PAIR
-    sums = shares[...].astype(F32)
-    tail = sums[:, 256:]
-    joined = tail + pltpu.roll(tail, 128 - 16, 1) + pltpu.roll(tail, 128 - 32, 1)
-    totals = pltpu.roll(joined, 128 - 8, 1)
-    lane = iota(joined.shape, 1) - (STATS - 256)
-    peaks = jnp.where((lane >= 0) & (lane < heads) & (totals > 0.0), joined, VERY_LOW)
+def self_kernel(
+    mark,
+    query,
+    fresh,
+    token_hbm,
+    gain_hbm,
+    out_hbm,
+    up_hbm,
+    down_hbm,
+    scores,
+    values,
+    token,
+    gain,
+    out,
+    up,
+    down,
+    sems,
+):
+    copies = fetch(
+        [
+            (token_hbm, token),
+            (gain_hbm, gain.at[0]),
+            (out_hbm, out),
+            (up_hbm, up),
+            (down_hbm, down),
+        ],
+        sems,
+    )
+    rows, width = fresh.shape
+    heads = width // PAIR
     pair = fresh[...].astype(BF16).astype(F32)
     own = query[...].astype(F32)
     keys = jnp.concatenate([pair[:, PAIR * h : PAIR * h + HD] for h in range(heads)], axis=1)
-    values = jnp.concatenate(
-        [pair[:, PAIR * h + HD : PAIR * (h + 1)] for h in range(heads)], axis=1
+    values[...] = jnp.concatenate(
+        [pair[:, PAIR * h + HD : PAIR * (h + 1)] for h in range(heads)]
+        + [jnp.zeros((rows, WIDE - heads * HD), F32)],
+        axis=1,
     )
     product = own[:, : heads * HD] * keys
     head_of = iota((rows, heads * HD), 1) // HD
@@ -268,6 +304,22 @@
     for h in range(heads):
         score = jnp.sum(jnp.where(head_of == h, product, 0.0), axis=1, keepdims=True)
         self_score = jnp.where(own_lane == h, score, self_score)
+    scores[...] = self_score
+    for copy in copies:
+        copy.wait()
+
+
+def merge_kernel(shares, self_scores, values, homed, weight, spread):
+    rows = values.shape[0]
+    count = shares.shape[0] // rows
+    heads = weight.shape[0] // HD
+    sums = shares[...].astype(F32)
+    tail = sums[:, 256:]
+    joined = tail + pltpu.roll(tail, 128 - 16, 1) + pltpu.roll(tail, 128 - 32, 1)
+    totals = pltpu.roll(joined, 128 - 8, 1)
+    lane = iota(joined.shape, 1) - (STATS - 256)
+    peaks = jnp.where((lane >= 0) & (lane < heads) & (totals > 0.0), joined, VERY_LOW)
+    self_score = self_scores[...]
     top = self_score
     for s in range(count):
         top = jnp.maximum(top, peaks[s * rows : (s + 1) * rows])
@@ -282,8 +334,7 @@
             out = jnp.where(wide_of == h, value[:, at : at + 1], out)
         return out
 
-    values = jnp.concatenate([values, jnp.zeros((rows, WIDE - heads * HD), F32)], axis=1)
-    numerator = per_head(self_weight) * values
+    numerator = per_head(self_weight) * values[...]
     for s in range(count):
         at = slice(s * rows, (s + 1) * rows)
         factor = jnp.exp(peaks[at] - top)
@@ -309,9 +360,9 @@
     partial[...] = jnp.dot(active, down[...], preferred_element_type=F32).astype(BF16)
 
 
-def finish_kernel(served, residual, own, near, across, far, out):
-    own, near, across, far = (v[...].astype(F32) for v in (own, near, across, far))
-    result = residual[...] + ((own + near) + (across + far))
+def finish_kernel(served, residual, own, across, near, far, out):
+    own, across, near, far = (v[...].astype(F32) for v in (own, across, near, far))
+    result = residual[...] + ((own + across) + (near + far))
     out[...] = jnp.where(widen(served[...], result.shape[1]) > 0.0, result, 0.0)
 
 
@@ -319,12 +370,18 @@
     return jax.ShapeDtypeStruct(dims, dtype)
 
 
-def from_others(value, axis):
-    count = lax.axis_size(axis)
-    return [
-        lax.ppermute(value, axis, [(i, i ^ bits) for i in range(count)])
-        for bits in range(1, count)
-    ]
+def exchanged(value, partner):
+    axes = ("rep", "tp")
+    count = lax.axis_size("rep") * lax.axis_size("tp")
+    return lax.ppermute(value, axes, [(i, partner(i) % count) for i in range(count)])
+
+
+def from_others(value):
+    return (
+        exchanged(value, lambda i: i ^ 2),
+        exchanged(value, lambda i: i ^ 1),
+        exchanged(value, lambda i: i + 1 if i % 2 else i - 1),
+    )
 
 
 def body(
@@ -345,44 +402,47 @@
     rows, features = token_state.shape
     requests = home_replica.shape[0]
     _, blocks, tokens, width = kv_cache.shape
+    heads = width // PAIR
     place = jnp.stack([lax.axis_index("rep"), lax.axis_index("kv")]).astype(jnp.int32)
 
-    spread, query, fresh = pl.pallas_call(
-        project_kernel,
+    weight = qkv_weight.T
+    spread, query, normed = pl.pallas_call(
+        query_kernel,
         out_shape=(
             shape((requests, WIDE), BF16),
             shape((rows, WIDE), BF16),
-            shape((rows, width), F32),
+            shape((rows, features), BF16),
         ),
         in_specs=[HBM] * 3,
         out_specs=(VMEM,) * 3,
         scratch_shapes=[
             pltpu.VMEM((rows, features), BF16),
             pltpu.VMEM((1, features), F32),
-            pltpu.VMEM(qkv_weight.shape[::-1], BF16),
-            pltpu.SemaphoreType.DMA((3,)),
+            pltpu.VMEM((WIDE, features), BF16),
+            pltpu.SemaphoreType.DMA((2 + heads,)),
         ],
         compiler_params=PARAMS,
-        name="project",
-    )(*in_hbm(token_state, attn_gain, qkv_weight.T))
+        name="query",
+    )(*in_hbm(token_state, attn_gain, weight))
     queries = lax.all_to_all(spread, "kv", 0, 0, tiled=True)
 
     padded = -(-blocks // 16) * 16
-    early, owners, remains, entries, homed, served = pl.pallas_call(
+    early, owners, remains, fresh, entries, homed, served = pl.pallas_call(
         side_kernel,
         out_shape=(
             pltpu.VMEM((EARLY, tokens, width), BF16),
             shape((padded, 128), jnp.int32),
             shape((padded, 128), jnp.int32),
             shape((rows, width), F32),
+            shape((rows, width), F32),
             shape((rows, 128), F32),
             shape((rows, 128), F32),
         ),
-        in_specs=[SMEM] + [HBM] * 6 + [VMEM],
-        out_specs=(VMEM,) * 6,
+        in_specs=[SMEM] + [HBM] * 7 + [VMEM],
+        out_specs=(VMEM,) * 7,
         scratch_shapes=[pltpu.SMEM((1, blocks), jnp.int32)] * 2
         + [pltpu.SMEM((requests,), jnp.int32)] * 3
-        + [pltpu.SemaphoreType.DMA((6,))],
+        + [pltpu.VMEM((width, features), BF16), pltpu.SemaphoreType.DMA((6 + heads,))],
         compiler_params=PARAMS,
         cost_estimate=pl.CostEstimate(
             flops=0, bytes_accessed=2 * EARLY * tokens * width * 2, transcendentals=0
@@ -391,16 +451,16 @@
     )(
         place,
         *in_hbm(
-            block_owner, block_index, cache_length, home_replica, moving, kv_cache[0]
+            block_owner, block_index, cache_length, home_replica, moving, kv_cache[0], weight
         ),
-        fresh,
-    )
-
-    shares = pl.pallas_call(
+        normed,
+    )
+
+    shares, mark = pl.pallas_call(
         attend_kernel,
-        out_shape=shape((requests, WIDE), BF16),
+        out_shape=(shape((requests, WIDE), BF16), shape((8, 128), F32)),
         in_specs=[VMEM] * 4 + [HBM],
-        out_specs=VMEM,
+        out_specs=(VMEM,) * 2,
         scratch_shapes=[
             pltpu.VMEM((blocks - EARLY, tokens, width), BF16),
             pltpu.VMEM((blocks, 8, tokens), F32),
@@ -418,6 +478,25 @@
     )
     shares = lax.all_to_all(shares, "kv", 0, 0, tiled=True)
 
+    later = (out_weight, up_weight.T, down_weight)
+    held = [pltpu.VMEM((rows, features), BF16), pltpu.VMEM((1, features), F32)]
+    held += [pltpu.VMEM(w.shape, BF16) for w in later]
+    self_scores, values, *kept = pl.pallas_call(
+        self_kernel,
+        out_shape=(shape((rows, 128), F32), shape((rows, WIDE), F32), *held),
+        in_specs=[VMEM] * 3 + [HBM] * 5,
+        out_specs=(VMEM,) * 7,
+        scratch_shapes=[pltpu.SemaphoreType.DMA((5,))],
+        compiler_params=PARAMS,
+        cost_estimate=pl.CostEstimate(
+            flops=0, bytes_accessed=2 * sum(w.size for w in later) * 2, transcendentals=0
+        ),
+        name="self",
+    )(mark, query, fresh, *in_hbm(token_state, mlp_gain, *later))
+    token, gain, out_kept, up_kept, down_kept = (
+        pltpu.with_memory_space_constraint(k, pltpu.VMEM) for k in kept
+    )
+
     everyone = ("rep", "tp")
     count = lax.axis_size("rep") * lax.axis_size("tp")
     partials = pl.pallas_call(
@@ -427,7 +506,7 @@
         out_specs=VMEM,
         compiler_params=PARAMS,
         name="merge",
-    )(shares, query, fresh, homed, out_weight)
+    )(shares, self_scores, values, homed, out_kept)
     partials = lax.all_to_all(partials, everyone, 0, 0, tiled=True)
 
     residual, partial = pl.pallas_call(
@@ -437,7 +516,7 @@
         out_specs=(VMEM,) * 2,
         compiler_params=PARAMS,
         name="hidden",
-    )(token_state, partials, mlp_gain[None], up_weight.T, down_weight)
+    )(token, partials, gain, up_kept, down_kept)
     result = pl.pallas_call(
         finish_kernel,
         out_shape=shape((rows, features), F32),
@@ -445,7 +524,7 @@
         out_specs=VMEM,
         compiler_params=PARAMS,
         name="finish",
-    )(served, residual, partial, *from_others(partial, "tp"))
+    )(served, residual, partial, *from_others(partial))
     return (result[None], entries[None])
 
 

time: 65.3 us -> 62.5 us (0.957)
  blocking collectives: 12 us -> 18.7 us
  starting transfers between devices: 20.5 us -> 14.8 us
  waiting for transfers between devices: 16.3 us -> 11.9 us
  Pallas kernels: 14.5 us -> 15.7 us
    all_to_all x1, blocking collectives: 12 us -> 18.7 us  [body(): partials = lax.all_to_all(partials, everyone, 0, 0, tiled=True)]
    all_to_all x1, waiting for transfers between devices: 10.4 us -> 5.21 us  [body(): shares = lax.all_to_all(shares, 'kv', 0, 0, tiled=True)]
    all_to_all x1, starting transfers between devices: 8.47 us -> 5.09 us  [body(): shares = lax.all_to_all(shares, 'kv', 0, 0, tiled=True)]
    ppermute x3, starting transfers between devices: 4.4 us -> 2.04 us  [exchanged(): lax.ppermute(value, axes, [(i, partner(i) % count) for i in range(count)])]
    ppermute x3, waiting for transfers between devices: 1.76 us -> 3.3 us  [exchanged(): lax.ppermute(value, axes, [(i, partner(i) % count) for i in range(count)])]
    pallas_call x2 -> x3, Pallas kernels: 8.85 us -> 10.1 us  [the longest x1 5.93 us: body(): pl.pallas_call(attend_kernel, out_shape=(shape((requests, WIDE), BF16), s...]
    pallas_call x1, Pallas kernels: 2.75 us -> 3.49 us  [body(): pl.pallas_call(side_kernel, out_shape=(pltpu.VMEM((EARLY, tokens, width),...]
    all_to_all x1, waiting for transfers between devices: 4.15 us -> 3.41 us  [body(): queries = lax.all_to_all(spread, 'kv', 0, 0, tiled=True)]
  transfers between devices with their start and end apart: 5 -> 5, of which waited for: 4 -> 4; matrix products, arithmetic and copies ran while one was open for 0% -> 0% of each run, Pallas kernels for 4% -> 9%
where the time goes in v4:
time: 62.5 us; the launch traced here: 61.8 us
  blocking collectives  18.7 us (30%)
  Pallas kernels  15.7 us (25%)
  starting transfers between devices  14.8 us (24%)
  waiting for transfers between devices  11.9 us (19%)
  between operations  0.7 us (1%)
    all_to_all x1, blocking collectives, body(): partials = lax.all_to_all(partials, everyone, 0, 0, tiled=True)  18.7 us
    all_to_all x1, starting transfers between devices, body(): queries = lax.all_to_all(spread, 'kv', 0, 0, tiled=True)  7.63 us
    pallas_call x1, Pallas kernels, body(): pl.pallas_call(attend_kernel, out_shape=(shape((requests, WIDE), BF16), s...  5.93 us
    all_to_all x1, waiting for transfers between devices, body(): shares = lax.all_to_all(shares, 'kv', 0, 0, tiled=True)  5.21 us
    all_to_all x1, starting transfers between devices, body(): shares = lax.all_to_all(shares, 'kv', 0, 0, tiled=True)  5.09 us
    pallas_call x1, Pallas kernels, body(): pl.pallas_call(side_kernel, out_shape=(pltpu.VMEM((EARLY, tokens, width),...  3.49 us
    all_to_all x1, waiting for transfers between devices, body(): queries = lax.all_to_all(spread, 'kv', 0, 0, tiled=True)  3.41 us
    ppermute x3, waiting for transfers between devices, exchanged(): lax.ppermute(value, axes, [(i, partner(i) % count) for i in range(count)])  3.3 us
  transfers between devices with their start and end apart: 5, of which 4 were waited for; matrix products, arithmetic and copies ran while one was open for 0% of the time, Pallas kernels for 9%

profile of v4, /device:TPU:2, one launch (start us, length us, event | category | flops | bytes accessed | tf_op | source)
XLA Modules:
  0.0 61.8 jit_solution(11863476349728120391)
XLA Ops:
  0.6 2.4 %query.1 = (bf16[256,384]{1,0:T(8,128)(2,1)}, bf16[8,384]{1,0:T(8,128)(2,1)S(1)}, bf16[8,1280]{1,0:T(8,128)(2,1)S(1)}) custom-call(bf16[8,1280]{1,0:T(8,128)(2,1)} %token_hbm.3, f32[1280]{0:T(1024)} %gain_hbm.2, bf16[960,1280]{1,0:T(8,128)(2,1)} %bitcast.15), custom_call_target="tpu_custom_call" | custom-call | tf_op jit(solution)/shard_map/query/pallas_call | solution.py:409
  3.0 7.6 %all-to-all-start = ((bf16[32,8,384]{2,1,0:T(8,128)(2,1)}), bf16[32,8,384]{2,1,0:T(8,128)(2,1)S(1)}, u32[]{:S(2)}, u32[]{:S(2)}) async-start(bf16[32,8,384]{2,1,0:T(8,128)(2,1)} %bitcast.4), calls=%async_computation | async-start | bytes 393216 | tf_op jit(solution)/shard_map/all_to_all | solution.py:427
  10.7 0.1 pad_add_fusion.place
  10.7 3.5 %side.1 = (bf16[4,512,640]{2,1,0:T(8,128)(2,1)S(1)}, s32[16,128]{1,0:T(8,128)S(1)}, s32[16,128]{1,0:T(8,128)S(1)}, f32[8,640]{1,0:T(8,128)S(1)}, f32[8,640]{1,0:...) custom-call(s32[2]{0:T(128)S(1)} %pad_add_fusion.place, s32[1,11]{1,0:T(1,128)} %owner_hbm.1, s32[1,11]{1,0:T(1,128)} %index_hbm.1, ...), custom_call_target="tpu_custom_call" | custom-call | bytes 5242880 | tf_op jit(solution)/shard_map/side/pallas_call | solution.py:430
  14.2 3.4 %all-to-all-done = bf16[32,8,384]{2,1,0:T(8,128)(2,1)S(1)} async-done(((bf16[32,8,384]{2,1,0:T(8,128)(2,1)}), bf16[32,8,384]{2,1,0:T(8,128)(2,1)S(1)}, u32[]{:S(2)}, u32[]{:S(2)}) %all-to-all-start) | async-done | bytes 196640 | tf_op jit(solution)/shard_map/all_to_all | solution.py:427
  17.7 5.9 %attend.1 = (bf16[256,384]{1,0:T(8,128)(2,1)}, f32[8,128]{1,0:T(8,128)S(1)}) custom-call(s32[16,128]{1,0:T(8,128)S(1)} %get-tuple-element.25.owner_of, s32[16,128]{1,0:T(8,128)S(1)} %get-tuple-element.26.remains, bf16[256,384]{1,0:T(8,128)(2,1)S(1)} %bitcast.12, bf16[4,512,640]{2,1,0:T(8,128)(2,1)S(1)} %get-tuple-element.28.early, bf16[11,512,640]{2,1,0:T(8,128)(2,1)} %bitcast.14), custom_call_target="tpu_custom_call" | custom-call | tf_op jit(solution)/shard_map/attend/pallas_call | solution.py:459
  23.6 5.1 %all-to-all-start.1 = ((bf16[32,8,384]{2,1,0:T(8,128)(2,1)}), bf16[32,8,384]{2,1,0:T(8,128)(2,1)S(1)}, u32[]{:S(2)}, u32[]{:S(2)}) async-start(bf16[32,8,384]{2,1,0:T(8,128)(2,1)} %bitcast.7), calls=%async_computation.1 | async-start | bytes 393216 | tf_op jit(solution)/shard_map/all_to_all | solution.py:479
  28.7 1.8 %self.1 = (f32[8,128]{1,0:T(8,128)S(1)}, f32[8,384]{1,0:T(8,128)S(1)}, bf16[8,1280]{1,0:T(8,128)(2,1)S(1)}, f32[1,1280]{1,0:T(1,128)S(1)}, bf16[320,1280]{1,0:T(...) custom-call(f32[8,128]{1,0:T(8,128)S(1)} %get-tuple-element.29.mark, ...), custom_call_target="tpu_custom_call" | custom-call | bytes 4915200 | tf_op jit(solution)/shard_map/self/pallas_call | solution.py:484
  30.5 5.2 %all-to-all-done.1 = bf16[32,8,384]{2,1,0:T(8,128)(2,1)S(1)} async-done(((bf16[32,8,384]{2,1,0:T(8,128)(2,1)}), bf16[32,8,384]{2,1,0:T(8,128)(2,1)S(1)}, u32[]{:S(2)}, u32[]{:S(2)}) %all-to-all-start.1) | async-done | bytes 196640 | tf_op jit(solution)/shard_map/all_to_all | solution.py:479
  35.7 0.7 %merge.1 = bf16[8,8,1280]{2,1,0:T(8,128)(2,1)S(1)} custom-call(bf16[256,384]{1,0:T(8,128)(2,1)S(1)} %bitcast.11, f32[8,128]{1,0:T(8,128)S(1)} %get-tuple-element.34.self_scores, f32[8,384]{1,0:T(8,128)S(1)} %get-tuple-element.35.values, f32[8,128]{1,0:T(8,128)S(1)} %get-tuple-element.36.homed, bf16[320,1280]{1,0:T(8,128)(2,1)S(1)} %get-tuple-element.37.weight), custom_call_target="tpu_custom_call" | custom-call | tf_op jit(solution)/shard_map/merge/pallas_call | solution.py:502
  36.4 18.7 %all_to_all.27.shares = bf16[8,8,1280]{2,1,0:T(8,128)(2,1)S(1)} all-to-all(bf16[8,8,1280]{2,1,0:T(8,128)(2,1)S(1)} %merge.1), channel_id=1, replica_groups=mesh['rep'=2,'kv'=32,'tp'=4] {'rep','tp'}, dimensions={0} | all-to-all | bytes 327680 | tf_op jit(solution)/shard_map/all_to_all | solution.py:510
  55.1 0.8 %hidden.1 = (f32[8,1280]{1,0:T(8,128)S(1)}, bf16[8,1280]{1,0:T(8,128)(2,1)S(1)}) custom-call(bf16[8,1280]{1,0:T(8,128)(2,1)S(1)} %get-tuple-element.32.token, bf16[8,8,1280]{2,1,0:T(8,128)(2,1)S(1)} %all_to_all.27.shares, f32[1,1280]{1,0:T(1,128)S(1)} %get-tuple-element.38.gain, bf16[320,1280]{1,0:T(8,128)(2,1)S(1)} %get-tuple-element.39.up, ...), custom_call_target="tpu_custom_call" | custom-call | tf_op jit(solution)/shard_map/hidden/pallas_call | solution.py:512
  55.9 0.0 collective-permute-start.2
  55.9 0.7 %collective-permute-start.1 = (bf16[8,1280]{1,0:T(8,128)(2,1)S(1)}, bf16[8,1280]{1,0:T(8,128)(2,1)S(1)}, u32[]{:S(2)}, u32[]{:S(2)}) collective-permute-start(bf16[8,1280]{1,0:T(8,128)(2,1)S(1)} %get-tuple-element.42.own), channel_id=1, source_target_pairs={{0,1},{1,0},{2,3},{3,2},{128,129},{129,128},{130,131},{131,130},{4... | collective-permute-start | bytes 61448 | tf_op jit(solution)/shard_map/ppermute | solution.py:376
  56.5 1.4 %collective-permute-start = (bf16[8,1280]{1,0:T(8,128)(2,1)S(1)}, bf16[8,1280]{1,0:T(8,128)(2,1)S(1)}, u32[]{:S(2)}, u32[]{:S(2)}) collective-permute-start(bf16[8,1280]{1,0:T(8,128)(2,1)S(1)} %get-tuple-element.42.own), channel_id=1, source_target_pairs={{0,2},{1,3},{2,0},{3,1},{128,130},{129,131},{130,128},{131,129},{4... | collective-permute-start | bytes 61448 | tf_op jit(solution)/shard_map/ppermute | solution.py:376
  57.9 3.0 %collective-permute-done.2.far = bf16[8,1280]{1,0:T(8,128)(2,1)S(1)} collective-permute-done((bf16[8,1280]{1,0:T(8,128)(2,1)S(1)}, bf16[8,1280]{1,0:T(8,128)(2,1)S(1)}, u32[]{:S(2)}, u32[]{:S(2)}) %collective-permute-start.2) | collective-permute-done | bytes 20512 | tf_op jit(solution)/shard_map/ppermute | solution.py:376
  60.9 0.0 collective-permute-done.1.near
  60.9 0.3 collective-permute-done.across
  61.2 0.6 %finish.1 = f32[8,1280]{1,0:T(8,128)} custom-call(f32[8,128]{1,0:T(8,128)S(1)} %get-tuple-element.24.served, f32[8,1280]{1,0:T(8,128)S(1)} %get-tuple-element.41.residual, bf16[8,1280]{1,0:T(8,128)(2,1)S(1)} %get-tuple-element.42.own, bf16[8,1280]{1,0:T(8,128)(2,1)S(1)} %collective-permute-done.across, bf16[8,1280]{1,0:T(8,128)(2,1)S(1)} %collective-permute-done.1.near, ...), custom_call_target="tpu_custom_call" | custom-call | tf_op jit(solution)/shard_map/finish/pallas_call | solution.py:520
Async XLA Ops:
  3.0 14.6 %all-to-all-start = ((bf16[32,8,384]{2,1,0:T(8,128)(2,1)}), bf16[32,8,384]{2,1,0:T(8,128)(2,1)S(1)}, u32[]{:S(2)}, u32[]{:S(2)}) async-start(bf16[32,8,384]{2,1,0:T(8,128)(2,1)} %bitcast.4), calls=%async_computation | async-start | bytes 393216 | tf_op jit(solution)/shard_map/all_to_all | solution.py:427
  23.6 12.1 %all-to-all-start.1 = ((bf16[32,8,384]{2,1,0:T(8,128)(2,1)}), bf16[32,8,384]{2,1,0:T(8,128)(2,1)S(1)}, u32[]{:S(2)}, u32[]{:S(2)}) async-start(bf16[32,8,384]{2,1,0:T(8,128)(2,1)} %bitcast.7), calls=%async_computation.1 | async-start | bytes 393216 | tf_op jit(solution)/shard_map/all_to_all | solution.py:479
  55.9 5.0 %collective-permute-start.2 = (bf16[8,1280]{1,0:T(8,128)(2,1)S(1)}, bf16[8,1280]{1,0:T(8,128)(2,1)S(1)}, u32[]{:S(2)}, u32[]{:S(2)}) collective-permute-start(bf16[8,1280]{1,0:T(8,128)(2,1)S(1)} %get-tuple-element.42.own), channel_id=1, source_target_pairs={{0,131},{1,2},{2,1},{3,128},{128,3},{129,130},{130,129},{131,0},{4... | collective-permute-start | bytes 61448 | tf_op jit(solution)/shard_map/ppermute | solution.py:376
  55.9 5.0 %collective-permute-start.1 = (bf16[8,1280]{1,0:T(8,128)(2,1)S(1)}, bf16[8,1280]{1,0:T(8,128)(2,1)S(1)}, u32[]{:S(2)}, u32[]{:S(2)}) collective-permute-start(bf16[8,1280]{1,0:T(8,128)(2,1)S(1)} %get-tuple-element.42.own), channel_id=1, source_target_pairs={{0,1},{1,0},{2,3},{3,2},{128,129},{129,128},{130,131},{131,130},{4... | collective-permute-start | bytes 61448 | tf_op jit(solution)/shard_map/ppermute | solution.py:376
  56.5 4.7 %collective-permute-start = (bf16[8,1280]{1,0:T(8,128)(2,1)S(1)}, bf16[8,1280]{1,0:T(8,128)(2,1)S(1)}, u32[]{:S(2)}, u32[]{:S(2)}) collective-permute-start(bf16[8,1280]{1,0:T(8,128)(2,1)S(1)} %get-tuple-element.42.own), channel_id=1, source_target_pairs={{0,2},{1,3},{2,0},{3,1},{128,130},{129,131},{130,128},{131,129},{4... | collective-permute-start | bytes 61448 | tf_op jit(solution)/shard_map/ppermute | solution.py:376

commit v5 on v4

--- a/solution.py
+++ b/solution.py
@@ -11,7 +11,8 @@
 PAIR = 2 * HD
 VERY_LOW = -1e30
 NORM_EPS = 1e-06
-EARLY = 4
+EARLY = 3
+LATE_GROUP = 2
 STATS = 320
 WIDE = 384
 F32 = jnp.float32
@@ -101,14 +102,18 @@
     moving_hbm,
     cache_hbm,
     weight_hbm,
+    gain_hbm,
     normed,
+    query,
     cache,
     owners,
     remains,
-    fresh,
     entries,
     homed,
     served,
+    self_scores,
+    values,
+    gain,
     owner,
     index,
     length,
@@ -136,7 +141,7 @@
             )
             for h in range(heads)
         ]
-        + [(cache_hbm.at[: cache.shape[0]], cache)],
+        + [(gain_hbm, gain.at[0]), (cache_hbm.at[: cache.shape[0]], cache)],
         sems,
     )
     for copy in copies[:5]:
@@ -160,13 +165,27 @@
     for copy in copies[5:-1]:
         copy.wait()
     pairs = dot_transposed(normed[...], weight[...])
-    fresh[...] = pairs
     entries[...] = jnp.where(widen(serves, pairs.shape[1]) > 0.0, pairs, 0.0)
+    pair = pairs.astype(BF16).astype(F32)
+    keys = jnp.concatenate([pair[:, PAIR * h : PAIR * h + HD] for h in range(heads)], axis=1)
+    values[...] = jnp.concatenate(
+        [pair[:, PAIR * h + HD : PAIR * (h + 1)] for h in range(heads)]
+        + [jnp.zeros((rows, WIDE - heads * HD), F32)],
+        axis=1,
+    )
+    product = query[...].astype(F32)[:, : heads * HD] * keys
+    head_of = iota((rows, heads * HD), 1) // HD
+    own_lane = iota((rows, 128), 1) - (STATS - 256)
+    self_score = jnp.full((rows, 128), VERY_LOW, F32)
+    for h in range(heads):
+        score = jnp.sum(jnp.where(head_of == h, product, 0.0), axis=1, keepdims=True)
+        self_score = jnp.where(own_lane == h, score, self_score)
+    self_scores[...] = self_score
     copies[-1].wait()
 
 
 def attend_kernel(
-    owner_of, remains, queries, early, cache_hbm, out, mark, late, scores, sums, sems
+    owner_of, remains, queries, early, cache_hbm, out, late, parts, sums, sems
 ):
     blocks, tokens, width = cache_hbm.shape
     ready = early.shape[0]
@@ -183,7 +202,6 @@
     onehot = (iota((rows, requests), 1) == widen(owner_of[...], requests)).astype(BF16)
     picked = jnp.dot(onehot, queries[...], preferred_element_type=F32)
     picked = jnp.concatenate([picked, jnp.zeros((rows, width - WIDE), F32)], axis=1)
-    mark[...] = picked[:8, :128]
     lane = iota((rows, width), 1)
     spread = jnp.zeros((rows, width), F32)
     for h in range(heads):
@@ -196,18 +214,38 @@
     token_lane = iota((8, tokens), 1)
     every_peak = jnp.full((8, 128), VERY_LOW, F32)
     holders = jnp.full((8, 128), requests, jnp.int32)
-    usable = []
+    scores = [None] * blocks
+    uses = [None] * blocks
+    peaks = [None] * blocks
+    totals = [None] * blocks
+
+    def weigh(group):
+        for b in group:
+            peaks[b] = jnp.max(scores[b], axis=1, keepdims=True)
+        for b in group:
+            weights = jnp.where(uses[b], jnp.exp(scores[b] - peaks[b]), 0.0)
+            totals[b] = jnp.sum(weights, axis=1, keepdims=True)
+            acc = jnp.dot(weights.astype(BF16), cache(b), preferred_element_type=F32)
+            parts[b] = jnp.where(value_lanes, acc, 0.0)
+
+    before = ()
+    starts = [0] + list(range(ready, blocks, LATE_GROUP)) + [blocks]
+    for g in range(len(starts) - 1):
+        group = range(starts[g], starts[g + 1])
+        for b in group:
+            if b >= ready:
+                copies[b - ready].wait()
+        for b in group:
+            ask = jnp.where(key_lanes, jnp.broadcast_to(spread[b : b + 1], (8, width)), 0.0)
+            score = dot_transposed(ask.astype(BF16), cache(b))
+            left = widen(jnp.broadcast_to(remains[b : b + 1, :], (8, 128)), tokens)
+            uses[b] = token_lane < left
+            scores[b] = jnp.where(uses[b], score, VERY_LOW)
+        weigh(before)
+        before = group
+    weigh(before)
     for b in range(blocks):
-        ask = jnp.where(key_lanes, jnp.broadcast_to(spread[b : b + 1], (8, width)), 0.0)
-        if b >= ready:
-            copies[b - ready].wait()
-        score = dot_transposed(ask.astype(BF16), cache(b))
-        use = token_lane < widen(jnp.broadcast_to(remains[b : b + 1, :], (8, 128)), tokens)
-        score = jnp.where(use, score, VERY_LOW)
-        scores[b] = score
-        usable.append(use)
-        peak = jnp.max(score, axis=1, keepdims=True)
-        every_peak = jnp.where(block_lane == b, peak, every_peak)
+        every_peak = jnp.where(block_lane == b, peaks[b], every_peak)
         holders = jnp.where(block_lane == b, owner_of[b : b + 1, :], holders)
     stat_lane = iota((8, 128), 1) - (STATS - 256)
     stat_row = iota((8, 128), 0)
@@ -215,12 +253,10 @@
     for b in range(blocks):
         peers = jnp.where(holders == owner_of[b : b + 1, :], every_peak, VERY_LOW)
         joint = jnp.max(peers, axis=1, keepdims=True)
-        weights = jnp.where(usable[b], jnp.exp(scores[b] - joint), 0.0)
-        total = jnp.sum(weights, axis=1, keepdims=True)
-        acc = jnp.dot(weights.astype(BF16), cache(b), preferred_element_type=F32)
-        sums[b : b + 1, :] = jnp.sum(jnp.where(value_lanes, acc, 0.0), axis=0, keepdims=True)
+        factor = jnp.exp(peaks[b] - joint)
+        sums[b : b + 1, :] = jnp.sum(parts[b] * factor, axis=0, keepdims=True)
         stat = jnp.where(stat_lane == stat_row, joint, 0.0)
-        stat = stat + jnp.where(stat_lane == stat_row + 8, total, 0.0)
+        stat = stat + jnp.where(stat_lane == stat_row + 8, totals[b] * factor, 0.0)
         stats.append(jnp.sum(jnp.where(stat_row < heads, stat, 0.0), axis=0, keepdims=True))
     stats += [jnp.zeros((1, 128), F32)] * (rows - blocks)
     stats = jnp.concatenate(stats, axis=0)
@@ -232,22 +268,20 @@
         packed = jnp.where((lane >= HD * h) & (lane < HD * (h + 1)), moved, packed)
     packed = packed[:, :WIDE]
     added = jnp.zeros((rows, WIDE), F32)
-    totals = jnp.zeros((rows, 128), F32)
+    added_totals = jnp.zeros((rows, 128), F32)
     first = iota((rows, 128), 0) < blocks
     for b in range(blocks):
         same = owner_of[...] == owner_of[b : b + 1, :]
         added = added + jnp.where(widen(same, WIDE), packed[b : b + 1], 0.0)
-        totals = totals + jnp.where(same, stats[b : b + 1], 0.0)
+        added_totals = added_totals + jnp.where(same, stats[b : b + 1], 0.0)
         first = first & ((iota((rows, 128), 0) <= b) | ~same)
     tail = iota((rows, 128), 1) - (STATS - 256)
     peak_part = jnp.where((tail >= 0) & (tail < 8), stats, 0.0)
-    total_part = jnp.where((tail >= 8) & (tail < 16), totals, 0.0)
-    parts = jnp.zeros((rows, 128), F32)
-    for k, part in enumerate(split3(peak_part)):
-        parts = parts + (part if k == 0 else pltpu.roll(part, 16 * k, 1))
-    for k, part in enumerate(split3(total_part)):
-        parts = parts + (part if k == 0 else pltpu.roll(part, 16 * k, 1))
-    last = jnp.where(tail >= 0, parts, added[:, 256:])
+    total_part = jnp.where((tail >= 8) & (tail < 16), added_totals, 0.0)
+    terms = jnp.zeros((rows, 128), F32)
+    for k, term in enumerate(split3(peak_part + total_part)):
+        terms = terms + (term if k == 0 else pltpu.roll(term, 16 * k, 1))
+    last = jnp.where(tail >= 0, terms, added[:, 256:])
     full = jnp.concatenate([added[:, :256], last], axis=1)
     keep = jnp.where(first, 1.0, 0.0)
     full = jnp.where(widen(keep, WIDE) > 0.0, full, 0.0).astype(BF16)
@@ -257,56 +291,6 @@
         (((0,), (0,)), ((), ())),
         preferred_element_type=F32,
     ).astype(BF16)
-
-
-def self_kernel(
-    mark,
-    query,
-    fresh,
-    token_hbm,
-    gain_hbm,
-    out_hbm,
-    up_hbm,
-    down_hbm,
-    scores,
-    values,
-    token,
-    gain,
-    out,
-    up,
-    down,
-    sems,
-):
-    copies = fetch(
-        [
-            (token_hbm, token),
-            (gain_hbm, gain.at[0]),
-            (out_hbm, out),
-            (up_hbm, up),
-            (down_hbm, down),
-        ],
-        sems,
-    )
-    rows, width = fresh.shape
-    heads = width // PAIR
-    pair = fresh[...].astype(BF16).astype(F32)
-    own = query[...].astype(F32)
-    keys = jnp.concatenate([pair[:, PAIR * h : PAIR * h + HD] for h in range(heads)], axis=1)
-    values[...] = jnp.concatenate(
-        [pair[:, PAIR * h + HD : PAIR * (h + 1)] for h in range(heads)]
-        + [jnp.zeros((rows, WIDE - heads * HD), F32)],
-        axis=1,
-    )
-    product = own[:, : heads * HD] * keys
-    head_of = iota((rows, heads * HD), 1) // HD
-    own_lane = iota((rows, 128), 1) - (STATS - 256)
-    self_score = jnp.full((rows, 128), VERY_LOW, F32)
-    for h in range(heads):
-        score = jnp.sum(jnp.where(head_of == h, product, 0.0), axis=1, keepdims=True)
-        self_score = jnp.where(own_lane == h, score, self_score)
-    scores[...] = self_score
-    for copy in copies:
-        copy.wait()
 
 
 def merge_kernel(shares, self_scores, values, homed, weight, spread):
@@ -360,8 +344,8 @@
     partial[...] = jnp.dot(active, down[...], preferred_element_type=F32).astype(BF16)
 
 
-def finish_kernel(served, residual, own, across, near, far, out):
-    own, across, near, far = (v[...].astype(F32) for v in (own, across, near, far))
+def finish_kernel(served, residual, own, far, near, across, out):
+    own, far, near, across = (v[...].astype(F32) for v in (own, far, near, across))
     result = residual[...] + ((own + across) + (near + far))
     out[...] = jnp.where(widen(served[...], result.shape[1]) > 0.0, result, 0.0)
 
@@ -377,11 +361,10 @@
 
 
 def from_others(value):
-    return (
-        exchanged(value, lambda i: i ^ 2),
-        exchanged(value, lambda i: i ^ 1),
-        exchanged(value, lambda i: i + 1 if i % 2 else i - 1),
-    )
+    far = exchanged(value, lambda i: i + 1 if i % 2 else i - 1)
+    near = exchanged(value, lambda i: i ^ 1)
+    across = exchanged(value, lambda i: i ^ 2)
+    return far, near, across
 
 
 def body(
@@ -427,22 +410,24 @@
     queries = lax.all_to_all(spread, "kv", 0, 0, tiled=True)
 
     padded = -(-blocks // 16) * 16
-    early, owners, remains, fresh, entries, homed, served = pl.pallas_call(
+    early, owners, remains, entries, homed, served, self_scores, values, gain = pl.pallas_call(
         side_kernel,
         out_shape=(
             pltpu.VMEM((EARLY, tokens, width), BF16),
             shape((padded, 128), jnp.int32),
             shape((padded, 128), jnp.int32),
             shape((rows, width), F32),
-            shape((rows, width), F32),
             shape((rows, 128), F32),
             shape((rows, 128), F32),
+            shape((rows, 128), F32),
+            shape((rows, WIDE), F32),
+            shape((1, features), F32),
         ),
-        in_specs=[SMEM] + [HBM] * 7 + [VMEM],
-        out_specs=(VMEM,) * 7,
+        in_specs=[SMEM] + [HBM] * 8 + [VMEM] * 2,
+        out_specs=(VMEM,) * 9,
         scratch_shapes=[pltpu.SMEM((1, blocks), jnp.int32)] * 2
         + [pltpu.SMEM((requests,), jnp.int32)] * 3
-        + [pltpu.VMEM((width, features), BF16), pltpu.SemaphoreType.DMA((6 + heads,))],
+        + [pltpu.VMEM((width, features), BF16), pltpu.SemaphoreType.DMA((7 + heads,))],
         compiler_params=PARAMS,
         cost_estimate=pl.CostEstimate(
             flops=0, bytes_accessed=2 * EARLY * tokens * width * 2, transcendentals=0
@@ -451,19 +436,27 @@
     )(
         place,
         *in_hbm(
-            block_owner, block_index, cache_length, home_replica, moving, kv_cache[0], weight
+            block_owner,
+            block_index,
+            cache_length,
+            home_replica,
+            moving,
+            kv_cache[0],
+            weight,
+            mlp_gain,
         ),
         normed,
-    )
-
-    shares, mark = pl.pallas_call(
+        query,
+    )
+
+    shares = pl.pallas_call(
         attend_kernel,
-        out_shape=(shape((requests, WIDE), BF16), shape((8, 128), F32)),
+        out_shape=shape((requests, WIDE), BF16),
         in_specs=[VMEM] * 4 + [HBM],
-        out_specs=(VMEM,) * 2,
+        out_specs=VMEM,
         scratch_shapes=[
             pltpu.VMEM((blocks - EARLY, tokens, width), BF16),
-            pltpu.VMEM((blocks, 8, tokens), F32),
+            pltpu.VMEM((blocks, 8, width), F32),
             pltpu.VMEM((padded, width), F32),
             pltpu.SemaphoreType.DMA((blocks - EARLY,)),
         ],
@@ -478,25 +471,6 @@
     )
     shares = lax.all_to_all(shares, "kv", 0, 0, tiled=True)
 
-    later = (out_weight, up_weight.T, down_weight)
-    held = [pltpu.VMEM((rows, features), BF16), pltpu.VMEM((1, features), F32)]
-    held += [pltpu.VMEM(w.shape, BF16) for w in later]
-    self_scores, values, *kept = pl.pallas_call(
-        self_kernel,
-        out_shape=(shape((rows, 128), F32), shape((rows, WIDE), F32), *held),
-        in_specs=[VMEM] * 3 + [HBM] * 5,
-        out_specs=(VMEM,) * 7,
-        scratch_shapes=[pltpu.SemaphoreType.DMA((5,))],
-        compiler_params=PARAMS,
-        cost_estimate=pl.CostEstimate(
-            flops=0, bytes_accessed=2 * sum(w.size for w in later) * 2, transcendentals=0
-        ),
-        name="self",
-    )(mark, query, fresh, *in_hbm(token_state, mlp_gain, *later))
-    token, gain, out_kept, up_kept, down_kept = (
-        pltpu.with_memory_space_constraint(k, pltpu.VMEM) for k in kept
-    )
-
     everyone = ("rep", "tp")
     count = lax.axis_size("rep") * lax.axis_size("tp")
     partials = pl.pallas_call(
@@ -506,7 +480,7 @@
         out_specs=VMEM,
         compiler_params=PARAMS,
         name="merge",
-    )(shares, self_scores, values, homed, out_kept)
+    )(shares, self_scores, values, homed, out_weight)
     partials = lax.all_to_all(partials, everyone, 0, 0, tiled=True)
 
     residual, partial = pl.pallas_call(
@@ -516,7 +490,7 @@
         out_specs=(VMEM,) * 2,
         compiler_params=PARAMS,
         name="hidden",
-    )(token, partials, gain, up_kept, down_kept)
+    )(token_state, partials, gain, up_weight.T, down_weight)
     result = pl.pallas_call(
         finish_kernel,
         out_shape=shape((rows, features), F32),

time: 62.5 us -> 61.4 us (0.982)
  blocking collectives: 18.7 us -> 30.7 us
  starting transfers between devices: 14.8 us -> 9.34 us
  waiting for transfers between devices: 11.9 us -> 7.91 us
  Pallas kernels: 15.7 us -> 12.4 us
    all_to_all x0 -> x1, blocking collectives: none -> 12 us  [body(): shares = lax.all_to_all(shares, 'kv', 0, 0, tiled=True)]
    all_to_all x1 -> x0, waiting for transfers between devices: 5.21 us -> none  [body(): shares = lax.all_to_all(shares, 'kv', 0, 0, tiled=True)]
    all_to_all x1 -> x0, starting transfers between devices: 5.09 us -> none  [body(): shares = lax.all_to_all(shares, 'kv', 0, 0, tiled=True)]
    pallas_call x2 -> x1, Pallas kernels: 7.71 us -> 4.51 us  [body(): pl.pallas_call(attend_kernel, out_shape=shape((requests, WIDE), BF16), in...]
    ppermute x3, waiting for transfers between devices: 3.3 us -> 4.36 us  [exchanged(): lax.ppermute(value, axes, [(i, partner(i) % count) for i in range(count)])]
  transfers between devices with their start and end apart: 5 -> 4, of which waited for: 4 -> 3; matrix products, arithmetic and copies ran while one was open for 0% -> 0% of each run, Pallas kernels for 9% -> 5%
where the time goes in v5:
time: 61.4 us; the launch traced here: 61.1 us
  blocking collectives  30.7 us (50%)
  Pallas kernels  12.4 us (20%)
  starting transfers between devices  9.34 us (15%)
  waiting for transfers between devices  7.91 us (13%)
  between operations  0.69 us (1%)
    all_to_all x1, blocking collectives, body(): partials = lax.all_to_all(partials, everyone, 0, 0, tiled=True)  18.7 us
    all_to_all x1, blocking collectives, body(): shares = lax.all_to_all(shares, 'kv', 0, 0, tiled=True)  12 us
    all_to_all x1, starting transfers between devices, body(): queries = lax.all_to_all(spread, 'kv', 0, 0, tiled=True)  7.63 us
    pallas_call x1, Pallas kernels, body(): pl.pallas_call(attend_kernel, out_shape=shape((requests, WIDE), BF16), in...  4.51 us
    ppermute x3, waiting for transfers between devices, exchanged(): lax.ppermute(value, axes, [(i, partner(i) % count) for i in range(count)])  4.36 us
    all_to_all x1, waiting for transfers between devices, body(): queries = lax.all_to_all(spread, 'kv', 0, 0, tiled=True)  3.54 us
    pallas_call x1, Pallas kernels, body(): pl.pallas_call(side_kernel, out_shape=(pltpu.VMEM((EARLY, tokens, width),...  3.36 us
    pallas_call x1, Pallas kernels, body(): pl.pallas_call(query_kernel, out_shape=(shape((requests, WIDE), BF16), sh...  2.39 us
  transfers between devices with their start and end apart: 4, of which 3 were waited for; matrix products, arithmetic and copies ran while one was open for 0% of the time, Pallas kernels for 5%

profile of v5, /device:TPU:2, one launch (start us, length us, event | category | flops | bytes accessed | tf_op | source)
XLA Modules:
  0.0 61.1 jit_solution(8781385241527430459)
XLA Ops:
  0.6 2.4 %query.1 = (bf16[256,384]{1,0:T(8,128)(2,1)}, bf16[8,384]{1,0:T(8,128)(2,1)S(1)}, bf16[8,1280]{1,0:T(8,128)(2,1)S(1)}) custom-call(bf16[8,1280]{1,0:T(8,128)(2,1)} %token_.1, f32[1280]{0:T(1024)} %gain_hbm.2, bf16[960,1280]{1,0:T(8,128)(2,1)} %bitcast.17), custom_call_target="tpu_custom_call" | custom-call | tf_op jit(solution)/shard_map/query/pallas_call | solution.py:392
  3.0 7.6 %all-to-all-start = ((bf16[32,8,384]{2,1,0:T(8,128)(2,1)}), bf16[32,8,384]{2,1,0:T(8,128)(2,1)S(1)}, u32[]{:S(2)}, u32[]{:S(2)}) async-start(bf16[32,8,384]{2,1,0:T(8,128)(2,1)} %bitcast.4), calls=%async_computation | async-start | bytes 393216 | tf_op jit(solution)/shard_map/all_to_all | solution.py:410
  10.7 0.1 pad_add_fusion.place
  10.7 3.4 %side.1 = (bf16[3,512,640]{2,1,0:T(8,128)(2,1)S(1)}, s32[16,128]{1,0:T(8,128)S(1)}, s32[16,128]{1,0:T(8,128)S(1)}, f32[8,640]{1,0:T(8,128)}, f32[8,128]{1,0:T(8,...) custom-call(s32[2]{0:T(128)S(1)} %pad_add_fusion.place, ...), custom_call_target="tpu_custom_call" | custom-call | bytes 3932160 | tf_op jit(solution)/shard_map/side/pallas_call | solution.py:413
  14.1 3.5 %all-to-all-done = bf16[32,8,384]{2,1,0:T(8,128)(2,1)S(1)} async-done(((bf16[32,8,384]{2,1,0:T(8,128)(2,1)}), bf16[32,8,384]{2,1,0:T(8,128)(2,1)S(1)}, u32[]{:S(2)}, u32[]{:S(2)}) %all-to-all-start) | async-done | bytes 196640 | tf_op jit(solution)/shard_map/all_to_all | solution.py:410
  17.7 0.0 copy-start
  17.7 0.0 copy-start.3
  17.7 4.5 %attend.1 = bf16[256,384]{1,0:T(8,128)(2,1)S(1)} custom-call(s32[16,128]{1,0:T(8,128)S(1)} %get-tuple-element.19.owner_of, s32[16,128]{1,0:T(8,128)S(1)} %get-tuple-element.20.remains, bf16[256,384]{1,0:T(8,128)(2,1)S(1)} %bitcast.13, bf16[3,512,640]{2,1,0:T(8,128)(2,1)S(1)} %get-tuple-element.22.early, bf16[11,512,640]{2,1,0:T(8,128)(2,1)} %bitcast.16), custom_call_target="tpu_custom_call" | custom-call | tf_op jit(solution)/shard_map/attend/pallas_call | solution.py:452
  22.2 0.0 copy-start.1
  22.2 0.0 copy-start.2
  22.2 12.0 %all_to_all.27 = bf16[32,8,384]{2,1,0:T(8,128)(2,1)S(1)} all-to-all(bf16[32,8,384]{2,1,0:T(8,128)(2,1)S(1)} %bitcast.14), channel_id=1, replica_groups=mesh['rep'=2,'kv'=32,'tp'=4] {'kv'}, dimensions={0} | all-to-all | bytes 393216 | tf_op jit(solution)/shard_map/all_to_all | solution.py:472
  34.2 0.0 copy-done
  34.2 0.7 %merge.1 = bf16[8,8,1280]{2,1,0:T(8,128)(2,1)S(1)} custom-call(bf16[256,384]{1,0:T(8,128)(2,1)S(1)} %bitcast.12, f32[8,128]{1,0:T(8,128)S(1)} %get-tuple-element.23.self_scores, f32[8,384]{1,0:T(8,128)S(1)} %get-tuple-element.24.values, f32[8,128]{1,0:T(8,128)S(1)} %get-tuple-element.25.homed, bf16[320,1280]{1,0:T(8,128)(2,1)S(1)} %copy-done), custom_call_target="tpu_custom_call" | custom-call | tf_op jit(solution)/shard_map/merge/pallas_call | solution.py:476
  34.9 18.7 %all_to_all.28.shares = bf16[8,8,1280]{2,1,0:T(8,128)(2,1)S(1)} all-to-all(bf16[8,8,1280]{2,1,0:T(8,128)(2,1)S(1)} %merge.1), channel_id=1, replica_groups=mesh['rep'=2,'kv'=32,'tp'=4] {'rep','tp'}, dimensions={0} | all-to-all | bytes 327680 | tf_op jit(solution)/shard_map/all_to_all | solution.py:484
  53.6 0.0 copy-done.3
  53.6 0.0 copy-done.1
  53.6 0.0 copy-done.2
  53.6 0.8 %hidden.1 = (f32[8,1280]{1,0:T(8,128)S(1)}, bf16[8,1280]{1,0:T(8,128)(2,1)S(1)}) custom-call(bf16[8,1280]{1,0:T(8,128)(2,1)S(1)} %copy-done.3, bf16[8,8,1280]{2,1,0:T(8,128)(2,1)S(1)} %all_to_all.28.shares, f32[1,1280]{1,0:T(1,128)S(1)} %get-tuple-element.26.gain, bf16[320,1280]{1,0:T(8,128)(2,1)S(1)} %bitcast.11, bf16[320,1280]{1,0:T(8,128)(2,1)S(1)} %copy-done.2), custom_call_target="tpu_custom_call" | custom-call | tf_op jit(solution)/shard_map/hidden/pallas_call | solution.py:486
  54.4 0.1 collective-permute-start.2
  54.5 1.0 %collective-permute-start.1 = (bf16[8,1280]{1,0:T(8,128)(2,1)S(1)}, bf16[8,1280]{1,0:T(8,128)(2,1)S(1)}, u32[]{:S(2)}, u32[]{:S(2)}) collective-permute-start(bf16[8,1280]{1,0:T(8,128)(2,1)S(1)} %get-tuple-element.28.own), channel_id=1, source_target_pairs={{0,1},{1,0},{2,3},{3,2},{128,129},{129,128},{130,131},{131,130},{4... | collective-permute-start | bytes 61448 | tf_op jit(solution)/shard_map/ppermute | solution.py:360
  55.5 0.6 %collective-permute-start = (bf16[8,1280]{1,0:T(8,128)(2,1)S(1)}, bf16[8,1280]{1,0:T(8,128)(2,1)S(1)}, u32[]{:S(2)}, u32[]{:S(2)}) collective-permute-start(bf16[8,1280]{1,0:T(8,128)(2,1)S(1)} %get-tuple-element.28.own), channel_id=1, source_target_pairs={{0,131},{1,2},{2,1},{3,128},{128,3},{129,130},{130,129},{131,0},{4... | collective-permute-start | bytes 61448 | tf_op jit(solution)/shard_map/ppermute | solution.py:360
  56.1 3.2 %collective-permute-done.2.across = bf16[8,1280]{1,0:T(8,128)(2,1)S(1)} collective-permute-done((bf16[8,1280]{1,0:T(8,128)(2,1)S(1)}, bf16[8,1280]{1,0:T(8,128)(2,1)S(1)}, u32[]{:S(2)}, u32[]{:S(2)}) %collective-permute-start.2) | collective-permute-done | bytes 20512 | tf_op jit(solution)/shard_map/ppermute | solution.py:360
  59.3 0.0 collective-permute-done.1.near
  59.3 1.2 %collective-permute-done.far = bf16[8,1280]{1,0:T(8,128)(2,1)S(1)} collective-permute-done((bf16[8,1280]{1,0:T(8,128)(2,1)S(1)}, bf16[8,1280]{1,0:T(8,128)(2,1)S(1)}, u32[]{:S(2)}, u32[]{:S(2)}) %collective-permute-start) | collective-permute-done | bytes 20512 | tf_op jit(solution)/shard_map/ppermute | solution.py:360
  60.5 0.6 %finish.1 = f32[8,1280]{1,0:T(8,128)} custom-call(f32[8,128]{1,0:T(8,128)S(1)} %get-tuple-element.18.served, f32[8,1280]{1,0:T(8,128)S(1)} %get-tuple-element.27.residual, bf16[8,1280]{1,0:T(8,128)(2,1)S(1)} %get-tuple-element.28.own, bf16[8,1280]{1,0:T(8,128)(2,1)S(1)} %collective-permute-done.far, bf16[8,1280]{1,0:T(8,128)(2,1)S(1)} %collective-permute-done.1.near, ...), custom_call_target="tpu_custom_call" | custom-call | tf_op jit(solution)/shard_map/finish/pallas_call | solution.py:494
Async XLA Ops:
  3.0 14.6 %all-to-all-start = ((bf16[32,8,384]{2,1,0:T(8,128)(2,1)}), bf16[32,8,384]{2,1,0:T(8,128)(2,1)S(1)}, u32[]{:S(2)}, u32[]{:S(2)}) async-start(bf16[32,8,384]{2,1,0:T(8,128)(2,1)} %bitcast.4), calls=%async_computation | async-start | bytes 393216 | tf_op jit(solution)/shard_map/all_to_all | solution.py:410
  17.7 16.5 %copy-start = (bf16[320,1280]{1,0:T(8,128)(2,1)S(1)}, bf16[320,1280]{1,0:T(8,128)(2,1)}, u32[]{:S(2)}) copy-start(bf16[320,1280]{1,0:T(8,128)(2,1)} %weight.1) | copy-start | bytes 2457604
  17.7 35.9 %copy-start.3 = (bf16[8,1280]{1,0:T(8,128)(2,1)S(1)}, bf16[8,1280]{1,0:T(8,128)(2,1)}, u32[]{:S(2)}) copy-start(bf16[8,1280]{1,0:T(8,128)(2,1)} %token_.1) | copy-start | bytes 61444
  22.2 31.4 %copy-start.1 = (bf16[1280,320]{0,1:T(8,128)(2,1)S(1)}, bf16[1280,320]{0,1:T(8,128)(2,1)}, u32[]{:S(2)}) copy-start(bf16[1280,320]{0,1:T(8,128)(2,1)} %param.18) | copy-start | bytes 2457604
  22.2 31.4 %copy-start.2 = (bf16[320,1280]{1,0:T(8,128)(2,1)S(1)}, bf16[320,1280]{1,0:T(8,128)(2,1)}, u32[]{:S(2)}) copy-start(bf16[320,1280]{1,0:T(8,128)(2,1)} %down.1) | copy-start | bytes 2457604
  54.4 4.9 %collective-permute-start.2 = (bf16[8,1280]{1,0:T(8,128)(2,1)S(1)}, bf16[8,1280]{1,0:T(8,128)(2,1)S(1)}, u32[]{:S(2)}, u32[]{:S(2)}) collective-permute-start(bf16[8,1280]{1,0:T(8,128)(2,1)S(1)} %get-tuple-element.28.own), channel_id=1, source_target_pairs={{0,2},{1,3},{2,0},{3,1},{128,130},{129,131},{130,128},{131,129},{4... | collective-permute-start | bytes 61448 | tf_op jit(solution)/shard_map/ppermute | solution.py:360
  54.5 4.8 %collective-permute-start.1 = (bf16[8,1280]{1,0:T(8,128)(2,1)S(1)}, bf16[8,1280]{1,0:T(8,128)(2,1)S(1)}, u32[]{:S(2)}, u32[]{:S(2)}) collective-permute-start(bf16[8,1280]{1,0:T(8,128)(2,1)S(1)} %get-tuple-element.28.own), channel_id=1, source_target_pairs={{0,1},{1,0},{2,3},{3,2},{128,129},{129,128},{130,131},{131,130},{4... | collective-permute-start | bytes 61448 | tf_op jit(solution)/shard_map/ppermute | solution.py:360
  55.5 5.0 %collective-permute-start = (bf16[8,1280]{1,0:T(8,128)(2,1)S(1)}, bf16[8,1280]{1,0:T(8,128)(2,1)S(1)}, u32[]{:S(2)}, u32[]{:S(2)}) collective-permute-start(bf16[8,1280]{1,0:T(8,128)(2,1)S(1)} %get-tuple-element.28.own), channel_id=1, source_target_pairs={{0,131},{1,2},{2,1},{3,128},{128,3},{129,130},{130,129},{131,0},{4... | collective-permute-start | bytes 61448 | tf_op jit(solution)/shard_map/ppermute | solution.py:360

commit v6 on v5

--- a/solution.py
+++ b/solution.py
@@ -293,10 +293,10 @@
     ).astype(BF16)
 
 
-def merge_kernel(shares, self_scores, values, homed, weight, spread):
+def merge_kernel(shares, self_scores, values, attended):
     rows = values.shape[0]
     count = shares.shape[0] // rows
-    heads = weight.shape[0] // HD
+    heads = STATS // HD
     sums = shares[...].astype(F32)
     tail = sums[:, 256:]
     joined = tail + pltpu.roll(tail, 128 - 16, 1) + pltpu.roll(tail, 128 - 32, 1)
@@ -325,18 +325,24 @@
         denominator = denominator + factor * totals[at]
         numerator = numerator + per_head(factor) * sums[at]
     result = numerator / jnp.where(wide_of < heads, per_head(denominator), 1.0)
-    attended = jnp.where(widen(homed[...], WIDE) > 0.0, result, 0.0).astype(BF16)
-    partial = jnp.dot(
+    attended[...] = result.astype(BF16)
+
+
+def out_kernel(homed, here, there, weight, partial):
+    stay = widen(homed[...], WIDE) > 0.0
+    attended = jnp.where(stay, here[...].astype(F32), there[...].astype(F32)).astype(BF16)
+    partial[...] = jnp.dot(
         attended[:, : weight.shape[0]], weight[...], preferred_element_type=F32
     ).astype(BF16)
-    for copy in range(spread.shape[0]):
-        spread[copy] = partial
-
-
-def hidden_kernel(token, shares, gain, up, down, residual, partial):
-    total = token[...].astype(F32)
-    for share in range(shares.shape[0]):
-        total = total + shares[share].astype(F32)
+
+
+def joined(own, near, across, far):
+    own, near, across, far = (v[...].astype(F32) for v in (own, near, across, far))
+    return (own + near) + (across + far)
+
+
+def hidden_kernel(token, own, near, across, far, gain, up, down, residual, partial):
+    total = token[...].astype(F32) + joined(own, near, across, far)
     residual[...] = total
     normed = root_norm(total, gain[...]).astype(BF16)
     hidden = dot_transposed(normed, up[...])
@@ -344,9 +350,8 @@
     partial[...] = jnp.dot(active, down[...], preferred_element_type=F32).astype(BF16)
 
 
-def finish_kernel(served, residual, own, far, near, across, out):
-    own, far, near, across = (v[...].astype(F32) for v in (own, far, near, across))
-    result = residual[...] + ((own + across) + (near + far))
+def finish_kernel(served, residual, own, near, across, far, out):
+    result = residual[...] + joined(own, near, across, far)
     out[...] = jnp.where(widen(served[...], result.shape[1]) > 0.0, result, 0.0)
 
 
@@ -354,17 +359,12 @@
     return jax.ShapeDtypeStruct(dims, dtype)
 
 
-def exchanged(value, partner):
-    axes = ("rep", "tp")
-    count = lax.axis_size("rep") * lax.axis_size("tp")
-    return lax.ppermute(value, axes, [(i, partner(i) % count) for i in range(count)])
-
-
 def from_others(value):
-    far = exchanged(value, lambda i: i + 1 if i % 2 else i - 1)
-    near = exchanged(value, lambda i: i ^ 1)
-    across = exchanged(value, lambda i: i ^ 2)
-    return far, near, across
+    count = lax.axis_size("tp")
+    return [
+        lax.ppermute(value, "tp", [(i, i ^ bits) for i in range(count)])
+        for bits in range(1, count)
+    ]
 
 
 def body(
@@ -471,26 +471,33 @@
     )
     shares = lax.all_to_all(shares, "kv", 0, 0, tiled=True)
 
-    everyone = ("rep", "tp")
-    count = lax.axis_size("rep") * lax.axis_size("tp")
-    partials = pl.pallas_call(
+    attended = pl.pallas_call(
         merge_kernel,
-        out_shape=shape((count, rows, features), BF16),
-        in_specs=[VMEM] * 5,
+        out_shape=shape((rows, WIDE), BF16),
+        in_specs=[VMEM] * 3,
         out_specs=VMEM,
         compiler_params=PARAMS,
         name="merge",
-    )(shares, self_scores, values, homed, out_weight)
-    partials = lax.all_to_all(partials, everyone, 0, 0, tiled=True)
+    )(shares, self_scores, values)
+    other = lax.ppermute(attended, "rep", [(0, 1), (1, 0)])
+
+    partial = pl.pallas_call(
+        out_kernel,
+        out_shape=shape((rows, features), BF16),
+        in_specs=[VMEM] * 4,
+        out_specs=VMEM,
+        compiler_params=PARAMS,
+        name="out_projection",
+    )(homed, attended, other, out_weight)
 
     residual, partial = pl.pallas_call(
         hidden_kernel,
         out_shape=(shape((rows, features), F32), shape((rows, features), BF16)),
-        in_specs=[VMEM] * 5,
+        in_specs=[VMEM] * 8,
         out_specs=(VMEM,) * 2,
         compiler_params=PARAMS,
         name="hidden",
-    )(token_state, partials, gain, up_weight.T, down_weight)
+    )(token_state, partial, *from_others(partial), gain, up_weight.T, down_weight)
     result = pl.pallas_call(
         finish_kernel,
         out_shape=shape((rows, features), F32),

time: 61.4 us -> 60.7 us (0.989); the launches traced: 61.1 us -> 59.7 us
  blocking collectives: 30.7 us -> 11.9 us
  starting transfers between devices: 9.34 us -> 23.8 us
  waiting for transfers between devices: 7.91 us -> 10.8 us
    all_to_all x1 -> x0, blocking collectives: 18.7 us -> none  [body(): partials = lax.all_to_all(partials, everyone, 0, 0, tiled=True)]
    ppermute x3 -> x7, starting transfers between devices: 1.7 us -> 16.1 us  [the longest x6 8.87 us: from_others(): lax.ppermute(value, 'tp', [(i, i ^ bits) for i in range(count)])]
    ppermute x3 -> x7, waiting for transfers between devices: 4.36 us -> 7.24 us  [the longest x6 5.63 us: from_others(): lax.ppermute(value, 'tp', [(i, i ^ bits) for i in range(count)])]
  transfers between devices with their start and end apart: 4 -> 8, of which waited for: 3 -> 7; matrix products, arithmetic and copies ran while one was open for 0% -> 0% of each run, Pallas kernels for 5% -> 6%
where the time goes in v6:
time: 60.7 us; the launch traced here: 59.7 us
  starting transfers between devices  23.8 us (39%)
  Pallas kernels  12.5 us (21%)
  blocking collectives  11.9 us (20%)
  waiting for transfers between devices  10.8 us (18%)
  between operations  0.7 us (1%)
    all_to_all x1, blocking collectives, body(): shares = lax.all_to_all(shares, 'kv', 0, 0, tiled=True)  11.9 us
    ppermute x6, starting transfers between devices, from_others(): lax.ppermute(value, 'tp', [(i, i ^ bits) for i in range(count)])  8.87 us
    all_to_all x1, starting transfers between devices, body(): queries = lax.all_to_all(spread, 'kv', 0, 0, tiled=True)  7.63 us
    ppermute x1, starting transfers between devices, body(): other = lax.ppermute(attended, 'rep', [(0, 1), (1, 0)])  7.27 us
    ppermute x6, waiting for transfers between devices, from_others(): lax.ppermute(value, 'tp', [(i, i ^ bits) for i in range(count)])  5.63 us
    pallas_call x1, Pallas kernels, body(): pl.pallas_call(attend_kernel, out_shape=shape((requests, WIDE), BF16), in...  4.58 us
    all_to_all x1, waiting for transfers between devices, body(): queries = lax.all_to_all(spread, 'kv', 0, 0, tiled=True)  3.54 us
    pallas_call x1, Pallas kernels, body(): pl.pallas_call(side_kernel, out_shape=(pltpu.VMEM((EARLY, tokens, width),...  3.36 us
  transfers between devices with their start and end apart: 8, of which 7 were waited for; matrix products, arithmetic and copies ran while one was open for 0% of the time, Pallas kernels for 6%

profile of v6, /device:TPU:2, one launch (start us, length us, event | category | flops | bytes accessed | tf_op | source)
XLA Modules:
  0.0 59.7 jit_solution(13175153732576338369)
XLA Ops:
  0.6 2.4 %query.1 = (bf16[256,384]{1,0:T(8,128)(2,1)}, bf16[8,384]{1,0:T(8,128)(2,1)S(1)}, bf16[8,1280]{1,0:T(8,128)(2,1)S(1)}) custom-call(bf16[8,1280]{1,0:T(8,128)(2,1)} %token_.1, f32[1280]{0:T(1024)} %gain_hbm.2, bf16[960,1280]{1,0:T(8,128)(2,1)} %bitcast.17), custom_call_target="tpu_custom_call" | custom-call | tf_op jit(solution)/shard_map/query/pallas_call | solution.py:392
  3.0 7.6 %all-to-all-start = ((bf16[32,8,384]{2,1,0:T(8,128)(2,1)}), bf16[32,8,384]{2,1,0:T(8,128)(2,1)S(1)}, u32[]{:S(2)}, u32[]{:S(2)}) async-start(bf16[32,8,384]{2,1,0:T(8,128)(2,1)} %bitcast.4), calls=%async_computation | async-start | bytes 393216 | tf_op jit(solution)/shard_map/all_to_all | solution.py:410
  10.7 0.1 pad_add_fusion.place
  10.8 3.4 %side.1 = (bf16[3,512,640]{2,1,0:T(8,128)(2,1)S(1)}, s32[16,128]{1,0:T(8,128)S(1)}, s32[16,128]{1,0:T(8,128)S(1)}, f32[8,640]{1,0:T(8,128)}, f32[8,128]{1,0:T(8,...) custom-call(s32[2]{0:T(128)S(1)} %pad_add_fusion.place, ...), custom_call_target="tpu_custom_call" | custom-call | bytes 3932160 | tf_op jit(solution)/shard_map/side/pallas_call | solution.py:413
  14.1 3.5 %all-to-all-done = bf16[32,8,384]{2,1,0:T(8,128)(2,1)S(1)} async-done(((bf16[32,8,384]{2,1,0:T(8,128)(2,1)}), bf16[32,8,384]{2,1,0:T(8,128)(2,1)S(1)}, u32[]{:S(2)}, u32[]{:S(2)}) %all-to-all-start) | async-done | bytes 196640 | tf_op jit(solution)/shard_map/all_to_all | solution.py:410
  17.7 0.0 copy-start.2
  17.7 0.0 copy-start
  17.7 0.0 copy-start.1
  17.7 0.0 copy-start.3
  17.7 4.6 %attend.1 = bf16[256,384]{1,0:T(8,128)(2,1)S(1)} custom-call(s32[16,128]{1,0:T(8,128)S(1)} %get-tuple-element.20.owner_of, s32[16,128]{1,0:T(8,128)S(1)} %get-tuple-element.21.remains, bf16[256,384]{1,0:T(8,128)(2,1)S(1)} %bitcast.13, bf16[3,512,640]{2,1,0:T(8,128)(2,1)S(1)} %get-tuple-element.23.early, bf16[11,512,640]{2,1,0:T(8,128)(2,1)} %bitcast.16), custom_call_target="tpu_custom_call" | custom-call | tf_op jit(solution)/shard_map/attend/pallas_call | solution.py:452
  22.3 11.9 %all_to_all.22 = bf16[32,8,384]{2,1,0:T(8,128)(2,1)S(1)} all-to-all(bf16[32,8,384]{2,1,0:T(8,128)(2,1)S(1)} %bitcast.14), channel_id=1, replica_groups=mesh['rep'=2,'kv'=32,'tp'=4] {'kv'}, dimensions={0} | all-to-all | bytes 393216 | tf_op jit(solution)/shard_map/all_to_all | solution.py:472
  34.1 0.5 merge.1.here
  34.6 7.3 %collective-permute-start = (bf16[8,384]{1,0:T(8,128)(2,1)S(1)}, bf16[8,384]{1,0:T(8,128)(2,1)S(1)}, u32[]{:S(2)}, u32[]{:S(2)}) collective-permute-start(bf16[8,384]{1,0:T(8,128)(2,1)S(1)} %merge.1.here), channel_id=1, source_target_pairs={{0,128},{128,0},{1,129},{129,1},{2,130},{130,2},{3,131},{131,3},{4... | collective-permute-start | bytes 18440 | tf_op jit(solution)/shard_map/ppermute | solution.py:482
  41.9 1.6 %collective-permute-done.there = bf16[8,384]{1,0:T(8,128)(2,1)S(1)} collective-permute-done((bf16[8,384]{1,0:T(8,128)(2,1)S(1)}, bf16[8,384]{1,0:T(8,128)(2,1)S(1)}, u32[]{:S(2)}, u32[]{:S(2)}) %collective-permute-start) | collective-permute-done | bytes 6176 | tf_op jit(solution)/shard_map/ppermute | solution.py:482
  43.5 0.0 copy-done.2
  43.5 0.2 out_projection.1.own
  43.7 3.4 %collective-permute-start.3 = (bf16[8,1280]{1,0:T(8,128)(2,1)S(1)}, bf16[8,1280]{1,0:T(8,128)(2,1)S(1)}, u32[]{:S(2)}, u32[]{:S(2)}) collective-permute-start(bf16[8,1280]{1,0:T(8,128)(2,1)S(1)} %out_projection.1.own), channel_id=1, source_target_pairs={{0,3},{1,2},{2,1},{3,0},{4,7},{5,6},{6,5},{7,4},{8,11},{9,10},{10,... | collective-permute-start | bytes 61448 | tf_op jit(solution)/shard_map/ppermute | solution.py:365
  47.2 0.0 collective-permute-start.2
  47.2 1.0 %collective-permute-start.1 = (bf16[8,1280]{1,0:T(8,128)(2,1)S(1)}, bf16[8,1280]{1,0:T(8,128)(2,1)S(1)}, u32[]{:S(2)}, u32[]{:S(2)}) collective-permute-start(bf16[8,1280]{1,0:T(8,128)(2,1)S(1)} %out_projection.1.own), channel_id=1, source_target_pairs={{0,1},{1,0},{2,3},{3,2},{4,5},{5,4},{6,7},{7,6},{8,9},{9,8},{10,11... | collective-permute-start | bytes 61448 | tf_op jit(solution)/shard_map/ppermute | solution.py:365
  48.2 1.2 %collective-permute-done.3.far = bf16[8,1280]{1,0:T(8,128)(2,1)S(1)} collective-permute-done((bf16[8,1280]{1,0:T(8,128)(2,1)S(1)}, bf16[8,1280]{1,0:T(8,128)(2,1)S(1)}, u32[]{:S(2)}, u32[]{:S(2)}) %collective-permute-start.3) | collective-permute-done | bytes 20512 | tf_op jit(solution)/shard_map/ppermute | solution.py:365
  49.4 2.5 %collective-permute-done.2.across = bf16[8,1280]{1,0:T(8,128)(2,1)S(1)} collective-permute-done((bf16[8,1280]{1,0:T(8,128)(2,1)S(1)}, bf16[8,1280]{1,0:T(8,128)(2,1)S(1)}, u32[]{:S(2)}, u32[]{:S(2)}) %collective-permute-start.2) | collective-permute-done | bytes 20512 | tf_op jit(solution)/shard_map/ppermute | solution.py:365
  51.8 0.0 collective-permute-done.1.near
  51.9 0.0 copy-done
  51.9 0.0 copy-done.1
  51.9 0.0 copy-done.3
  51.9 0.8 %hidden.1 = (f32[8,1280]{1,0:T(8,128)S(1)}, bf16[8,1280]{1,0:T(8,128)(2,1)S(1)}) custom-call(bf16[8,1280]{1,0:T(8,128)(2,1)S(1)} %copy-done.3, bf16[8,1280]{1,0:T(8,128)(2,1)S(1)} %out_projection.1.own, bf16[8,1280]{1,0:T(8,128)(2,1)S(1)} %collective-permute-done.1.near, bf16[8,1280]{1,0:T(8,128)(2,1)S(1)} %collective-permute-done.2.across, ...), custom_call_target="tpu_custom_call" | custom-call | tf_op jit(solution)/shard_map/hidden/pallas_call | solution.py:493
  52.7 1.5 %collective-permute-start.6 = (bf16[8,1280]{1,0:T(8,128)(2,1)S(1)}, bf16[8,1280]{1,0:T(8,128)(2,1)S(1)}, u32[]{:S(2)}, u32[]{:S(2)}) collective-permute-start(bf16[8,1280]{1,0:T(8,128)(2,1)S(1)} %get-tuple-element.28.own), channel_id=1, source_target_pairs={{0,3},{1,2},{2,1},{3,0},{4,7},{5,6},{6,5},{7,4},{8,11},{9,10},{10,... | collective-permute-start | bytes 61448 | tf_op jit(solution)/shard_map/ppermute | solution.py:365
  54.1 0.6 %collective-permute-start.5 = (bf16[8,1280]{1,0:T(8,128)(2,1)S(1)}, bf16[8,1280]{1,0:T(8,128)(2,1)S(1)}, u32[]{:S(2)}, u32[]{:S(2)}) collective-permute-start(bf16[8,1280]{1,0:T(8,128)(2,1)S(1)} %get-tuple-element.28.own), channel_id=1, source_target_pairs={{0,2},{1,3},{2,0},{3,1},{4,6},{5,7},{6,4},{7,5},{8,10},{9,11},{10,... | collective-permute-start | bytes 61448 | tf_op jit(solution)/shard_map/ppermute | solution.py:365
  54.8 2.3 %collective-permute-start.4 = (bf16[8,1280]{1,0:T(8,128)(2,1)S(1)}, bf16[8,1280]{1,0:T(8,128)(2,1)S(1)}, u32[]{:S(2)}, u32[]{:S(2)}) collective-permute-start(bf16[8,1280]{1,0:T(8,128)(2,1)S(1)} %get-tuple-element.28.own), channel_id=1, source_target_pairs={{0,1},{1,0},{2,3},{3,2},{4,5},{5,4},{6,7},{7,6},{8,9},{9,8},{10,11... | collective-permute-start | bytes 61448 | tf_op jit(solution)/shard_map/ppermute | solution.py:365
  57.1 1.2 %collective-permute-done.6.far = bf16[8,1280]{1,0:T(8,128)(2,1)S(1)} collective-permute-done((bf16[8,1280]{1,0:T(8,128)(2,1)S(1)}, bf16[8,1280]{1,0:T(8,128)(2,1)S(1)}, u32[]{:S(2)}, u32[]{:S(2)}) %collective-permute-start.6) | collective-permute-done | bytes 20512 | tf_op jit(solution)/shard_map/ppermute | solution.py:365
  58.3 0.6 collective-permute-done.5.across
  58.8 0.2 collective-permute-done.4.near
  59.0 0.6 %finish.1 = f32[8,1280]{1,0:T(8,128)} custom-call(f32[8,128]{1,0:T(8,128)S(1)} %get-tuple-element.18.served, f32[8,1280]{1,0:T(8,128)S(1)} %get-tuple-element.27.residual, bf16[8,1280]{1,0:T(8,128)(2,1)S(1)} %get-tuple-element.28.own, bf16[8,1280]{1,0:T(8,128)(2,1)S(1)} %collective-permute-done.4.near, bf16[8,1280]{1,0:T(8,128)(2,1)S(1)} %collective-permute-done.5.across, ...), custom_call_target="tpu_custom_call" | custom-call | tf_op jit(solution)/shard_map/finish/pallas_call | solution.py:501
Async XLA Ops:
  3.0 14.6 %all-to-all-start = ((bf16[32,8,384]{2,1,0:T(8,128)(2,1)}), bf16[32,8,384]{2,1,0:T(8,128)(2,1)S(1)}, u32[]{:S(2)}, u32[]{:S(2)}) async-start(bf16[32,8,384]{2,1,0:T(8,128)(2,1)} %bitcast.4), calls=%async_computation | async-start | bytes 393216 | tf_op jit(solution)/shard_map/all_to_all | solution.py:410
  17.7 25.9 %copy-start.2 = (bf16[320,1280]{1,0:T(8,128)(2,1)S(1)}, bf16[320,1280]{1,0:T(8,128)(2,1)}, u32[]{:S(2)}) copy-start(bf16[320,1280]{1,0:T(8,128)(2,1)} %weight.1) | copy-start | bytes 2457604
  17.7 34.2 %copy-start = (bf16[1280,320]{0,1:T(8,128)(2,1)S(1)}, bf16[1280,320]{0,1:T(8,128)(2,1)}, u32[]{:S(2)}) copy-start(bf16[1280,320]{0,1:T(8,128)(2,1)} %param.18) | copy-start | bytes 2457604
  17.7 34.2 %copy-start.1 = (bf16[320,1280]{1,0:T(8,128)(2,1)S(1)}, bf16[320,1280]{1,0:T(8,128)(2,1)}, u32[]{:S(2)}) copy-start(bf16[320,1280]{1,0:T(8,128)(2,1)} %down.1) | copy-start | bytes 2457604
  17.7 34.2 %copy-start.3 = (bf16[8,1280]{1,0:T(8,128)(2,1)S(1)}, bf16[8,1280]{1,0:T(8,128)(2,1)}, u32[]{:S(2)}) copy-start(bf16[8,1280]{1,0:T(8,128)(2,1)} %token_.1) | copy-start | bytes 61444
  34.6 8.9 %collective-permute-start = (bf16[8,384]{1,0:T(8,128)(2,1)S(1)}, bf16[8,384]{1,0:T(8,128)(2,1)S(1)}, u32[]{:S(2)}, u32[]{:S(2)}) collective-permute-start(bf16[8,384]{1,0:T(8,128)(2,1)S(1)} %merge.1.here), channel_id=1, source_target_pairs={{0,128},{128,0},{1,129},{129,1},{2,130},{130,2},{3,131},{131,3},{4... | collective-permute-start | bytes 18440 | tf_op jit(solution)/shard_map/ppermute | solution.py:482
  43.7 5.7 %collective-permute-start.3 = (bf16[8,1280]{1,0:T(8,128)(2,1)S(1)}, bf16[8,1280]{1,0:T(8,128)(2,1)S(1)}, u32[]{:S(2)}, u32[]{:S(2)}) collective-permute-start(bf16[8,1280]{1,0:T(8,128)(2,1)S(1)} %out_projection.1.own), channel_id=1, source_target_pairs={{0,3},{1,2},{2,1},{3,0},{4,7},{5,6},{6,5},{7,4},{8,11},{9,10},{10,... | collective-permute-start | bytes 61448 | tf_op jit(solution)/shard_map/ppermute | solution.py:365
  47.2 4.7 %collective-permute-start.2 = (bf16[8,1280]{1,0:T(8,128)(2,1)S(1)}, bf16[8,1280]{1,0:T(8,128)(2,1)S(1)}, u32[]{:S(2)}, u32[]{:S(2)}) collective-permute-start(bf16[8,1280]{1,0:T(8,128)(2,1)S(1)} %out_projection.1.own), channel_id=1, source_target_pairs={{0,2},{1,3},{2,0},{3,1},{4,6},{5,7},{6,4},{7,5},{8,10},{9,11},{10,... | collective-permute-start | bytes 61448 | tf_op jit(solution)/shard_map/ppermute | solution.py:365
  47.2 4.7 %collective-permute-start.1 = (bf16[8,1280]{1,0:T(8,128)(2,1)S(1)}, bf16[8,1280]{1,0:T(8,128)(2,1)S(1)}, u32[]{:S(2)}, u32[]{:S(2)}) collective-permute-start(bf16[8,1280]{1,0:T(8,128)(2,1)S(1)} %out_projection.1.own), channel_id=1, source_target_pairs={{0,1},{1,0},{2,3},{3,2},{4,5},{5,4},{6,7},{7,6},{8,9},{9,8},{10,11... | collective-permute-start | bytes 61448 | tf_op jit(solution)/shard_map/ppermute | solution.py:365
  52.7 5.6 %collective-permute-start.6 = (bf16[8,1280]{1,0:T(8,128)(2,1)S(1)}, bf16[8,1280]{1,0:T(8,128)(2,1)S(1)}, u32[]{:S(2)}, u32[]{:S(2)}) collective-permute-start(bf16[8,1280]{1,0:T(8,128)(2,1)S(1)} %get-tuple-element.28.own), channel_id=1, source_target_pairs={{0,3},{1,2},{2,1},{3,0},{4,7},{5,6},{6,5},{7,4},{8,11},{9,10},{10,... | collective-permute-start | bytes 61448 | tf_op jit(solution)/shard_map/ppermute | solution.py:365
  54.1 4.7 %collective-permute-start.5 = (bf16[8,1280]{1,0:T(8,128)(2,1)S(1)}, bf16[8,1280]{1,0:T(8,128)(2,1)S(1)}, u32[]{:S(2)}, u32[]{:S(2)}) collective-permute-start(bf16[8,1280]{1,0:T(8,128)(2,1)S(1)} %get-tuple-element.28.own), channel_id=1, source_target_pairs={{0,2},{1,3},{2,0},{3,1},{4,6},{5,7},{6,4},{7,5},{8,10},{9,11},{10,... | collective-permute-start | bytes 61448 | tf_op jit(solution)/shard_map/ppermute | solution.py:365
  54.8 4.3 %collective-permute-start.4 = (bf16[8,1280]{1,0:T(8,128)(2,1)S(1)}, bf16[8,1280]{1,0:T(8,128)(2,1)S(1)}, u32[]{:S(2)}, u32[]{:S(2)}) collective-permute-start(bf16[8,1280]{1,0:T(8,128)(2,1)S(1)} %get-tuple-element.28.own), channel_id=1, source_target_pairs={{0,1},{1,0},{2,3},{3,2},{4,5},{5,4},{6,7},{7,6},{8,9},{9,8},{10,11... | collective-permute-start | bytes 61448 | tf_op jit(solution)/shard_map/ppermute | solution.py:365

commit v7 on v6

--- a/solution.py
+++ b/solution.py
@@ -11,7 +11,7 @@
 PAIR = 2 * HD
 VERY_LOW = -1e30
 NORM_EPS = 1e-06
-EARLY = 3
+EARLY = 5
 LATE_GROUP = 2
 STATS = 320
 WIDE = 384
@@ -20,7 +20,6 @@
 
 VMEM = pl.BlockSpec(memory_space=pltpu.VMEM)
 HBM = pl.BlockSpec(memory_space=pltpu.HBM)
-SMEM = pl.BlockSpec(memory_space=pltpu.SMEM)
 PARAMS = pltpu.CompilerParams(vmem_limit_bytes=16 * 1024 * 1024)
 
 
@@ -73,19 +72,19 @@
     rows = token.shape[0]
     heads = weight_hbm.shape[0] // (3 * HD)
     copies = fetch(
-        [(token_hbm, token), (gain_hbm, gain.at[0])]
-        + [
+        [
             (weight_hbm.at[3 * HD * h : 3 * HD * h + HD], weight.at[HD * h : HD * (h + 1)])
             for h in range(heads)
-        ],
+        ]
+        + [(token_hbm, token), (gain_hbm, gain.at[0])],
         sems,
     )
     weight[heads * HD :, :] = jnp.zeros((WIDE - heads * HD, weight.shape[1]), BF16)
-    copies[0].wait()
-    copies[1].wait()
+    copies[heads].wait()
+    copies[heads + 1].wait()
     norm = root_norm(token[...].astype(F32), gain[...]).astype(BF16)
     normed[...] = norm
-    for copy in copies[2:]:
+    for copy in copies[:heads]:
         copy.wait()
     own = (dot_transposed(norm, weight[...]) * HD ** (-0.5)).astype(BF16)
     query[...] = own
@@ -94,7 +93,6 @@
 
 
 def side_kernel(
-    place,
     owner_hbm,
     index_hbm,
     length_hbm,
@@ -156,11 +154,12 @@
         left = jnp.where(row == b, most - index[0, b] * tokens, left)
     owners[...] = holders
     remains[...] = left
-    start = place[1] * rows
+    start = lax.axis_index("kv") * rows
+    replica = lax.axis_index("rep")
     at_home = row_values(home, start, rows, 128)
     target = at_home ^ row_values(moving, start, rows, 128)
-    homed[...] = jnp.where(at_home == place[0], 1.0, 0.0)
-    serves = jnp.where(target == place[0], 1.0, 0.0)
+    homed[...] = jnp.where(at_home == replica, 1.0, 0.0)
+    serves = jnp.where(target == replica, 1.0, 0.0)
     served[...] = serves
     for copy in copies[5:-1]:
         copy.wait()
@@ -341,7 +340,7 @@
     return (own + near) + (across + far)
 
 
-def hidden_kernel(token, own, near, across, far, gain, up, down, residual, partial):
+def hidden_kernel(token, own, near, far, across, gain, up, down, residual, partial):
     total = token[...].astype(F32) + joined(own, near, across, far)
     residual[...] = total
     normed = root_norm(total, gain[...]).astype(BF16)
@@ -350,7 +349,7 @@
     partial[...] = jnp.dot(active, down[...], preferred_element_type=F32).astype(BF16)
 
 
-def finish_kernel(served, residual, own, near, across, far, out):
+def finish_kernel(served, residual, own, near, far, across, out):
     result = residual[...] + joined(own, near, across, far)
     out[...] = jnp.where(widen(served[...], result.shape[1]) > 0.0, result, 0.0)
 
@@ -363,7 +362,7 @@
     count = lax.axis_size("tp")
     return [
         lax.ppermute(value, "tp", [(i, i ^ bits) for i in range(count)])
-        for bits in range(1, count)
+        for bits in (1, 3, 2)
     ]
 
 
@@ -386,7 +385,6 @@
     requests = home_replica.shape[0]
     _, blocks, tokens, width = kv_cache.shape
     heads = width // PAIR
-    place = jnp.stack([lax.axis_index("rep"), lax.axis_index("kv")]).astype(jnp.int32)
 
     weight = qkv_weight.T
     spread, query, normed = pl.pallas_call(
@@ -423,7 +421,7 @@
             shape((rows, WIDE), F32),
             shape((1, features), F32),
         ),
-        in_specs=[SMEM] + [HBM] * 8 + [VMEM] * 2,
+        in_specs=[HBM] * 8 + [VMEM] * 2,
         out_specs=(VMEM,) * 9,
         scratch_shapes=[pltpu.SMEM((1, blocks), jnp.int32)] * 2
         + [pltpu.SMEM((requests,), jnp.int32)] * 3
@@ -434,7 +432,6 @@
         ),
         name="side",
     )(
-        place,
         *in_hbm(
             block_owner,
             block_index,

time: 60.7 us -> 59.9 us (0.987); the launches traced: 59.7 us -> 59.6 us
  waiting for transfers between devices: 10.8 us -> 12.7 us
  starting transfers between devices: 23.8 us -> 22.4 us
    ppermute x6, waiting for transfers between devices: 5.63 us -> 7.33 us  [from_others(): lax.ppermute(value, 'tp', [(i, i ^ bits) for i in range(count)])]
    ppermute x6, starting transfers between devices: 8.87 us -> 7.51 us  [from_others(): lax.ppermute(value, 'tp', [(i, i ^ bits) for i in range(count)])]
  transfers between devices with their start and end apart: 8 -> 8, of which waited for: 7 -> 6; matrix products, arithmetic and copies ran while one was open for 0% -> 0% of each run, Pallas kernels for 6% -> 5%
where the time goes in v7:
time: 59.9 us; the launch traced here: 59.6 us
  starting transfers between devices  22.4 us (37%)
  waiting for transfers between devices  12.7 us (21%)
  Pallas kernels  11.9 us (20%)
  blocking collectives  11.9 us (20%)
  between operations  0.69 us (1%)
    all_to_all x1, blocking collectives, body(): shares = lax.all_to_all(shares, 'kv', 0, 0, tiled=True)  11.9 us
    all_to_all x1, starting transfers between devices, body(): queries = lax.all_to_all(spread, 'kv', 0, 0, tiled=True)  7.63 us
    ppermute x6, starting transfers between devices, from_others(): lax.ppermute(value, 'tp', [(i, i ^ bits) for i in range(count)])  7.51 us
    ppermute x6, waiting for transfers between devices, from_others(): lax.ppermute(value, 'tp', [(i, i ^ bits) for i in range(count)])  7.33 us
    ppermute x1, starting transfers between devices, body(): other = lax.ppermute(attended, 'rep', [(0, 1), (1, 0)])  7.28 us
    pallas_call x1, Pallas kernels, body(): pl.pallas_call(attend_kernel, out_shape=shape((requests, WIDE), BF16), in...  4.24 us
    all_to_all x1, waiting for transfers between devices, body(): queries = lax.all_to_all(spread, 'kv', 0, 0, tiled=True)  3.81 us
    pallas_call x1, Pallas kernels, body(): pl.pallas_call(side_kernel, out_shape=(pltpu.VMEM((EARLY, tokens, width),...  3.17 us
  transfers between devices with their start and end apart: 8, of which 6 were waited for; matrix products, arithmetic and copies ran while one was open for 0% of the time, Pallas kernels for 5%

profile of v7, /device:TPU:2, one launch (start us, length us, event | category | flops | bytes accessed | tf_op | source)
XLA Modules:
  0.0 59.6 jit_solution(19976395082783275)
XLA Ops:
  0.6 2.4 %query.1 = (bf16[256,384]{1,0:T(8,128)(2,1)}, bf16[8,384]{1,0:T(8,128)(2,1)S(1)}, bf16[8,1280]{1,0:T(8,128)(2,1)S(1)}) custom-call(bf16[8,1280]{1,0:T(8,128)(2,1)} %token_.1, f32[1280]{0:T(1024)} %gain_hbm.2, bf16[960,1280]{1,0:T(8,128)(2,1)} %bitcast.15), custom_call_target="tpu_custom_call" | custom-call | tf_op jit(solution)/shard_map/query/pallas_call | solution.py:390
  3.0 7.6 %all-to-all-start = ((bf16[32,8,384]{2,1,0:T(8,128)(2,1)}), bf16[32,8,384]{2,1,0:T(8,128)(2,1)S(1)}, u32[]{:S(2)}, u32[]{:S(2)}) async-start(bf16[32,8,384]{2,1,0:T(8,128)(2,1)} %bitcast.2), calls=%async_computation | async-start | bytes 393216 | tf_op jit(solution)/shard_map/all_to_all | solution.py:408
  10.6 3.2 %side.1 = (bf16[5,512,640]{2,1,0:T(8,128)(2,1)S(1)}, s32[16,128]{1,0:T(8,128)S(1)}, s32[16,128]{1,0:T(8,128)S(1)}, f32[8,640]{1,0:T(8,128)}, f32[8,128]{1,0:T(8,...) custom-call(s32[1,11]{1,0:T(1,128)} %owner_hbm.1, ...), custom_call_target="tpu_custom_call" | custom-call | bytes 6553600 | tf_op jit(solution)/shard_map/side/pallas_call | solution.py:411
  13.8 3.8 %all-to-all-done = bf16[32,8,384]{2,1,0:T(8,128)(2,1)S(1)} async-done(((bf16[32,8,384]{2,1,0:T(8,128)(2,1)}), bf16[32,8,384]{2,1,0:T(8,128)(2,1)S(1)}, u32[]{:S(2)}, u32[]{:S(2)}) %all-to-all-start) | async-done | bytes 196640 | tf_op jit(solution)/shard_map/all_to_all | solution.py:408
  17.6 0.0 copy-start.2
  17.6 0.0 copy-start
  17.6 0.0 copy-start.1
  17.6 0.0 copy-start.3
  17.6 4.2 %attend.1 = bf16[256,384]{1,0:T(8,128)(2,1)S(1)} custom-call(s32[16,128]{1,0:T(8,128)S(1)} %get-tuple-element.20.owner_of, s32[16,128]{1,0:T(8,128)S(1)} %get-tuple-element.21.remains, bf16[256,384]{1,0:T(8,128)(2,1)S(1)} %bitcast.11, bf16[5,512,640]{2,1,0:T(8,128)(2,1)S(1)} %get-tuple-element.23.early, bf16[11,512,640]{2,1,0:T(8,128)(2,1)} %bitcast.14), custom_call_target="tpu_custom_call" | custom-call | tf_op jit(solution)/shard_map/attend/pallas_call | solution.py:449
  21.9 11.9 %all_to_all.22 = bf16[32,8,384]{2,1,0:T(8,128)(2,1)S(1)} all-to-all(bf16[32,8,384]{2,1,0:T(8,128)(2,1)S(1)} %bitcast.12), channel_id=1, replica_groups=mesh['rep'=2,'kv'=32,'tp'=4] {'kv'}, dimensions={0} | all-to-all | bytes 393216 | tf_op jit(solution)/shard_map/all_to_all | solution.py:469
  33.8 0.5 merge.1.here
  34.3 7.3 %collective-permute-start = (bf16[8,384]{1,0:T(8,128)(2,1)S(1)}, bf16[8,384]{1,0:T(8,128)(2,1)S(1)}, u32[]{:S(2)}, u32[]{:S(2)}) collective-permute-start(bf16[8,384]{1,0:T(8,128)(2,1)S(1)} %merge.1.here), channel_id=1, source_target_pairs={{0,128},{128,0},{1,129},{129,1},{2,130},{130,2},{3,131},{131,3},{4... | collective-permute-start | bytes 18440 | tf_op jit(solution)/shard_map/ppermute | solution.py:479
  41.5 1.6 %collective-permute-done.there = bf16[8,384]{1,0:T(8,128)(2,1)S(1)} collective-permute-done((bf16[8,384]{1,0:T(8,128)(2,1)S(1)}, bf16[8,384]{1,0:T(8,128)(2,1)S(1)}, u32[]{:S(2)}, u32[]{:S(2)}) %collective-permute-start) | collective-permute-done | bytes 6176 | tf_op jit(solution)/shard_map/ppermute | solution.py:479
  43.2 0.0 copy-done.2
  43.2 0.2 out_projection.1.own
  43.4 2.1 %collective-permute-start.3 = (bf16[8,1280]{1,0:T(8,128)(2,1)S(1)}, bf16[8,1280]{1,0:T(8,128)(2,1)S(1)}, u32[]{:S(2)}, u32[]{:S(2)}) collective-permute-start(bf16[8,1280]{1,0:T(8,128)(2,1)S(1)} %out_projection.1.own), channel_id=1, source_target_pairs={{0,2},{1,3},{2,0},{3,1},{4,6},{5,7},{6,4},{7,5},{8,10},{9,11},{10,... | collective-permute-start | bytes 61448 | tf_op jit(solution)/shard_map/ppermute | solution.py:364
  45.4 1.5 %collective-permute-start.2 = (bf16[8,1280]{1,0:T(8,128)(2,1)S(1)}, bf16[8,1280]{1,0:T(8,128)(2,1)S(1)}, u32[]{:S(2)}, u32[]{:S(2)}) collective-permute-start(bf16[8,1280]{1,0:T(8,128)(2,1)S(1)} %out_projection.1.own), channel_id=1, source_target_pairs={{0,3},{1,2},{2,1},{3,0},{4,7},{5,6},{6,5},{7,4},{8,11},{9,10},{10,... | collective-permute-start | bytes 61448 | tf_op jit(solution)/shard_map/ppermute | solution.py:364
  46.9 0.5 collective-permute-start.1
  47.4 0.8 %collective-permute-done.3.across = bf16[8,1280]{1,0:T(8,128)(2,1)S(1)} collective-permute-done((bf16[8,1280]{1,0:T(8,128)(2,1)S(1)}, bf16[8,1280]{1,0:T(8,128)(2,1)S(1)}, u32[]{:S(2)}, u32[]{:S(2)}) %collective-permute-start.3) | collective-permute-done | bytes 20512 | tf_op jit(solution)/shard_map/ppermute | solution.py:364
  48.1 2.9 %collective-permute-done.2.far = bf16[8,1280]{1,0:T(8,128)(2,1)S(1)} collective-permute-done((bf16[8,1280]{1,0:T(8,128)(2,1)S(1)}, bf16[8,1280]{1,0:T(8,128)(2,1)S(1)}, u32[]{:S(2)}, u32[]{:S(2)}) %collective-permute-start.2) | collective-permute-done | bytes 20512 | tf_op jit(solution)/shard_map/ppermute | solution.py:364
  51.0 0.0 collective-permute-done.1.near
  51.0 0.0 copy-done
  51.0 0.0 copy-done.1
  51.0 0.0 copy-done.3
  51.0 0.8 %hidden.1 = (f32[8,1280]{1,0:T(8,128)S(1)}, bf16[8,1280]{1,0:T(8,128)(2,1)S(1)}) custom-call(bf16[8,1280]{1,0:T(8,128)(2,1)S(1)} %copy-done.3, bf16[8,1280]{1,0:T(8,128)(2,1)S(1)} %out_projection.1.own, bf16[8,1280]{1,0:T(8,128)(2,1)S(1)} %collective-permute-done.1.near, bf16[8,1280]{1,0:T(8,128)(2,1)S(1)} %collective-permute-done.2.far, ...), custom_call_target="tpu_custom_call" | custom-call | tf_op jit(solution)/shard_map/hidden/pallas_call | solution.py:490
  51.8 1.6 %collective-permute-start.6 = (bf16[8,1280]{1,0:T(8,128)(2,1)S(1)}, bf16[8,1280]{1,0:T(8,128)(2,1)S(1)}, u32[]{:S(2)}, u32[]{:S(2)}) collective-permute-start(bf16[8,1280]{1,0:T(8,128)(2,1)S(1)} %get-tuple-element.28.own), channel_id=1, source_target_pairs={{0,2},{1,3},{2,0},{3,1},{4,6},{5,7},{6,4},{7,5},{8,10},{9,11},{10,... | collective-permute-start | bytes 61448 | tf_op jit(solution)/shard_map/ppermute | solution.py:364
  53.4 0.9 %collective-permute-start.5 = (bf16[8,1280]{1,0:T(8,128)(2,1)S(1)}, bf16[8,1280]{1,0:T(8,128)(2,1)S(1)}, u32[]{:S(2)}, u32[]{:S(2)}) collective-permute-start(bf16[8,1280]{1,0:T(8,128)(2,1)S(1)} %get-tuple-element.28.own), channel_id=1, source_target_pairs={{0,3},{1,2},{2,1},{3,0},{4,7},{5,6},{6,5},{7,4},{8,11},{9,10},{10,... | collective-permute-start | bytes 61448 | tf_op jit(solution)/shard_map/ppermute | solution.py:364
  54.3 1.0 %collective-permute-start.4 = (bf16[8,1280]{1,0:T(8,128)(2,1)S(1)}, bf16[8,1280]{1,0:T(8,128)(2,1)S(1)}, u32[]{:S(2)}, u32[]{:S(2)}) collective-permute-start(bf16[8,1280]{1,0:T(8,128)(2,1)S(1)} %get-tuple-element.28.own), channel_id=1, source_target_pairs={{0,1},{1,0},{2,3},{3,2},{4,5},{5,4},{6,7},{7,6},{8,9},{9,8},{10,11... | collective-permute-start | bytes 61448 | tf_op jit(solution)/shard_map/ppermute | solution.py:364
  55.3 1.2 %collective-permute-done.6.across = bf16[8,1280]{1,0:T(8,128)(2,1)S(1)} collective-permute-done((bf16[8,1280]{1,0:T(8,128)(2,1)S(1)}, bf16[8,1280]{1,0:T(8,128)(2,1)S(1)}, u32[]{:S(2)}, u32[]{:S(2)}) %collective-permute-start.6) | collective-permute-done | bytes 20512 | tf_op jit(solution)/shard_map/ppermute | solution.py:364
  56.5 2.5 %collective-permute-done.5.far = bf16[8,1280]{1,0:T(8,128)(2,1)S(1)} collective-permute-done((bf16[8,1280]{1,0:T(8,128)(2,1)S(1)}, bf16[8,1280]{1,0:T(8,128)(2,1)S(1)}, u32[]{:S(2)}, u32[]{:S(2)}) %collective-permute-start.5) | collective-permute-done | bytes 20512 | tf_op jit(solution)/shard_map/ppermute | solution.py:364
  59.0 0.0 collective-permute-done.4.near
  59.0 0.6 %finish.1 = f32[8,1280]{1,0:T(8,128)} custom-call(f32[8,128]{1,0:T(8,128)S(1)} %get-tuple-element.18.served, f32[8,1280]{1,0:T(8,128)S(1)} %get-tuple-element.27.residual, bf16[8,1280]{1,0:T(8,128)(2,1)S(1)} %get-tuple-element.28.own, bf16[8,1280]{1,0:T(8,128)(2,1)S(1)} %collective-permute-done.4.near, bf16[8,1280]{1,0:T(8,128)(2,1)S(1)} %collective-permute-done.5.far, ...), custom_call_target="tpu_custom_call" | custom-call | tf_op jit(solution)/shard_map/finish/pallas_call | solution.py:498
Async XLA Ops:
  3.0 14.6 %all-to-all-start = ((bf16[32,8,384]{2,1,0:T(8,128)(2,1)}), bf16[32,8,384]{2,1,0:T(8,128)(2,1)S(1)}, u32[]{:S(2)}, u32[]{:S(2)}) async-start(bf16[32,8,384]{2,1,0:T(8,128)(2,1)} %bitcast.2), calls=%async_computation | async-start | bytes 393216 | tf_op jit(solution)/shard_map/all_to_all | solution.py:408
  17.6 25.5 %copy-start.2 = (bf16[320,1280]{1,0:T(8,128)(2,1)S(1)}, bf16[320,1280]{1,0:T(8,128)(2,1)}, u32[]{:S(2)}) copy-start(bf16[320,1280]{1,0:T(8,128)(2,1)} %weight.1) | copy-start | bytes 2457604
  17.6 33.4 %copy-start = (bf16[1280,320]{0,1:T(8,128)(2,1)S(1)}, bf16[1280,320]{0,1:T(8,128)(2,1)}, u32[]{:S(2)}) copy-start(bf16[1280,320]{0,1:T(8,128)(2,1)} %param.18) | copy-start | bytes 2457604
  17.6 33.4 %copy-start.1 = (bf16[320,1280]{1,0:T(8,128)(2,1)S(1)}, bf16[320,1280]{1,0:T(8,128)(2,1)}, u32[]{:S(2)}) copy-start(bf16[320,1280]{1,0:T(8,128)(2,1)} %down.1) | copy-start | bytes 2457604
  17.6 33.4 %copy-start.3 = (bf16[8,1280]{1,0:T(8,128)(2,1)S(1)}, bf16[8,1280]{1,0:T(8,128)(2,1)}, u32[]{:S(2)}) copy-start(bf16[8,1280]{1,0:T(8,128)(2,1)} %token_.1) | copy-start | bytes 61444
  34.3 8.9 %collective-permute-start = (bf16[8,384]{1,0:T(8,128)(2,1)S(1)}, bf16[8,384]{1,0:T(8,128)(2,1)S(1)}, u32[]{:S(2)}, u32[]{:S(2)}) collective-permute-start(bf16[8,384]{1,0:T(8,128)(2,1)S(1)} %merge.1.here), channel_id=1, source_target_pairs={{0,128},{128,0},{1,129},{129,1},{2,130},{130,2},{3,131},{131,3},{4... | collective-permute-start | bytes 18440 | tf_op jit(solution)/shard_map/ppermute | solution.py:479
  43.4 4.8 %collective-permute-start.3 = (bf16[8,1280]{1,0:T(8,128)(2,1)S(1)}, bf16[8,1280]{1,0:T(8,128)(2,1)S(1)}, u32[]{:S(2)}, u32[]{:S(2)}) collective-permute-start(bf16[8,1280]{1,0:T(8,128)(2,1)S(1)} %out_projection.1.own), channel_id=1, source_target_pairs={{0,2},{1,3},{2,0},{3,1},{4,6},{5,7},{6,4},{7,5},{8,10},{9,11},{10,... | collective-permute-start | bytes 61448 | tf_op jit(solution)/shard_map/ppermute | solution.py:364
  45.4 5.6 %collective-permute-start.2 = (bf16[8,1280]{1,0:T(8,128)(2,1)S(1)}, bf16[8,1280]{1,0:T(8,128)(2,1)S(1)}, u32[]{:S(2)}, u32[]{:S(2)}) collective-permute-start(bf16[8,1280]{1,0:T(8,128)(2,1)S(1)} %out_projection.1.own), channel_id=1, source_target_pairs={{0,3},{1,2},{2,1},{3,0},{4,7},{5,6},{6,5},{7,4},{8,11},{9,10},{10,... | collective-permute-start | bytes 61448 | tf_op jit(solution)/shard_map/ppermute | solution.py:364
  46.9 4.1 %collective-permute-start.1 = (bf16[8,1280]{1,0:T(8,128)(2,1)S(1)}, bf16[8,1280]{1,0:T(8,128)(2,1)S(1)}, u32[]{:S(2)}, u32[]{:S(2)}) collective-permute-start(bf16[8,1280]{1,0:T(8,128)(2,1)S(1)} %out_projection.1.own), channel_id=1, source_target_pairs={{0,1},{1,0},{2,3},{3,2},{4,5},{5,4},{6,7},{7,6},{8,9},{9,8},{10,11... | collective-permute-start | bytes 61448 | tf_op jit(solution)/shard_map/ppermute | solution.py:364
  51.8 4.7 %collective-permute-start.6 = (bf16[8,1280]{1,0:T(8,128)(2,1)S(1)}, bf16[8,1280]{1,0:T(8,128)(2,1)S(1)}, u32[]{:S(2)}, u32[]{:S(2)}) collective-permute-start(bf16[8,1280]{1,0:T(8,128)(2,1)S(1)} %get-tuple-element.28.own), channel_id=1, source_target_pairs={{0,2},{1,3},{2,0},{3,1},{4,6},{5,7},{6,4},{7,5},{8,10},{9,11},{10,... | collective-permute-start | bytes 61448 | tf_op jit(solution)/shard_map/ppermute | solution.py:364
  53.4 5.6 %collective-permute-start.5 = (bf16[8,1280]{1,0:T(8,128)(2,1)S(1)}, bf16[8,1280]{1,0:T(8,128)(2,1)S(1)}, u32[]{:S(2)}, u32[]{:S(2)}) collective-permute-start(bf16[8,1280]{1,0:T(8,128)(2,1)S(1)} %get-tuple-element.28.own), channel_id=1, source_target_pairs={{0,3},{1,2},{2,1},{3,0},{4,7},{5,6},{6,5},{7,4},{8,11},{9,10},{10,... | collective-permute-start | bytes 61448 | tf_op jit(solution)/shard_map/ppermute | solution.py:364
  54.3 4.7 %collective-permute-start.4 = (bf16[8,1280]{1,0:T(8,128)(2,1)S(1)}, bf16[8,1280]{1,0:T(8,128)(2,1)S(1)}, u32[]{:S(2)}, u32[]{:S(2)}) collective-permute-start(bf16[8,1280]{1,0:T(8,128)(2,1)S(1)} %get-tuple-element.28.own), channel_id=1, source_target_pairs={{0,1},{1,0},{2,3},{3,2},{4,5},{5,4},{6,7},{7,6},{8,9},{9,8},{10,11... | collective-permute-start | bytes 61448 | tf_op jit(solution)/shard_map/ppermute | solution.py:364

commit v8 on v7

--- a/solution.py
+++ b/solution.py
@@ -246,13 +246,17 @@
     for b in range(blocks):
         every_peak = jnp.where(block_lane == b, peaks[b], every_peak)
         holders = jnp.where(block_lane == b, owner_of[b : b + 1, :], holders)
+    every_joint = every_peak
+    for b in range(blocks):
+        peer = jnp.where(holders == owner_of[b : b + 1, :], peaks[b], VERY_LOW)
+        every_joint = jnp.maximum(every_joint, peer)
+    every_factor = jnp.exp(every_peak - every_joint)
     stat_lane = iota((8, 128), 1) - (STATS - 256)
     stat_row = iota((8, 128), 0)
     stats = []
     for b in range(blocks):
-        peers = jnp.where(holders == owner_of[b : b + 1, :], every_peak, VERY_LOW)
-        joint = jnp.max(peers, axis=1, keepdims=True)
-        factor = jnp.exp(peaks[b] - joint)
+        joint = every_joint[:, b : b + 1]
+        factor = every_factor[:, b : b + 1]
         sums[b : b + 1, :] = jnp.sum(parts[b] * factor, axis=0, keepdims=True)
         stat = jnp.where(stat_lane == stat_row, joint, 0.0)
         stat = stat + jnp.where(stat_lane == stat_row + 8, totals[b] * factor, 0.0)

time: 59.9 us -> 59.9 us (level)
  no operation moved by 1% of the time
where the time goes in v8:
time: 59.9 us; the launch traced here: 59.6 us
  starting transfers between devices  22.4 us (37%)
  waiting for transfers between devices  12.7 us (21%)
  Pallas kernels  11.9 us (20%)
  blocking collectives  11.9 us (20%)
  between operations  0.69 us (1%)
    all_to_all x1, blocking collectives, body(): shares = lax.all_to_all(shares, 'kv', 0, 0, tiled=True)  11.9 us
    all_to_all x1, starting transfers between devices, body(): queries = lax.all_to_all(spread, 'kv', 0, 0, tiled=True)  7.63 us
    ppermute x6, starting transfers between devices, from_others(): lax.ppermute(value, 'tp', [(i, i ^ bits) for i in range(count)])  7.51 us
    ppermute x6, waiting for transfers between devices, from_others(): lax.ppermute(value, 'tp', [(i, i ^ bits) for i in range(count)])  7.33 us
    ppermute x1, starting transfers between devices, body(): other = lax.ppermute(attended, 'rep', [(0, 1), (1, 0)])  7.28 us
    pallas_call x1, Pallas kernels, body(): pl.pallas_call(attend_kernel, out_shape=shape((requests, WIDE), BF16), in...  4.24 us
    all_to_all x1, waiting for transfers between devices, body(): queries = lax.all_to_all(spread, 'kv', 0, 0, tiled=True)  3.81 us
    pallas_call x1, Pallas kernels, body(): pl.pallas_call(side_kernel, out_shape=(pltpu.VMEM((EARLY, tokens, width),...  3.17 us
  transfers between devices with their start and end apart: 8, of which 6 were waited for; matrix products, arithmetic and copies ran while one was open for 0% of the time, Pallas kernels for 5%

profile of v8, /device:TPU:2, one launch (start us, length us, event | category | flops | bytes accessed | tf_op | source)
XLA Modules:
  0.0 59.6 jit_solution(17594756856398894407)
XLA Ops:
  0.6 2.4 %query.1 = (bf16[256,384]{1,0:T(8,128)(2,1)}, bf16[8,384]{1,0:T(8,128)(2,1)S(1)}, bf16[8,1280]{1,0:T(8,128)(2,1)S(1)}) custom-call(bf16[8,1280]{1,0:T(8,128)(2,1)} %token_.1, f32[1280]{0:T(1024)} %gain_hbm.2, bf16[960,1280]{1,0:T(8,128)(2,1)} %bitcast.15), custom_call_target="tpu_custom_call" | custom-call | tf_op jit(solution)/shard_map/query/pallas_call | solution.py:394
  3.0 7.6 %all-to-all-start = ((bf16[32,8,384]{2,1,0:T(8,128)(2,1)}), bf16[32,8,384]{2,1,0:T(8,128)(2,1)S(1)}, u32[]{:S(2)}, u32[]{:S(2)}) async-start(bf16[32,8,384]{2,1,0:T(8,128)(2,1)} %bitcast.2), calls=%async_computation | async-start | bytes 393216 | tf_op jit(solution)/shard_map/all_to_all | solution.py:412
  10.6 3.2 %side.1 = (bf16[5,512,640]{2,1,0:T(8,128)(2,1)S(1)}, s32[16,128]{1,0:T(8,128)S(1)}, s32[16,128]{1,0:T(8,128)S(1)}, f32[8,640]{1,0:T(8,128)}, f32[8,128]{1,0:T(8,...) custom-call(s32[1,11]{1,0:T(1,128)} %owner_hbm.1, ...), custom_call_target="tpu_custom_call" | custom-call | bytes 6553600 | tf_op jit(solution)/shard_map/side/pallas_call | solution.py:415
  13.8 3.8 %all-to-all-done = bf16[32,8,384]{2,1,0:T(8,128)(2,1)S(1)} async-done(((bf16[32,8,384]{2,1,0:T(8,128)(2,1)}), bf16[32,8,384]{2,1,0:T(8,128)(2,1)S(1)}, u32[]{:S(2)}, u32[]{:S(2)}) %all-to-all-start) | async-done | bytes 196640 | tf_op jit(solution)/shard_map/all_to_all | solution.py:412
  17.6 0.0 copy-start.2
  17.6 0.0 copy-start
  17.6 0.0 copy-start.1
  17.6 0.0 copy-start.3
  17.6 4.2 %attend.1 = bf16[256,384]{1,0:T(8,128)(2,1)S(1)} custom-call(s32[16,128]{1,0:T(8,128)S(1)} %get-tuple-element.20.owner_of, s32[16,128]{1,0:T(8,128)S(1)} %get-tuple-element.21.remains, bf16[256,384]{1,0:T(8,128)(2,1)S(1)} %bitcast.11, bf16[5,512,640]{2,1,0:T(8,128)(2,1)S(1)} %get-tuple-element.23.early, bf16[11,512,640]{2,1,0:T(8,128)(2,1)} %bitcast.14), custom_call_target="tpu_custom_call" | custom-call | tf_op jit(solution)/shard_map/attend/pallas_call | solution.py:453
  21.9 11.9 %all_to_all.22 = bf16[32,8,384]{2,1,0:T(8,128)(2,1)S(1)} all-to-all(bf16[32,8,384]{2,1,0:T(8,128)(2,1)S(1)} %bitcast.12), channel_id=1, replica_groups=mesh['rep'=2,'kv'=32,'tp'=4] {'kv'}, dimensions={0} | all-to-all | bytes 393216 | tf_op jit(solution)/shard_map/all_to_all | solution.py:473
  33.8 0.5 merge.1.here
  34.3 7.3 %collective-permute-start = (bf16[8,384]{1,0:T(8,128)(2,1)S(1)}, bf16[8,384]{1,0:T(8,128)(2,1)S(1)}, u32[]{:S(2)}, u32[]{:S(2)}) collective-permute-start(bf16[8,384]{1,0:T(8,128)(2,1)S(1)} %merge.1.here), channel_id=1, source_target_pairs={{0,128},{128,0},{1,129},{129,1},{2,130},{130,2},{3,131},{131,3},{4... | collective-permute-start | bytes 18440 | tf_op jit(solution)/shard_map/ppermute | solution.py:483
  41.5 1.6 %collective-permute-done.there = bf16[8,384]{1,0:T(8,128)(2,1)S(1)} collective-permute-done((bf16[8,384]{1,0:T(8,128)(2,1)S(1)}, bf16[8,384]{1,0:T(8,128)(2,1)S(1)}, u32[]{:S(2)}, u32[]{:S(2)}) %collective-permute-start) | collective-permute-done | bytes 6176 | tf_op jit(solution)/shard_map/ppermute | solution.py:483
  43.2 0.0 copy-done.2
  43.2 0.2 out_projection.1.own
  43.4 2.1 %collective-permute-start.3 = (bf16[8,1280]{1,0:T(8,128)(2,1)S(1)}, bf16[8,1280]{1,0:T(8,128)(2,1)S(1)}, u32[]{:S(2)}, u32[]{:S(2)}) collective-permute-start(bf16[8,1280]{1,0:T(8,128)(2,1)S(1)} %out_projection.1.own), channel_id=1, source_target_pairs={{0,2},{1,3},{2,0},{3,1},{4,6},{5,7},{6,4},{7,5},{8,10},{9,11},{10,... | collective-permute-start | bytes 61448 | tf_op jit(solution)/shard_map/ppermute | solution.py:368
  45.4 1.5 %collective-permute-start.2 = (bf16[8,1280]{1,0:T(8,128)(2,1)S(1)}, bf16[8,1280]{1,0:T(8,128)(2,1)S(1)}, u32[]{:S(2)}, u32[]{:S(2)}) collective-permute-start(bf16[8,1280]{1,0:T(8,128)(2,1)S(1)} %out_projection.1.own), channel_id=1, source_target_pairs={{0,3},{1,2},{2,1},{3,0},{4,7},{5,6},{6,5},{7,4},{8,11},{9,10},{10,... | collective-permute-start | bytes 61448 | tf_op jit(solution)/shard_map/ppermute | solution.py:368
  46.9 0.5 collective-permute-start.1
  47.4 0.8 %collective-permute-done.3.across = bf16[8,1280]{1,0:T(8,128)(2,1)S(1)} collective-permute-done((bf16[8,1280]{1,0:T(8,128)(2,1)S(1)}, bf16[8,1280]{1,0:T(8,128)(2,1)S(1)}, u32[]{:S(2)}, u32[]{:S(2)}) %collective-permute-start.3) | collective-permute-done | bytes 20512 | tf_op jit(solution)/shard_map/ppermute | solution.py:368
  48.1 2.9 %collective-permute-done.2.far = bf16[8,1280]{1,0:T(8,128)(2,1)S(1)} collective-permute-done((bf16[8,1280]{1,0:T(8,128)(2,1)S(1)}, bf16[8,1280]{1,0:T(8,128)(2,1)S(1)}, u32[]{:S(2)}, u32[]{:S(2)}) %collective-permute-start.2) | collective-permute-done | bytes 20512 | tf_op jit(solution)/shard_map/ppermute | solution.py:368
  51.0 0.0 collective-permute-done.1.near
  51.0 0.0 copy-done
  51.0 0.0 copy-done.1
  51.0 0.0 copy-done.3
  51.0 0.8 %hidden.1 = (f32[8,1280]{1,0:T(8,128)S(1)}, bf16[8,1280]{1,0:T(8,128)(2,1)S(1)}) custom-call(bf16[8,1280]{1,0:T(8,128)(2,1)S(1)} %copy-done.3, bf16[8,1280]{1,0:T(8,128)(2,1)S(1)} %out_projection.1.own, bf16[8,1280]{1,0:T(8,128)(2,1)S(1)} %collective-permute-done.1.near, bf16[8,1280]{1,0:T(8,128)(2,1)S(1)} %collective-permute-done.2.far, ...), custom_call_target="tpu_custom_call" | custom-call | tf_op jit(solution)/shard_map/hidden/pallas_call | solution.py:494
  51.8 1.6 %collective-permute-start.6 = (bf16[8,1280]{1,0:T(8,128)(2,1)S(1)}, bf16[8,1280]{1,0:T(8,128)(2,1)S(1)}, u32[]{:S(2)}, u32[]{:S(2)}) collective-permute-start(bf16[8,1280]{1,0:T(8,128)(2,1)S(1)} %get-tuple-element.28.own), channel_id=1, source_target_pairs={{0,2},{1,3},{2,0},{3,1},{4,6},{5,7},{6,4},{7,5},{8,10},{9,11},{10,... | collective-permute-start | bytes 61448 | tf_op jit(solution)/shard_map/ppermute | solution.py:368
  53.4 0.9 %collective-permute-start.5 = (bf16[8,1280]{1,0:T(8,128)(2,1)S(1)}, bf16[8,1280]{1,0:T(8,128)(2,1)S(1)}, u32[]{:S(2)}, u32[]{:S(2)}) collective-permute-start(bf16[8,1280]{1,0:T(8,128)(2,1)S(1)} %get-tuple-element.28.own), channel_id=1, source_target_pairs={{0,3},{1,2},{2,1},{3,0},{4,7},{5,6},{6,5},{7,4},{8,11},{9,10},{10,... | collective-permute-start | bytes 61448 | tf_op jit(solution)/shard_map/ppermute | solution.py:368
  54.3 1.0 %collective-permute-start.4 = (bf16[8,1280]{1,0:T(8,128)(2,1)S(1)}, bf16[8,1280]{1,0:T(8,128)(2,1)S(1)}, u32[]{:S(2)}, u32[]{:S(2)}) collective-permute-start(bf16[8,1280]{1,0:T(8,128)(2,1)S(1)} %get-tuple-element.28.own), channel_id=1, source_target_pairs={{0,1},{1,0},{2,3},{3,2},{4,5},{5,4},{6,7},{7,6},{8,9},{9,8},{10,11... | collective-permute-start | bytes 61448 | tf_op jit(solution)/shard_map/ppermute | solution.py:368
  55.3 1.2 %collective-permute-done.6.across = bf16[8,1280]{1,0:T(8,128)(2,1)S(1)} collective-permute-done((bf16[8,1280]{1,0:T(8,128)(2,1)S(1)}, bf16[8,1280]{1,0:T(8,128)(2,1)S(1)}, u32[]{:S(2)}, u32[]{:S(2)}) %collective-permute-start.6) | collective-permute-done | bytes 20512 | tf_op jit(solution)/shard_map/ppermute | solution.py:368
  56.5 2.5 %collective-permute-done.5.far = bf16[8,1280]{1,0:T(8,128)(2,1)S(1)} collective-permute-done((bf16[8,1280]{1,0:T(8,128)(2,1)S(1)}, bf16[8,1280]{1,0:T(8,128)(2,1)S(1)}, u32[]{:S(2)}, u32[]{:S(2)}) %collective-permute-start.5) | collective-permute-done | bytes 20512 | tf_op jit(solution)/shard_map/ppermute | solution.py:368
  59.0 0.0 collective-permute-done.4.near
  59.0 0.6 %finish.1 = f32[8,1280]{1,0:T(8,128)} custom-call(f32[8,128]{1,0:T(8,128)S(1)} %get-tuple-element.18.served, f32[8,1280]{1,0:T(8,128)S(1)} %get-tuple-element.27.residual, bf16[8,1280]{1,0:T(8,128)(2,1)S(1)} %get-tuple-element.28.own, bf16[8,1280]{1,0:T(8,128)(2,1)S(1)} %collective-permute-done.4.near, bf16[8,1280]{1,0:T(8,128)(2,1)S(1)} %collective-permute-done.5.far, ...), custom_call_target="tpu_custom_call" | custom-call | tf_op jit(solution)/shard_map/finish/pallas_call | solution.py:502
Async XLA Ops:
  3.0 14.6 %all-to-all-start = ((bf16[32,8,384]{2,1,0:T(8,128)(2,1)}), bf16[32,8,384]{2,1,0:T(8,128)(2,1)S(1)}, u32[]{:S(2)}, u32[]{:S(2)}) async-start(bf16[32,8,384]{2,1,0:T(8,128)(2,1)} %bitcast.2), calls=%async_computation | async-start | bytes 393216 | tf_op jit(solution)/shard_map/all_to_all | solution.py:412
  17.6 25.5 %copy-start.2 = (bf16[320,1280]{1,0:T(8,128)(2,1)S(1)}, bf16[320,1280]{1,0:T(8,128)(2,1)}, u32[]{:S(2)}) copy-start(bf16[320,1280]{1,0:T(8,128)(2,1)} %weight.1) | copy-start | bytes 2457604
  17.6 33.4 %copy-start = (bf16[1280,320]{0,1:T(8,128)(2,1)S(1)}, bf16[1280,320]{0,1:T(8,128)(2,1)}, u32[]{:S(2)}) copy-start(bf16[1280,320]{0,1:T(8,128)(2,1)} %param.18) | copy-start | bytes 2457604
  17.6 33.4 %copy-start.1 = (bf16[320,1280]{1,0:T(8,128)(2,1)S(1)}, bf16[320,1280]{1,0:T(8,128)(2,1)}, u32[]{:S(2)}) copy-start(bf16[320,1280]{1,0:T(8,128)(2,1)} %down.1) | copy-start | bytes 2457604
  17.6 33.4 %copy-start.3 = (bf16[8,1280]{1,0:T(8,128)(2,1)S(1)}, bf16[8,1280]{1,0:T(8,128)(2,1)}, u32[]{:S(2)}) copy-start(bf16[8,1280]{1,0:T(8,128)(2,1)} %token_.1) | copy-start | bytes 61444
  34.3 8.9 %collective-permute-start = (bf16[8,384]{1,0:T(8,128)(2,1)S(1)}, bf16[8,384]{1,0:T(8,128)(2,1)S(1)}, u32[]{:S(2)}, u32[]{:S(2)}) collective-permute-start(bf16[8,384]{1,0:T(8,128)(2,1)S(1)} %merge.1.here), channel_id=1, source_target_pairs={{0,128},{128,0},{1,129},{129,1},{2,130},{130,2},{3,131},{131,3},{4... | collective-permute-start | bytes 18440 | tf_op jit(solution)/shard_map/ppermute | solution.py:483
  43.4 4.8 %collective-permute-start.3 = (bf16[8,1280]{1,0:T(8,128)(2,1)S(1)}, bf16[8,1280]{1,0:T(8,128)(2,1)S(1)}, u32[]{:S(2)}, u32[]{:S(2)}) collective-permute-start(bf16[8,1280]{1,0:T(8,128)(2,1)S(1)} %out_projection.1.own), channel_id=1, source_target_pairs={{0,2},{1,3},{2,0},{3,1},{4,6},{5,7},{6,4},{7,5},{8,10},{9,11},{10,... | collective-permute-start | bytes 61448 | tf_op jit(solution)/shard_map/ppermute | solution.py:368
  45.4 5.6 %collective-permute-start.2 = (bf16[8,1280]{1,0:T(8,128)(2,1)S(1)}, bf16[8,1280]{1,0:T(8,128)(2,1)S(1)}, u32[]{:S(2)}, u32[]{:S(2)}) collective-permute-start(bf16[8,1280]{1,0:T(8,128)(2,1)S(1)} %out_projection.1.own), channel_id=1, source_target_pairs={{0,3},{1,2},{2,1},{3,0},{4,7},{5,6},{6,5},{7,4},{8,11},{9,10},{10,... | collective-permute-start | bytes 61448 | tf_op jit(solution)/shard_map/ppermute | solution.py:368
  46.9 4.1 %collective-permute-start.1 = (bf16[8,1280]{1,0:T(8,128)(2,1)S(1)}, bf16[8,1280]{1,0:T(8,128)(2,1)S(1)}, u32[]{:S(2)}, u32[]{:S(2)}) collective-permute-start(bf16[8,1280]{1,0:T(8,128)(2,1)S(1)} %out_projection.1.own), channel_id=1, source_target_pairs={{0,1},{1,0},{2,3},{3,2},{4,5},{5,4},{6,7},{7,6},{8,9},{9,8},{10,11... | collective-permute-start | bytes 61448 | tf_op jit(solution)/shard_map/ppermute | solution.py:368
  51.8 4.7 %collective-permute-start.6 = (bf16[8,1280]{1,0:T(8,128)(2,1)S(1)}, bf16[8,1280]{1,0:T(8,128)(2,1)S(1)}, u32[]{:S(2)}, u32[]{:S(2)}) collective-permute-start(bf16[8,1280]{1,0:T(8,128)(2,1)S(1)} %get-tuple-element.28.own), channel_id=1, source_target_pairs={{0,2},{1,3},{2,0},{3,1},{4,6},{5,7},{6,4},{7,5},{8,10},{9,11},{10,... | collective-permute-start | bytes 61448 | tf_op jit(solution)/shard_map/ppermute | solution.py:368
  53.4 5.6 %collective-permute-start.5 = (bf16[8,1280]{1,0:T(8,128)(2,1)S(1)}, bf16[8,1280]{1,0:T(8,128)(2,1)S(1)}, u32[]{:S(2)}, u32[]{:S(2)}) collective-permute-start(bf16[8,1280]{1,0:T(8,128)(2,1)S(1)} %get-tuple-element.28.own), channel_id=1, source_target_pairs={{0,3},{1,2},{2,1},{3,0},{4,7},{5,6},{6,5},{7,4},{8,11},{9,10},{10,... | collective-permute-start | bytes 61448 | tf_op jit(solution)/shard_map/ppermute | solution.py:368
  54.3 4.7 %collective-permute-start.4 = (bf16[8,1280]{1,0:T(8,128)(2,1)S(1)}, bf16[8,1280]{1,0:T(8,128)(2,1)S(1)}, u32[]{:S(2)}, u32[]{:S(2)}) collective-permute-start(bf16[8,1280]{1,0:T(8,128)(2,1)S(1)} %get-tuple-element.28.own), channel_id=1, source_target_pairs={{0,1},{1,0},{2,3},{3,2},{4,5},{5,4},{6,7},{7,6},{8,9},{9,8},{10,11... | collective-permute-start | bytes 61448 | tf_op jit(solution)/shard_map/ppermute | solution.py:368

commit v9 on v8

--- a/solution.py
+++ b/solution.py
@@ -347,8 +347,8 @@
 def hidden_kernel(token, own, near, far, across, gain, up, down, residual, partial):
     total = token[...].astype(F32) + joined(own, near, across, far)
     residual[...] = total
-    normed = root_norm(total, gain[...]).astype(BF16)
-    hidden = dot_transposed(normed, up[...])
+    scale = lax.rsqrt(jnp.mean(total * total, axis=-1, keepdims=True) + NORM_EPS)
+    hidden = dot_transposed((total * gain[...]).astype(BF16), up[...]) * scale
     active = jax.nn.gelu(hidden, approximate=True).astype(BF16)
     partial[...] = jnp.dot(active, down[...], preferred_element_type=F32).astype(BF16)
 

time: 59.9 us -> 59.9 us (level)
  no operation moved by 1% of the time
where the time goes in v9:
time: 59.9 us; the launch traced here: 59.6 us
  starting transfers between devices  22.4 us (37%)
  waiting for transfers between devices  12.7 us (21%)
  Pallas kernels  11.9 us (20%)
  blocking collectives  11.9 us (20%)
  between operations  0.69 us (1%)
    all_to_all x1, blocking collectives, body(): shares = lax.all_to_all(shares, 'kv', 0, 0, tiled=True)  11.9 us
    all_to_all x1, starting transfers between devices, body(): queries = lax.all_to_all(spread, 'kv', 0, 0, tiled=True)  7.63 us
    ppermute x6, starting transfers between devices, from_others(): lax.ppermute(value, 'tp', [(i, i ^ bits) for i in range(count)])  7.51 us
    ppermute x6, waiting for transfers between devices, from_others(): lax.ppermute(value, 'tp', [(i, i ^ bits) for i in range(count)])  7.33 us
    ppermute x1, starting transfers between devices, body(): other = lax.ppermute(attended, 'rep', [(0, 1), (1, 0)])  7.28 us
    pallas_call x1, Pallas kernels, body(): pl.pallas_call(attend_kernel, out_shape=shape((requests, WIDE), BF16), in...  4.24 us
    all_to_all x1, waiting for transfers between devices, body(): queries = lax.all_to_all(spread, 'kv', 0, 0, tiled=True)  3.81 us
    pallas_call x1, Pallas kernels, body(): pl.pallas_call(side_kernel, out_shape=(pltpu.VMEM((EARLY, tokens, width),...  3.17 us
  transfers between devices with their start and end apart: 8, of which 6 were waited for; matrix products, arithmetic and copies ran while one was open for 0% of the time, Pallas kernels for 5%

profile of v9, /device:TPU:2, one launch (start us, length us, event | category | flops | bytes accessed | tf_op | source)
XLA Modules:
  0.0 59.6 jit_solution(17394201279025835107)
XLA Ops:
  0.6 2.4 %query.1 = (bf16[256,384]{1,0:T(8,128)(2,1)}, bf16[8,384]{1,0:T(8,128)(2,1)S(1)}, bf16[8,1280]{1,0:T(8,128)(2,1)S(1)}) custom-call(bf16[8,1280]{1,0:T(8,128)(2,1)} %token_.1, f32[1280]{0:T(1024)} %gain_hbm.2, bf16[960,1280]{1,0:T(8,128)(2,1)} %bitcast.15), custom_call_target="tpu_custom_call" | custom-call | tf_op jit(solution)/shard_map/query/pallas_call | solution.py:394
  3.0 7.6 %all-to-all-start = ((bf16[32,8,384]{2,1,0:T(8,128)(2,1)}), bf16[32,8,384]{2,1,0:T(8,128)(2,1)S(1)}, u32[]{:S(2)}, u32[]{:S(2)}) async-start(bf16[32,8,384]{2,1,0:T(8,128)(2,1)} %bitcast.2), calls=%async_computation | async-start | bytes 393216 | tf_op jit(solution)/shard_map/all_to_all | solution.py:412
  10.6 3.2 %side.1 = (bf16[5,512,640]{2,1,0:T(8,128)(2,1)S(1)}, s32[16,128]{1,0:T(8,128)S(1)}, s32[16,128]{1,0:T(8,128)S(1)}, f32[8,640]{1,0:T(8,128)}, f32[8,128]{1,0:T(8,...) custom-call(s32[1,11]{1,0:T(1,128)} %owner_hbm.1, ...), custom_call_target="tpu_custom_call" | custom-call | bytes 6553600 | tf_op jit(solution)/shard_map/side/pallas_call | solution.py:415
  13.8 3.8 %all-to-all-done = bf16[32,8,384]{2,1,0:T(8,128)(2,1)S(1)} async-done(((bf16[32,8,384]{2,1,0:T(8,128)(2,1)}), bf16[32,8,384]{2,1,0:T(8,128)(2,1)S(1)}, u32[]{:S(2)}, u32[]{:S(2)}) %all-to-all-start) | async-done | bytes 196640 | tf_op jit(solution)/shard_map/all_to_all | solution.py:412
  17.6 0.0 copy-start.2
  17.6 0.0 copy-start
  17.6 0.0 copy-start.1
  17.6 0.0 copy-start.3
  17.6 4.2 %attend.1 = bf16[256,384]{1,0:T(8,128)(2,1)S(1)} custom-call(s32[16,128]{1,0:T(8,128)S(1)} %get-tuple-element.20.owner_of, s32[16,128]{1,0:T(8,128)S(1)} %get-tuple-element.21.remains, bf16[256,384]{1,0:T(8,128)(2,1)S(1)} %bitcast.11, bf16[5,512,640]{2,1,0:T(8,128)(2,1)S(1)} %get-tuple-element.23.early, bf16[11,512,640]{2,1,0:T(8,128)(2,1)} %bitcast.14), custom_call_target="tpu_custom_call" | custom-call | tf_op jit(solution)/shard_map/attend/pallas_call | solution.py:453
  21.9 11.9 %all_to_all.22 = bf16[32,8,384]{2,1,0:T(8,128)(2,1)S(1)} all-to-all(bf16[32,8,384]{2,1,0:T(8,128)(2,1)S(1)} %bitcast.12), channel_id=1, replica_groups=mesh['rep'=2,'kv'=32,'tp'=4] {'kv'}, dimensions={0} | all-to-all | bytes 393216 | tf_op jit(solution)/shard_map/all_to_all | solution.py:473
  33.8 0.5 merge.1.here
  34.3 7.3 %collective-permute-start = (bf16[8,384]{1,0:T(8,128)(2,1)S(1)}, bf16[8,384]{1,0:T(8,128)(2,1)S(1)}, u32[]{:S(2)}, u32[]{:S(2)}) collective-permute-start(bf16[8,384]{1,0:T(8,128)(2,1)S(1)} %merge.1.here), channel_id=1, source_target_pairs={{0,128},{128,0},{1,129},{129,1},{2,130},{130,2},{3,131},{131,3},{4... | collective-permute-start | bytes 18440 | tf_op jit(solution)/shard_map/ppermute | solution.py:483
  41.5 1.6 %collective-permute-done.there = bf16[8,384]{1,0:T(8,128)(2,1)S(1)} collective-permute-done((bf16[8,384]{1,0:T(8,128)(2,1)S(1)}, bf16[8,384]{1,0:T(8,128)(2,1)S(1)}, u32[]{:S(2)}, u32[]{:S(2)}) %collective-permute-start) | collective-permute-done | bytes 6176 | tf_op jit(solution)/shard_map/ppermute | solution.py:483
  43.2 0.0 copy-done.2
  43.2 0.2 out_projection.1.own
  43.4 2.1 %collective-permute-start.3 = (bf16[8,1280]{1,0:T(8,128)(2,1)S(1)}, bf16[8,1280]{1,0:T(8,128)(2,1)S(1)}, u32[]{:S(2)}, u32[]{:S(2)}) collective-permute-start(bf16[8,1280]{1,0:T(8,128)(2,1)S(1)} %out_projection.1.own), channel_id=1, source_target_pairs={{0,2},{1,3},{2,0},{3,1},{4,6},{5,7},{6,4},{7,5},{8,10},{9,11},{10,... | collective-permute-start | bytes 61448 | tf_op jit(solution)/shard_map/ppermute | solution.py:368
  45.4 1.5 %collective-permute-start.2 = (bf16[8,1280]{1,0:T(8,128)(2,1)S(1)}, bf16[8,1280]{1,0:T(8,128)(2,1)S(1)}, u32[]{:S(2)}, u32[]{:S(2)}) collective-permute-start(bf16[8,1280]{1,0:T(8,128)(2,1)S(1)} %out_projection.1.own), channel_id=1, source_target_pairs={{0,3},{1,2},{2,1},{3,0},{4,7},{5,6},{6,5},{7,4},{8,11},{9,10},{10,... | collective-permute-start | bytes 61448 | tf_op jit(solution)/shard_map/ppermute | solution.py:368
  46.9 0.5 collective-permute-start.1
  47.4 0.8 %collective-permute-done.3.across = bf16[8,1280]{1,0:T(8,128)(2,1)S(1)} collective-permute-done((bf16[8,1280]{1,0:T(8,128)(2,1)S(1)}, bf16[8,1280]{1,0:T(8,128)(2,1)S(1)}, u32[]{:S(2)}, u32[]{:S(2)}) %collective-permute-start.3) | collective-permute-done | bytes 20512 | tf_op jit(solution)/shard_map/ppermute | solution.py:368
  48.1 2.9 %collective-permute-done.2.far = bf16[8,1280]{1,0:T(8,128)(2,1)S(1)} collective-permute-done((bf16[8,1280]{1,0:T(8,128)(2,1)S(1)}, bf16[8,1280]{1,0:T(8,128)(2,1)S(1)}, u32[]{:S(2)}, u32[]{:S(2)}) %collective-permute-start.2) | collective-permute-done | bytes 20512 | tf_op jit(solution)/shard_map/ppermute | solution.py:368
  51.0 0.0 collective-permute-done.1.near
  51.0 0.0 copy-done
  51.0 0.0 copy-done.1
  51.0 0.0 copy-done.3
  51.0 0.8 %hidden.1 = (f32[8,1280]{1,0:T(8,128)S(1)}, bf16[8,1280]{1,0:T(8,128)(2,1)S(1)}) custom-call(bf16[8,1280]{1,0:T(8,128)(2,1)S(1)} %copy-done.3, bf16[8,1280]{1,0:T(8,128)(2,1)S(1)} %out_projection.1.own, bf16[8,1280]{1,0:T(8,128)(2,1)S(1)} %collective-permute-done.1.near, bf16[8,1280]{1,0:T(8,128)(2,1)S(1)} %collective-permute-done.2.far, ...), custom_call_target="tpu_custom_call" | custom-call | tf_op jit(solution)/shard_map/hidden/pallas_call | solution.py:494
  51.8 1.6 %collective-permute-start.6 = (bf16[8,1280]{1,0:T(8,128)(2,1)S(1)}, bf16[8,1280]{1,0:T(8,128)(2,1)S(1)}, u32[]{:S(2)}, u32[]{:S(2)}) collective-permute-start(bf16[8,1280]{1,0:T(8,128)(2,1)S(1)} %get-tuple-element.28.own), channel_id=1, source_target_pairs={{0,2},{1,3},{2,0},{3,1},{4,6},{5,7},{6,4},{7,5},{8,10},{9,11},{10,... | collective-permute-start | bytes 61448 | tf_op jit(solution)/shard_map/ppermute | solution.py:368
  53.4 0.9 %collective-permute-start.5 = (bf16[8,1280]{1,0:T(8,128)(2,1)S(1)}, bf16[8,1280]{1,0:T(8,128)(2,1)S(1)}, u32[]{:S(2)}, u32[]{:S(2)}) collective-permute-start(bf16[8,1280]{1,0:T(8,128)(2,1)S(1)} %get-tuple-element.28.own), channel_id=1, source_target_pairs={{0,3},{1,2},{2,1},{3,0},{4,7},{5,6},{6,5},{7,4},{8,11},{9,10},{10,... | collective-permute-start | bytes 61448 | tf_op jit(solution)/shard_map/ppermute | solution.py:368
  54.3 1.0 %collective-permute-start.4 = (bf16[8,1280]{1,0:T(8,128)(2,1)S(1)}, bf16[8,1280]{1,0:T(8,128)(2,1)S(1)}, u32[]{:S(2)}, u32[]{:S(2)}) collective-permute-start(bf16[8,1280]{1,0:T(8,128)(2,1)S(1)} %get-tuple-element.28.own), channel_id=1, source_target_pairs={{0,1},{1,0},{2,3},{3,2},{4,5},{5,4},{6,7},{7,6},{8,9},{9,8},{10,11... | collective-permute-start | bytes 61448 | tf_op jit(solution)/shard_map/ppermute | solution.py:368
  55.3 1.2 %collective-permute-done.6.across = bf16[8,1280]{1,0:T(8,128)(2,1)S(1)} collective-permute-done((bf16[8,1280]{1,0:T(8,128)(2,1)S(1)}, bf16[8,1280]{1,0:T(8,128)(2,1)S(1)}, u32[]{:S(2)}, u32[]{:S(2)}) %collective-permute-start.6) | collective-permute-done | bytes 20512 | tf_op jit(solution)/shard_map/ppermute | solution.py:368
  56.5 2.5 %collective-permute-done.5.far = bf16[8,1280]{1,0:T(8,128)(2,1)S(1)} collective-permute-done((bf16[8,1280]{1,0:T(8,128)(2,1)S(1)}, bf16[8,1280]{1,0:T(8,128)(2,1)S(1)}, u32[]{:S(2)}, u32[]{:S(2)}) %collective-permute-start.5) | collective-permute-done | bytes 20512 | tf_op jit(solution)/shard_map/ppermute | solution.py:368
  59.0 0.0 collective-permute-done.4.near
  59.0 0.6 %finish.1 = f32[8,1280]{1,0:T(8,128)} custom-call(f32[8,128]{1,0:T(8,128)S(1)} %get-tuple-element.18.served, f32[8,1280]{1,0:T(8,128)S(1)} %get-tuple-element.27.residual, bf16[8,1280]{1,0:T(8,128)(2,1)S(1)} %get-tuple-element.28.own, bf16[8,1280]{1,0:T(8,128)(2,1)S(1)} %collective-permute-done.4.near, bf16[8,1280]{1,0:T(8,128)(2,1)S(1)} %collective-permute-done.5.far, ...), custom_call_target="tpu_custom_call" | custom-call | tf_op jit(solution)/shard_map/finish/pallas_call | solution.py:502
Async XLA Ops:
  3.0 14.6 %all-to-all-start = ((bf16[32,8,384]{2,1,0:T(8,128)(2,1)}), bf16[32,8,384]{2,1,0:T(8,128)(2,1)S(1)}, u32[]{:S(2)}, u32[]{:S(2)}) async-start(bf16[32,8,384]{2,1,0:T(8,128)(2,1)} %bitcast.2), calls=%async_computation | async-start | bytes 393216 | tf_op jit(solution)/shard_map/all_to_all | solution.py:412
  17.6 25.5 %copy-start.2 = (bf16[320,1280]{1,0:T(8,128)(2,1)S(1)}, bf16[320,1280]{1,0:T(8,128)(2,1)}, u32[]{:S(2)}) copy-start(bf16[320,1280]{1,0:T(8,128)(2,1)} %weight.1) | copy-start | bytes 2457604
  17.6 33.4 %copy-start = (bf16[1280,320]{0,1:T(8,128)(2,1)S(1)}, bf16[1280,320]{0,1:T(8,128)(2,1)}, u32[]{:S(2)}) copy-start(bf16[1280,320]{0,1:T(8,128)(2,1)} %param.18) | copy-start | bytes 2457604
  17.6 33.4 %copy-start.1 = (bf16[320,1280]{1,0:T(8,128)(2,1)S(1)}, bf16[320,1280]{1,0:T(8,128)(2,1)}, u32[]{:S(2)}) copy-start(bf16[320,1280]{1,0:T(8,128)(2,1)} %down.1) | copy-start | bytes 2457604
  17.6 33.4 %copy-start.3 = (bf16[8,1280]{1,0:T(8,128)(2,1)S(1)}, bf16[8,1280]{1,0:T(8,128)(2,1)}, u32[]{:S(2)}) copy-start(bf16[8,1280]{1,0:T(8,128)(2,1)} %token_.1) | copy-start | bytes 61444
  34.3 8.9 %collective-permute-start = (bf16[8,384]{1,0:T(8,128)(2,1)S(1)}, bf16[8,384]{1,0:T(8,128)(2,1)S(1)}, u32[]{:S(2)}, u32[]{:S(2)}) collective-permute-start(bf16[8,384]{1,0:T(8,128)(2,1)S(1)} %merge.1.here), channel_id=1, source_target_pairs={{0,128},{128,0},{1,129},{129,1},{2,130},{130,2},{3,131},{131,3},{4... | collective-permute-start | bytes 18440 | tf_op jit(solution)/shard_map/ppermute | solution.py:483
  43.4 4.8 %collective-permute-start.3 = (bf16[8,1280]{1,0:T(8,128)(2,1)S(1)}, bf16[8,1280]{1,0:T(8,128)(2,1)S(1)}, u32[]{:S(2)}, u32[]{:S(2)}) collective-permute-start(bf16[8,1280]{1,0:T(8,128)(2,1)S(1)} %out_projection.1.own), channel_id=1, source_target_pairs={{0,2},{1,3},{2,0},{3,1},{4,6},{5,7},{6,4},{7,5},{8,10},{9,11},{10,... | collective-permute-start | bytes 61448 | tf_op jit(solution)/shard_map/ppermute | solution.py:368
  45.4 5.6 %collective-permute-start.2 = (bf16[8,1280]{1,0:T(8,128)(2,1)S(1)}, bf16[8,1280]{1,0:T(8,128)(2,1)S(1)}, u32[]{:S(2)}, u32[]{:S(2)}) collective-permute-start(bf16[8,1280]{1,0:T(8,128)(2,1)S(1)} %out_projection.1.own), channel_id=1, source_target_pairs={{0,3},{1,2},{2,1},{3,0},{4,7},{5,6},{6,5},{7,4},{8,11},{9,10},{10,... | collective-permute-start | bytes 61448 | tf_op jit(solution)/shard_map/ppermute | solution.py:368
  46.9 4.1 %collective-permute-start.1 = (bf16[8,1280]{1,0:T(8,128)(2,1)S(1)}, bf16[8,1280]{1,0:T(8,128)(2,1)S(1)}, u32[]{:S(2)}, u32[]{:S(2)}) collective-permute-start(bf16[8,1280]{1,0:T(8,128)(2,1)S(1)} %out_projection.1.own), channel_id=1, source_target_pairs={{0,1},{1,0},{2,3},{3,2},{4,5},{5,4},{6,7},{7,6},{8,9},{9,8},{10,11... | collective-permute-start | bytes 61448 | tf_op jit(solution)/shard_map/ppermute | solution.py:368
  51.8 4.7 %collective-permute-start.6 = (bf16[8,1280]{1,0:T(8,128)(2,1)S(1)}, bf16[8,1280]{1,0:T(8,128)(2,1)S(1)}, u32[]{:S(2)}, u32[]{:S(2)}) collective-permute-start(bf16[8,1280]{1,0:T(8,128)(2,1)S(1)} %get-tuple-element.28.own), channel_id=1, source_target_pairs={{0,2},{1,3},{2,0},{3,1},{4,6},{5,7},{6,4},{7,5},{8,10},{9,11},{10,... | collective-permute-start | bytes 61448 | tf_op jit(solution)/shard_map/ppermute | solution.py:368
  53.4 5.6 %collective-permute-start.5 = (bf16[8,1280]{1,0:T(8,128)(2,1)S(1)}, bf16[8,1280]{1,0:T(8,128)(2,1)S(1)}, u32[]{:S(2)}, u32[]{:S(2)}) collective-permute-start(bf16[8,1280]{1,0:T(8,128)(2,1)S(1)} %get-tuple-element.28.own), channel_id=1, source_target_pairs={{0,3},{1,2},{2,1},{3,0},{4,7},{5,6},{6,5},{7,4},{8,11},{9,10},{10,... | collective-permute-start | bytes 61448 | tf_op jit(solution)/shard_map/ppermute | solution.py:368
  54.3 4.7 %collective-permute-start.4 = (bf16[8,1280]{1,0:T(8,128)(2,1)S(1)}, bf16[8,1280]{1,0:T(8,128)(2,1)S(1)}, u32[]{:S(2)}, u32[]{:S(2)}) collective-permute-start(bf16[8,1280]{1,0:T(8,128)(2,1)S(1)} %get-tuple-element.28.own), channel_id=1, source_target_pairs={{0,1},{1,0},{2,3},{3,2},{4,5},{5,4},{6,7},{7,6},{8,9},{9,8},{10,11... | collective-permute-start | bytes 61448 | tf_op jit(solution)/shard_map/ppermute | solution.py:368
